TPU v7x, 32 devices: a whole 2x2x4 slice. The times are simulated.
32 devices in a mesh: dp: 4 (over x, core), chan: 8 (over z, y).
Axes of the slice: x: 2, y: 2, z: 4, core: 2. Of those that a mesh axis runs over, the one named last changes fastest.
Arguments:
- patches: bfloat16 [8192, 768], P(('dp', 'chan')), may hold values from -6 to 6
- valid_mask: int32 [8192], P('dp'), may hold values from 0 to 1, as said below
- target_mask: int32 [8192], P('dp'), may hold values 0 or 1
- keep_mask: int32 [32, 2, 2], P('dp'), may hold values 0 or 1
- embed_weight: float32 [768, 384], replicated, may hold values from -0.21875 to 0.21875
- embed_moment: float32 [768, 384], replicated, may hold values from -0.0029296875 to 0.0029296875
- head_weight: float32 [384, 768], replicated, may hold values from -0.3125 to 0.3125
- head_moment: float32 [384, 768], replicated, may hold values from -0.0029296875 to 0.0029296875
- vectors: float32 [26, 384], replicated
- vector_moment: float32 [26, 384], replicated, may hold values from -0.015625 to 0.015625
- vector_average: float32 [26, 384], replicated
- focal_input: float32 [2, 384, 2, 384], P(None, None, None, 'chan'), may hold values from -0.3125 to 0.3125
- focal_moment: float32 [2, 384, 2, 384], P(None, None, None, 'chan'), may hold values from -0.0029296875 to 0.0029296875
- focal_average: float32 [2, 384, 2, 384], P(None, None, None, 'chan'), may hold values from -0.3125 to 0.3125
- mixers: float32 [2, 2, 384, 384], P(None, None, None, 'chan'), may hold values from -0.3125 to 0.3125
- mixer_moment: float32 [2, 2, 384, 384], P(None, None, None, 'chan'), may hold values from -0.0029296875 to 0.0029296875
- mixer_average: float32 [2, 2, 384, 384], P(None, None, None, 'chan'), may hold values from -0.3125 to 0.3125
- mlp_weights: float32 [2, 2, 384, 1536], P(None, None, None, 'chan'), may hold values from -0.3125 to 0.3125
- mlp_moment: float32 [2, 2, 384, 1536], P(None, None, None, 'chan'), may hold values from -0.0029296875 to 0.0029296875
- mlp_average: float32 [2, 2, 384, 1536], P(None, None, None, 'chan'), may hold values from -0.3125 to 0.3125
- kernels: float32 [2, 83, 384], P(None, None, 'chan'), may hold values from -1.25 to 1.25
- kernel_moment: float32 [2, 83, 384], P(None, None, 'chan'), may hold values from -0.0029296875 to 0.0029296875
- kernel_average: float32 [2, 83, 384], P(None, None, 'chan'), may hold values from -1.25 to 1.25
Outputs:
- loss: float32 [], replicated
- new_embed: float32 [768, 384], replicated
- new_embed_moment: float32 [768, 384], replicated
- new_head: float32 [384, 768], replicated
- new_head_moment: float32 [384, 768], replicated
- new_vectors: float32 [26, 384], replicated
- new_vector_moment: float32 [26, 384], replicated
- new_vector_average: float32 [26, 384], replicated
- new_focal: float32 [2, 384, 2, 384], P(None, None, None, 'chan')
- new_focal_moment: float32 [2, 384, 2, 384], P(None, None, None, 'chan')
- new_focal_average: float32 [2, 384, 2, 384], P(None, None, None, 'chan')
- new_mixers: float32 [2, 2, 384, 384], P(None, None, None, 'chan')
- new_mixer_moment: float32 [2, 2, 384, 384], P(None, None, None, 'chan')
- new_mixer_average: float32 [2, 2, 384, 384], P(None, None, None, 'chan')
- new_mlp: float32 [2, 2, 384, 1536], P(None, None, None, 'chan')
- new_mlp_moment: float32 [2, 2, 384, 1536], P(None, None, None, 'chan')
- new_mlp_average: float32 [2, 2, 384, 1536], P(None, None, None, 'chan')
- new_kernels: float32 [2, 83, 384], P(None, None, 'chan')
- new_kernel_moment: float32 [2, 83, 384], P(None, None, 'chan')
- new_kernel_average: float32 [2, 83, 384], P(None, None, 'chan')
Inputs may be any that keep to these rules, and one draw needn't show every extreme that they name: `valid_mask`: each image's valid patches form its top-left rectangle with 8 to 16 rows and columns; image 0 is whole.
All inputs are finite; a program needn't handle non-finite values. No bound on the sum of `target_mask` or of `keep_mask` on one device may be relied on, other than what follows from the above.
Results may differ from a plain program's by a relative error of at most 0.012.
Values may be sent and summed in bfloat16 or wider, within the bound.
No kernel may reach another device: no remote copies, remote signals or barrier semaphores. Data moves between devices by JAX's collectives and lax.ppermute only.
A program may use at most 320 MiB of HBM per device.

v0:
```python
import math

import jax
import jax.numpy as jnp
from jax import lax
from jax.sharding import PartitionSpec as P

PATCH_IN = 768
GRID = 16
BLOCKS = 2


EPS = 1e-05
MOMENTUM = 0.9
AVERAGE = 0.5
KEEP_RATE = 0.8
KERNEL_SIZES = (3, 5, 7)
KERNEL_STARTS = (0, 9, 34)


def matmul(left, right):
    return jnp.dot(left, right, preferred_element_type=jnp.float32)


def contract_rows(left, right):
    return lax.dot_general(
        left, right, (((0,), (0,)), ((), ())), preferred_element_type=jnp.float32
    )


def times_transposed(left, right):
    return lax.dot_general(
        left, right, (((1,), (1,)), ((), ())), preferred_element_type=jnp.float32
    )


def split_low(values):
    high_part = values.astype(jnp.bfloat16)
    rest_part = (values - high_part.astype(jnp.float32)).astype(jnp.bfloat16)
    return (high_part, rest_part)


def layer_norm(values, norm_gain, norm_shift):
    average = jnp.mean(values, axis=-1, keepdims=True)
    centred = values - average
    variance = jnp.mean(centred * centred, axis=-1, keepdims=True)
    return centred * lax.rsqrt(variance + EPS) * norm_gain + norm_shift


def exact_gelu(values):
    return jax.nn.gelu(values, approximate=False)


def depthwise(field, kernel_taps, kernel_width):
    margin = kernel_width // 2
    padded = jnp.pad(field, ((0, 0), (margin, margin), (margin, margin), (0, 0)))
    summed = jnp.zeros_like(field)
    for kernel_row in range(kernel_width):
        for kernel_col in range(kernel_width):
            window = padded[:, kernel_row : kernel_row + GRID, kernel_col : kernel_col + GRID, :]
            summed = summed + window * kernel_taps[kernel_row * kernel_width + kernel_col]
    return summed


def focal_levels(context, gates, kernel_block, validity):
    image_count = validity.shape[0] // (GRID * GRID)
    channels = context.shape[-1]
    current = context.reshape(image_count, GRID, GRID, channels)
    gate_grid = gates.reshape(image_count, GRID, GRID, 4)
    summed = jnp.zeros_like(current)
    for level_index in range(3):
        kernel_width = KERNEL_SIZES[level_index]
        first_tap = KERNEL_STARTS[level_index]
        kernel_taps = kernel_block[first_tap : first_tap + kernel_width * kernel_width]
        current = exact_gelu(depthwise(current, kernel_taps, kernel_width))
        summed = summed + current * gate_grid[..., level_index : level_index + 1]
    valid_grid = validity.reshape(image_count, GRID, GRID, 1)
    valid_total = jnp.sum(valid_grid, axis=(1, 2), keepdims=True)
    pooled = exact_gelu(jnp.sum(current * valid_grid, axis=(1, 2), keepdims=True) / valid_total)
    summed = summed + pooled * gate_grid[..., 3:4]
    return summed.reshape(image_count * GRID * GRID, channels)


def gather_rows(values):
    return lax.all_gather(values, "chan", axis=0, tiled=True)


def gather_grads(values):
    return lax.all_gather(values, "chan", axis=0, tiled=True)


def regather_rows(values):
    return lax.all_gather(values, "chan", axis=0, tiled=True)


def reduce_rows(row_terms, row_total):
    return lax.psum_scatter(
        row_terms(jnp.int32(0), lax.axis_size("chan") * row_total).astype(jnp.bfloat16),
        "chan",
        scatter_dimension=0,
        tiled=True,
    ).astype(jnp.float32)


def reduce_inputs(row_terms, row_total):
    return lax.psum_scatter(
        row_terms(jnp.int32(0), lax.axis_size("chan") * row_total).astype(jnp.bfloat16),
        "chan",
        scatter_dimension=0,
        tiled=True,
    ).astype(jnp.float32)


def focal_inputs(first_full, block_vectors, focal_block):
    channels = focal_block.shape[-1]
    joined = focal_block.astype(jnp.bfloat16).reshape(focal_block.shape[0], 2 * channels)
    both = matmul(first_full, joined).reshape(first_full.shape[0], 2, channels)
    gates = matmul(first_full, block_vectors[6:10].astype(jnp.bfloat16).T)
    return (both[:, 0], both[:, 1], gates, joined)


def block_forward(
    residual, block_vectors, focal_block, mixer_block, mlp_block, kernel_block, keep_block, validity
):
    local_rows = residual.shape[0]
    proj_low = mixer_block[1].astype(jnp.bfloat16)
    down_low = mlp_block[1].astype(jnp.bfloat16)
    first_low = layer_norm(residual, block_vectors[0], block_vectors[1]).astype(jnp.bfloat16)
    first_full = gather_rows(first_low)
    query, context, gates, joined = focal_inputs(first_full, block_vectors, focal_block)
    context_low = focal_levels(context, gates, kernel_block, validity).astype(jnp.bfloat16)
    context_full = lax.all_gather(context_low, "chan", axis=1, tiled=True)
    modulator = matmul(context_full, mixer_block[0].astype(jnp.bfloat16))
    product = (query * modulator).astype(jnp.bfloat16)

    def projection_rows(row_start, row_count):
        return times_transposed(product, proj_low)

    projected = reduce_rows(projection_rows, local_rows)
    middle = residual + keep_block[:, 0:1] * (projected + block_vectors[4])
    second_low = layer_norm(middle, block_vectors[2], block_vectors[3]).astype(jnp.bfloat16)
    second_full = gather_rows(second_low)
    hidden = exact_gelu(matmul(second_full, mlp_block[0].astype(jnp.bfloat16))).astype(jnp.bfloat16)

    def down_rows(row_start, row_count):
        return times_transposed(hidden, down_low)

    lowered = reduce_rows(down_rows, local_rows)
    output = middle + keep_block[:, 1:2] * (lowered + block_vectors[5])
    saved = (residual, middle, None, None, None)
    return (output, saved)


def block_backward(
    d_residual,
    saved,
    block_vectors,
    focal_block,
    mixer_block,
    mlp_block,
    kernel_block,
    keep_block,
    validity,
):
    residual, middle, first_kept, context_kept, second_kept = saved
    local_rows = residual.shape[0]
    second_full = regather_rows(
        layer_norm(middle, block_vectors[2], block_vectors[3]).astype(jnp.bfloat16)
    )
    up_low = mlp_block[0].astype(jnp.bfloat16)
    down_low = mlp_block[1].astype(jnp.bfloat16)
    hidden_value, gelu_back = jax.vjp(exact_gelu, matmul(second_full, up_low))
    hidden = hidden_value.astype(jnp.bfloat16)
    d_down = d_residual * keep_block[:, 1:2]
    d_down_full = gather_grads(d_down.astype(jnp.bfloat16))
    grad_down = contract_rows(d_down_full, hidden)
    d_pre = gelu_back(matmul(d_down_full, down_low))[0].astype(jnp.bfloat16)
    grad_up = contract_rows(second_full, d_pre)

    def up_rows(row_start, row_count):
        return times_transposed(d_pre, up_low)

    d_second = reduce_inputs(up_rows, local_rows)
    second_value, second_back = jax.vjp(layer_norm, middle, block_vectors[2], block_vectors[3])
    d_middle, grad_gain_two, grad_shift_two = second_back(d_second)
    d_middle = d_middle + d_residual
    first_full = regather_rows(
        layer_norm(residual, block_vectors[0], block_vectors[1]).astype(jnp.bfloat16)
    )
    query, context, gates, joined = focal_inputs(first_full, block_vectors, focal_block)

    def levels(context_in, gates_in, kernel_in):
        return focal_levels(context_in, gates_in, kernel_in, validity)

    context_sum, levels_back = jax.vjp(levels, context, gates, kernel_block)
    context_full = lax.all_gather(context_sum.astype(jnp.bfloat16), "chan", axis=1, tiled=True)
    mix_low = mixer_block[0].astype(jnp.bfloat16)
    modulator = matmul(context_full, mix_low)
    product = (query * modulator).astype(jnp.bfloat16)
    proj_low = mixer_block[1].astype(jnp.bfloat16)
    d_proj = d_middle * keep_block[:, 0:1]
    d_proj_full = gather_grads(d_proj.astype(jnp.bfloat16))
    grad_proj = contract_rows(d_proj_full, product)
    d_product = matmul(d_proj_full, proj_low)
    d_query = (d_product * modulator).astype(jnp.bfloat16)
    d_modulator = (d_product * query).astype(jnp.bfloat16)
    grad_mix = contract_rows(context_full, d_modulator)
    d_context_sum = lax.psum_scatter(
        times_transposed(d_modulator, mix_low).astype(jnp.bfloat16),
        "chan",
        scatter_dimension=1,
        tiled=True,
    ).astype(jnp.float32)
    d_context, d_gates, grad_kernel = levels_back(d_context_sum)
    d_both = jnp.stack([d_query, d_context.astype(jnp.bfloat16)], axis=1).reshape(
        first_full.shape[0], -1
    )
    grad_focal = contract_rows(first_full, d_both).reshape(focal_block.shape)
    gate_high, gate_rest = split_low(d_gates)
    grad_gate = contract_rows(first_full, gate_high) + contract_rows(first_full, gate_rest)
    gate_low = block_vectors[6:10].astype(jnp.bfloat16)

    def first_rows(row_start, row_count):
        return (
            times_transposed(d_both, joined)
            + matmul(gate_high, gate_low)
            + matmul(gate_rest, gate_low)
        )

    d_first = reduce_inputs(first_rows, local_rows)
    first_value, first_back = jax.vjp(layer_norm, residual, block_vectors[0], block_vectors[1])
    d_input, grad_gain_one, grad_shift_one = first_back(d_first)
    d_input = d_input + d_middle
    grad_vectors = jnp.concatenate(
        [
            jnp.stack(
                [
                    grad_gain_one,
                    grad_shift_one,
                    grad_gain_two,
                    grad_shift_two,
                    jnp.sum(d_proj, axis=0),
                    jnp.sum(d_down, axis=0),
                ]
            ),
            grad_gate.T,
        ],
        axis=0,
    )
    return (
        d_input,
        grad_vectors,
        grad_focal,
        jnp.stack([grad_mix, grad_proj]),
        jnp.stack([grad_up, grad_down]),
        grad_kernel,
    )


def nesterov(weight, moment, gradient, rate):
    new_moment = MOMENTUM * moment + gradient
    new_weight = weight - rate * (gradient + MOMENTUM * new_moment)
    return (new_weight, new_moment)


def shards(
    patches,
    valid_mask,
    target_mask,
    keep_mask,
    embed_weight,
    embed_moment,
    head_weight,
    head_moment,
    vectors,
    vector_moment,
    vector_average,
    focal_input,
    focal_moment,
    focal_average,
    mixers,
    mixer_moment,
    mixer_average,
    mlp_weights,
    mlp_moment,
    mlp_average,
    kernels,
    kernel_moment,
    kernel_average,
):
    local_rows = patches.shape[0]
    group_rows = valid_mask.shape[0]
    first_row = lax.axis_index("chan") * local_rows
    outer = 10 * BLOCKS
    validity = valid_mask.astype(jnp.float32)
    valid_local = lax.dynamic_slice_in_dim(validity, first_row, local_rows)[:, None]
    masked_local = lax.dynamic_slice_in_dim(target_mask, first_row, local_rows).astype(jnp.float32)[
        :, None
    ]
    loss_weight = masked_local * valid_local
    counted = lax.psum(jnp.sum(loss_weight), ("dp", "chan"))
    denominator = counted * PATCH_IN
    keep_rows = jnp.repeat(keep_mask.astype(jnp.float32) / KEEP_RATE, GRID * GRID, axis=0)
    keep_local = lax.dynamic_slice_in_dim(keep_rows, first_row, local_rows)
    embed_low = embed_weight.astype(jnp.bfloat16)
    embed_full = matmul(patches, embed_low) + vectors[outer]
    start_state = layer_norm(embed_full, vectors[outer + 1], vectors[outer + 2])
    residual = start_state * (1.0 - masked_local) + vectors[outer + 5] * masked_local
    saved_blocks = []
    for block_index in range(BLOCKS):
        residual, saved = block_forward(
            residual,
            vectors[10 * block_index : 10 * block_index + 10],
            focal_input[block_index],
            mixers[block_index],
            mlp_weights[block_index],
            kernels[block_index],
            keep_local[:, block_index],
            validity,
        )
        saved_blocks.append(saved)
    final_low = layer_norm(residual, vectors[outer + 3], vectors[outer + 4]).astype(jnp.bfloat16)
    head_low = head_weight.astype(jnp.bfloat16)
    error = matmul(final_low, head_low) - patches.astype(jnp.float32)
    loss_part = jnp.sum(loss_weight * error * error) / denominator
    d_prediction = (2.0 * loss_weight * error / denominator).astype(jnp.bfloat16)
    grad_head = contract_rows(final_low, d_prediction)
    d_final = times_transposed(d_prediction, head_low)
    final_value, final_back = jax.vjp(layer_norm, residual, vectors[outer + 3], vectors[outer + 4])
    d_residual, grad_final_gain, grad_final_shift = final_back(d_final)
    vector_parts = [None] * BLOCKS
    focal_parts = [None] * BLOCKS
    mixer_parts = [None] * BLOCKS
    mlp_parts = [None] * BLOCKS
    kernel_parts = [None] * BLOCKS
    for block_index in reversed(range(BLOCKS)):
        d_residual, grad_vec, grad_focal, grad_mixer, grad_mlp, grad_kernel = block_backward(
            d_residual,
            saved_blocks[block_index],
            vectors[10 * block_index : 10 * block_index + 10],
            focal_input[block_index],
            mixers[block_index],
            mlp_weights[block_index],
            kernels[block_index],
            keep_local[:, block_index],
            validity,
        )
        vector_parts[block_index] = grad_vec
        focal_parts[block_index] = grad_focal
        mixer_parts[block_index] = grad_mixer
        mlp_parts[block_index] = grad_mlp
        kernel_parts[block_index] = grad_kernel
    d_start = d_residual * (1.0 - masked_local)
    grad_token = jnp.sum(d_residual * masked_local, axis=0)
    embed_value, embed_back = jax.vjp(
        layer_norm, embed_full, vectors[outer + 1], vectors[outer + 2]
    )
    d_embed, grad_embed_gain, grad_embed_shift = embed_back(d_start)
    grad_embed = contract_rows(patches, d_embed.astype(jnp.bfloat16))
    outer_grads = jnp.stack(
        [
            jnp.sum(d_embed, axis=0),
            grad_embed_gain,
            grad_embed_shift,
            grad_final_gain,
            grad_final_shift,
            grad_token,
        ]
    )
    grad_vectors = jnp.concatenate(vector_parts + [outer_grads], axis=0)
    grad_embed, grad_head, grad_vectors, loss = lax.psum(
        (grad_embed, grad_head, grad_vectors, loss_part), ("dp", "chan")
    )
    grad_focal = jnp.stack(focal_parts)
    grad_mixer = jnp.stack(mixer_parts)
    grad_mlp = jnp.stack(mlp_parts)
    grad_kernel = jnp.stack(kernel_parts)
    grad_focal, grad_mixer, grad_mlp, grad_kernel = (
        lax.psum(grad_focal.astype(jnp.bfloat16), "dp").astype(jnp.float32),
        lax.psum(grad_mixer.astype(jnp.bfloat16), "dp").astype(jnp.float32),
        lax.psum(grad_mlp.astype(jnp.bfloat16), "dp").astype(jnp.float32),
        lax.psum(grad_kernel.astype(jnp.bfloat16), "dp").astype(jnp.float32),
    )
    rate = 0.2 * math.sqrt(group_rows * lax.axis_size("dp"))
    new_embed, new_embed_moment = nesterov(embed_weight, embed_moment, grad_embed, rate)
    new_head, new_head_moment = nesterov(head_weight, head_moment, grad_head, rate)
    results = []
    for weight, moment, average, gradient in (
        (vectors, vector_moment, vector_average, grad_vectors),
        (focal_input, focal_moment, focal_average, grad_focal),
        (mixers, mixer_moment, mixer_average, grad_mixer),
        (mlp_weights, mlp_moment, mlp_average, grad_mlp),
        (kernels, kernel_moment, kernel_average, grad_kernel),
    ):
        new_weight, new_moment = nesterov(weight, moment, gradient, rate)
        results.append((new_weight, new_moment, AVERAGE * average + (1.0 - AVERAGE) * new_weight))
    return (
        loss,
        new_embed,
        new_embed_moment,
        new_head,
        new_head_moment,
        results[0][0],
        results[0][1],
        results[0][2],
        results[1][0],
        results[1][1],
        results[1][2],
        results[2][0],
        results[2][1],
        results[2][2],
        results[3][0],
        results[3][1],
        results[3][2],
        results[4][0],
        results[4][1],
        results[4][2],
    )


def solution(mesh):
    return jax.shard_map(
        shards,
        mesh=mesh,
        in_specs=(
            P(("dp", "chan"), None),
            P("dp"),
            P("dp"),
            P("dp", None, None),
            P(),
            P(),
            P(),
            P(),
            P(),
            P(),
            P(),
            P(None, None, None, "chan"),
            P(None, None, None, "chan"),
            P(None, None, None, "chan"),
            P(None, None, None, "chan"),
            P(None, None, None, "chan"),
            P(None, None, None, "chan"),
            P(None, None, None, "chan"),
            P(None, None, None, "chan"),
            P(None, None, None, "chan"),
            P(None, None, "chan"),
            P(None, None, "chan"),
            P(None, None, "chan"),
        ),
        out_specs=(
            P(),
            P(),
            P(),
            P(),
            P(),
            P(),
            P(),
            P(),
            P(None, None, None, "chan"),
            P(None, None, None, "chan"),
            P(None, None, None, "chan"),
            P(None, None, None, "chan"),
            P(None, None, None, "chan"),
            P(None, None, None, "chan"),
            P(None, None, None, "chan"),
            P(None, None, None, "chan"),
            P(None, None, None, "chan"),
            P(None, None, "chan"),
            P(None, None, "chan"),
            P(None, None, "chan"),
        ),
        check_vma=False,
    )
```

profile of v0, /device:TPU:0, one launch (start us, length us, event | category | flops | bytes accessed | tf_op | source)
XLA Modules:
  0.0 1619.3 jit_solution(6386499638076548524)
XLA Ops:
  20.7 41.1 %all-gather.11.cloned.1.call-done = bf16[2048,384]{1,0:T(8,128)(2,1)} async-done(((bf16[256,384]{1,0:T(8,128)(2,1)}), bf16[2048,384]{1,0:T(8,128)(2,1)}) %all-gather.11.cloned.1.call-update) | async-done | bytes 1572880 | tf_op jit(solution)/shard_map/all_gather | solution.py:85
  94.1 41.6 %all-gather.13.cloned.1.call-done = bf16[2048,384]{0,1:T(8,128)(2,1)} async-done(((bf16[2048,48]{0,1:T(8,128)(2,1)}), bf16[2048,384]{0,1:T(8,128)(2,1)}) %all-gather.13.cloned.1.call-update) | async-done | bytes 1572880 | tf_op jit(solution)/shard_map/all_gather | solution.py:132
  140.9 63.0 %reduce-scatter.11.cloned.1.call-done = bf16[256,384]{1,0:T(8,128)(2,1)} async-done(((bf16[2048,384]{1,0:T(8,128)(2,1)}), bf16[256,384]{1,0:T(8,128)(2,1)}) %reduce-scatter.11.cloned.1.call-update) | async-done | bytes 196624 | tf_op jit(solution)/shard_map/reduce_scatter | solution.py:97
  207.8 42.3 %all-gather.15.cloned.1.call-done = bf16[2048,384]{1,0:T(8,128)(2,1)} async-done(((bf16[256,384]{1,0:T(8,128)(2,1)}), bf16[2048,384]{1,0:T(8,128)(2,1)}) %all-gather.15.cloned.1.call-update) | async-done | bytes 1572880 | tf_op jit(solution)/shard_map/all_gather | solution.py:85
  260.5 63.7 %reduce-scatter.13.cloned.1.call-done = bf16[256,384]{1,0:T(8,128)(2,1)} async-done(((bf16[2048,384]{1,0:T(8,128)(2,1)}), bf16[256,384]{1,0:T(8,128)(2,1)}) %reduce-scatter.13.cloned.1.call-update) | async-done | bytes 196624 | tf_op jit(solution)/shard_map/reduce_scatter | solution.py:97
  331.1 38.9 %all-gather.17.cloned.1.call-done = bf16[2048,384]{1,0:T(8,128)(2,1)} async-done(((bf16[256,384]{1,0:T(8,128)(2,1)}), bf16[2048,384]{1,0:T(8,128)(2,1)}) %all-gather.17.cloned.1.call-update) | async-done | bytes 1572880 | tf_op jit(solution)/shard_map/all_gather | solution.py:85
  403.6 43.1 %all-gather.19.cloned.1.call-done = bf16[2048,384]{0,1:T(8,128)(2,1)} async-done(((bf16[2048,48]{0,1:T(8,128)(2,1)}), bf16[2048,384]{0,1:T(8,128)(2,1)}) %all-gather.19.cloned.1.call-update) | async-done | bytes 1572880 | tf_op jit(solution)/shard_map/all_gather | solution.py:132
  451.2 63.7 %reduce-scatter.15.cloned.1.call-done = bf16[256,384]{1,0:T(8,128)(2,1)} async-done(((bf16[2048,384]{1,0:T(8,128)(2,1)}), bf16[256,384]{1,0:T(8,128)(2,1)}) %reduce-scatter.15.cloned.1.call-update) | async-done | bytes 196624 | tf_op jit(solution)/shard_map/reduce_scatter | solution.py:97
  517.3 43.7 %all-gather.21.cloned.1.call-done = bf16[2048,384]{1,0:T(8,128)(2,1)} async-done(((bf16[256,384]{1,0:T(8,128)(2,1)}), bf16[2048,384]{1,0:T(8,128)(2,1)}) %all-gather.21.cloned.1.call-update) | async-done | bytes 1572880 | tf_op jit(solution)/shard_map/all_gather | solution.py:85
  572.7 39.9 %psum.63 = f32[]{:T(128)} all-reduce(f32[]{:T(128)} %reduce_sum.1980), channel_id=1, replica_groups=mesh['dp'=4,'chan'=8] {'dp','chan'}, use_global_device_ids=true, to_apply=%region_21.22 | all-reduce | flops 1 | bytes 8 | tf_op jit(solution)/shard_map/psum | solution.py:301
  613.3 22.0 %reduce-scatter.17.cloned.1.call-done = bf16[256,384]{1,0:T(8,128)(2,1)} async-done(((bf16[2048,384]{1,0:T(8,128)(2,1)}), bf16[256,384]{1,0:T(8,128)(2,1)}) %reduce-scatter.17.cloned.1.call-update) | async-done | bytes 196624 | tf_op jit(solution)/shard_map/reduce_scatter | solution.py:97
  641.7 43.2 %all-gather.23.cloned.1.call-done = bf16[2048,384]{1,0:T(8,128)(2,1)} async-done(((bf16[256,384]{1,0:T(8,128)(2,1)}), bf16[2048,384]{1,0:T(8,128)(2,1)}) %all-gather.23.cloned.1.call-update) | async-done | bytes 1572880 | tf_op jit(solution)/shard_map/all_gather | solution.py:89
  691.2 63.8 %reduce-scatter.19.cloned.1.call-done = bf16[256,384]{1,0:T(8,128)(2,1)} async-done(((bf16[2048,384]{1,0:T(8,128)(2,1)}), bf16[256,384]{1,0:T(8,128)(2,1)}) %reduce-scatter.19.cloned.1.call-update) | async-done | bytes 196624 | tf_op jit(solution)/shard_map/reduce_scatter | solution.py:106
  761.8 43.2 %all-gather.25.cloned.1.call-done = bf16[2048,384]{1,0:T(8,128)(2,1)} async-done(((bf16[256,384]{1,0:T(8,128)(2,1)}), bf16[2048,384]{1,0:T(8,128)(2,1)}) %all-gather.25.cloned.1.call-update) | async-done | bytes 1572880 | tf_op jit(solution)/shard_map/all_gather | solution.py:89
  810.7 62.5 %reduce-scatter.21.cloned.1.call-done = bf16[2048,48]{0,1:T(8,128)(2,1)} async-done(((bf16[2048,384]{0,1:T(8,128)(2,1)}), bf16[2048,48]{0,1:T(8,128)(2,1)}) %reduce-scatter.21.cloned.1.call-update) | async-done | bytes 196624 | tf_op jit(solution)/shard_map/reduce_scatter | solution.py:208
  971.5 63.6 %reduce-scatter.23.cloned.1.call-done = bf16[256,384]{1,0:T(8,128)(2,1)} async-done(((bf16[2048,384]{1,0:T(8,128)(2,1)}), bf16[256,384]{1,0:T(8,128)(2,1)}) %reduce-scatter.23.cloned.1.call-update) | async-done | bytes 196624 | tf_op jit(solution)/shard_map/reduce_scatter | solution.py:106
  1039.5 43.2 %all-gather.27.cloned.1.call-done = bf16[2048,384]{1,0:T(8,128)(2,1)} async-done(((bf16[256,384]{1,0:T(8,128)(2,1)}), bf16[2048,384]{1,0:T(8,128)(2,1)}) %all-gather.27.cloned.1.call-update) | async-done | bytes 1572880 | tf_op jit(solution)/shard_map/all_gather | solution.py:89
  1090.0 63.9 %reduce-scatter.25.cloned.1.call-done = bf16[256,384]{1,0:T(8,128)(2,1)} async-done(((bf16[2048,384]{1,0:T(8,128)(2,1)}), bf16[256,384]{1,0:T(8,128)(2,1)}) %reduce-scatter.25.cloned.1.call-update) | async-done | bytes 196624 | tf_op jit(solution)/shard_map/reduce_scatter | solution.py:106
  1180.2 23.0 %all-gather.29.cloned.1.call-done = bf16[2048,384]{1,0:T(8,128)(2,1)} async-done(((bf16[256,384]{1,0:T(8,128)(2,1)}), bf16[2048,384]{1,0:T(8,128)(2,1)}) %all-gather.29.cloned.1.call-update) | async-done | bytes 1572880 | tf_op jit(solution)/shard_map/all_gather | solution.py:89
  1235.3 37.1 %reduce-scatter.27.cloned.1.call-done = bf16[2048,48]{0,1:T(8,128)(2,1)} async-done(((bf16[2048,384]{0,1:T(8,128)(2,1)}), bf16[2048,48]{0,1:T(8,128)(2,1)}) %reduce-scatter.27.cloned.1.call-update) | async-done | bytes 196624 | tf_op jit(solution)/shard_map/reduce_scatter | solution.py:208
  1391.1 31.2 %reduce-scatter.29.cloned.1.call-done = bf16[256,384]{1,0:T(8,128)(2,1)} async-done(((bf16[2048,384]{1,0:T(8,128)(2,1)}), bf16[256,384]{1,0:T(8,128)(2,1)}) %reduce-scatter.29.cloned.1.call-update) | async-done | bytes 196624 | tf_op jit(solution)/shard_map/reduce_scatter | solution.py:106
  1428.0 31.7 %all-reduce.360.cloned.1.call-done = (bf16[2,384,2,48]{1,3,2,0:T(8,128)(2,1)}, bf16[2,2,384,48]{2,3,1,0:T(8,128)(2,1)}, bf16[2,2,384,192]{2,3,1,0:T(8,128)(2,1)}) async-done(((bf16[2,384,2,48]{1,3,2,0:T(8,128)(2,1)}, bf16[2,2,384,48]{2,3,1,0:T(8,128)(2,1)}, bf16[2,2,384,192]{2,3,1,0:T(8,128)(2,1)}), (bf16[2,384,2,48]{1,3,2,0:T(8,128)(2,1)}, bf16[2,2,384,48]{2,3,1,0:T(8,128)(2,1)}, ...) | async-done | bytes 884752 | tf_op jit(solution)/shard_map/psum | solution.py:379
  1473.5 40.2 %all-reduce.352 = (f32[]{:T(128)}, f32[26,384]{1,0:T(8,128)S(1)}) all-reduce(f32[]{:T(128)S(6)} %div.214, f32[26,384]{1,0:T(8,128)S(1)} %concatenate.3), channel_id=1, replica_groups=mesh['dp'=4,'chan'=8] {'dp','chan'}, use_global_device_ids=true, to_apply=%region_22.23 | all-reduce | flops 9985 | bytes 79880 | tf_op jit(solution)/shard_map/psum | solution.py:371
  1514.4 87.5 %all-reduce.358.cloned.1.call-done = (f32[768,384]{0,1:T(8,128)}, f32[384,768]{1,0:T(8,128)}) async-done(((f32[768,384]{0,1:T(8,128)}, f32[384,768]{1,0:T(8,128)}), (f32[768,384]{0,1:T(8,128)}, f32[384,768]{1,0:T(8,128)})) %all-reduce.358.cloned.1.call-update) | async-done | bytes 2359312 | tf_op jit(solution)/shard_map/psum | solution.py:371
  (1431 shorter events, 458.9 us)
Async XLA Ops:
  7.2 54.6 %all-gather.11.cloned.1.call-start = ((), (), s32[]{:S(2)}) async-start(), calls=%async_computation.10 | async-start | bytes 1769472 | tf_op jit(solution)/shard_map/all_gather | solution.py:85
  9.7 630.3 %copy-start.166 = (f32[384]{0:T(512)}, f32[384]{0:T(512)S(1)}, u32[]{:S(2)}) copy-start(f32[384]{0:T(512)S(1)} %get-tuple-element.275) | copy-start | bytes 4612
  14.8 121.0 %all-gather.13.cloned.1.call-start = ((), (), s32[]{:S(2)}) async-start(), calls=%async_computation.11 | async-start | bytes 1769472 | tf_op jit(solution)/shard_map/all_gather | solution.py:132
  15.1 384.3 %copy-start.193 = (f32[8]{0:T(128)}, f32[8]{0:T(128)S(1)}, u32[]{:S(2)}) copy-start(f32[8]{0:T(128)S(1)} %reduce_sum.1960) | copy-start | bytes 100
  92.6 111.3 %reduce-scatter.11.cloned.1.call-start = ((), (), s32[]{:S(2)}) async-start(), calls=%async_computation.12 | async-start | bytes 1769472 | tf_op jit(solution)/shard_map/reduce_scatter | solution.py:97
  140.2 109.9 %all-gather.15.cloned.1.call-start = ((), (), s32[]{:S(2)}) async-start(), calls=%async_computation.13 | async-start | bytes 1769472 | tf_op jit(solution)/shard_map/all_gather | solution.py:85
  206.8 117.4 %reduce-scatter.13.cloned.1.call-start = ((), (), s32[]{:S(2)}) async-start(), calls=%async_computation.14 | async-start | bytes 1769472 | tf_op jit(solution)/shard_map/reduce_scatter | solution.py:97
  260.5 109.5 %all-gather.17.cloned.1.call-start = ((), (), s32[]{:S(2)}) async-start(), calls=%async_computation.15 | async-start | bytes 1769472 | tf_op jit(solution)/shard_map/all_gather | solution.py:85
  326.5 120.2 %all-gather.19.cloned.1.call-start = ((), (), s32[]{:S(2)}) async-start(), calls=%async_computation.16 | async-start | bytes 1769472 | tf_op jit(solution)/shard_map/all_gather | solution.py:132
  403.6 111.3 %reduce-scatter.15.cloned.1.call-start = ((), (), s32[]{:S(2)}) async-start(), calls=%async_computation.17 | async-start | bytes 1769472 | tf_op jit(solution)/shard_map/reduce_scatter | solution.py:97
  451.1 109.9 %all-gather.21.cloned.1.call-start = ((), (), s32[]{:S(2)}) async-start(), calls=%async_computation.18 | async-start | bytes 1769472 | tf_op jit(solution)/shard_map/all_gather | solution.py:85
  517.1 118.3 %reduce-scatter.17.cloned.1.call-start = ((), (), s32[]{:S(2)}) async-start(), calls=%async_computation.19 | async-start | bytes 1769472 | tf_op jit(solution)/shard_map/reduce_scatter | solution.py:97
  571.3 113.6 %all-gather.23.cloned.1.call-start = ((), (), s32[]{:S(2)}) async-start(), calls=%async_computation.20 | async-start | bytes 1769472 | tf_op jit(solution)/shard_map/all_gather | solution.py:89
  641.7 113.3 %reduce-scatter.19.cloned.1.call-start = ((), (), s32[]{:S(2)}) async-start(), calls=%async_computation.21 | async-start | bytes 1769472 | tf_op jit(solution)/shard_map/reduce_scatter | solution.py:106
  691.1 113.9 %all-gather.25.cloned.1.call-start = ((), (), s32[]{:S(2)}) async-start(), calls=%async_computation.22 | async-start | bytes 1769472 | tf_op jit(solution)/shard_map/all_gather | solution.py:89
  761.7 111.5 %reduce-scatter.21.cloned.1.call-start = ((), (), s32[]{:S(2)}) async-start(), calls=%async_computation.23 | async-start | bytes 1769472 | tf_op jit(solution)/shard_map/reduce_scatter | solution.py:208
  809.5 225.6 %reduce-scatter.23.cloned.1.call-start = ((), (), s32[]{:S(2)}) async-start(), calls=%async_computation.24 | async-start | bytes 1769472 | tf_op jit(solution)/shard_map/reduce_scatter | solution.py:106
  971.3 111.5 %all-gather.27.cloned.1.call-start = ((), (), s32[]{:S(2)}) async-start(), calls=%async_computation.25 | async-start | bytes 1769472 | tf_op jit(solution)/shard_map/all_gather | solution.py:89
  1039.5 114.4 %reduce-scatter.25.cloned.1.call-start = ((), (), s32[]{:S(2)}) async-start(), calls=%async_computation.26 | async-start | bytes 1769472 | tf_op jit(solution)/shard_map/reduce_scatter | solution.py:106
  1090.0 113.2 %all-gather.29.cloned.1.call-start = ((), (), s32[]{:S(2)}) async-start(), calls=%async_computation.27 | async-start | bytes 1769472 | tf_op jit(solution)/shard_map/all_gather | solution.py:89
  1159.9 112.5 %reduce-scatter.27.cloned.1.call-start = ((), (), s32[]{:S(2)}) async-start(), calls=%async_computation.28 | async-start | bytes 1769472 | tf_op jit(solution)/shard_map/reduce_scatter | solution.py:208
  1208.6 213.7 %reduce-scatter.29.cloned.1.call-start = ((), (), s32[]{:S(2)}) async-start(), calls=%async_computation.29 | async-start | bytes 1769472 | tf_op jit(solution)/shard_map/reduce_scatter | solution.py:106
  1358.4 101.2 %all-reduce.360.cloned.1.call-start = ((), (), s32[]{:S(2)}) async-start(), calls=%async_computation.31 | async-start | bytes 1769472 | tf_op jit(solution)/shard_map/psum | solution.py:379
  1389.5 212.4 %all-reduce.358.cloned.1.call-start = ((), (), s32[]{:S(2)}) async-start(), calls=%async_computation.30 | async-start | bytes 4718592 | tf_op jit(solution)/shard_map/psum | solution.py:371
  (566 other events, 8438.2 us)
Sparse Core Ops, SparseCore 0:
  14.9 46.8 all-gather.10
  92.7 42.9 all-gather.12
  140.3 63.5 reduce-scatter.10
  206.9 43.0 all-gather.14
  260.6 63.5 reduce-scatter.12
  326.9 43.1 all-gather.16
  403.7 42.9 all-gather.18
  451.2 63.5 reduce-scatter.14
  517.9 43.1 all-gather.20
  571.5 63.8 reduce-scatter.16
  641.8 43.1 all-gather.22
  691.2 63.6 reduce-scatter.18
  761.8 43.1 all-gather.24
  809.6 63.5 reduce-scatter.20
  971.4 63.6 reduce-scatter.22
  1039.6 43.1 all-gather.26
  1090.1 63.7 reduce-scatter.24
  1160.1 43.0 all-gather.28
  1208.7 63.6 reduce-scatter.26
  1358.5 63.7 reduce-scatter.28
  1425.4 34.2 all-reduce.359
  1465.9 135.8 all-reduce.357
where the time goes:
time: 1630 us; the launch traced here: 1620 us
  waiting for transfers between devices  1060 us (65%)
  other arithmetic  289 us (18%)
  blocking collectives  91.1 us (6%)
  matrix products  89.7 us (6%)
  local copies, waits for them, and re-layouts  66.8 us (4%)
  between operations  23.3 us (1%)
    reduce_scatter x4, waiting for transfers between devices, reduce_inputs(): lax.psum_scatter(row_terms(jnp.int32(0), lax.axis_size('chan') * row_tota...  222 us
    reduce_scatter x4, waiting for transfers between devices, reduce_rows(): lax.psum_scatter(row_terms(jnp.int32(0), lax.axis_size('chan') * row_tota...  212 us
    all_gather x4, waiting for transfers between devices, gather_rows(): return lax.all_gather(values, 'chan', axis=0, tiled=True)  166 us
    all_gather x4, waiting for transfers between devices, gather_grads(): return lax.all_gather(values, 'chan', axis=0, tiled=True)  153 us
    reduce_scatter x2, waiting for transfers between devices, block_backward(): lax.psum_scatter(times_transposed(d_modulator, mix_low).astype(jnp.bfloat...  99.6 us
    psum x1, waiting for transfers between devices, shards(): lax.psum((grad_embed, grad_head, grad_vectors, loss_part), ('dp', 'chan'))  87.5 us
    all_gather x2, waiting for transfers between devices, block_forward(): context_full = lax.all_gather(context_low, 'chan', axis=1, tiled=True)  84.7 us
    reduce_sum x12, other arithmetic, depthwise(): window * kernel_taps[kernel_row * kernel_width + kernel_col]  79.8 us
  transfers between devices with their start and end apart: 22, of which 22 were waited for; matrix products, arithmetic and copies ran while one was open for 6% of the time, Pallas kernels for 0%

commit v1 on v0

v1 whole, which is shorter than its diff:
```python
import math

import jax
import jax.numpy as jnp
from jax import lax
from jax.sharding import PartitionSpec as P

PATCH_IN = 768
GRID = 16
BLOCKS = 2
IMAGE_ROWS = GRID * GRID

EPS = 1e-05
MOMENTUM = 0.9
AVERAGE = 0.5
KEEP_RATE = 0.8
KERNEL_SIZES = (3, 5, 7)
KERNEL_STARTS = (0, 9, 34)
ROOT_HALF = math.sqrt(0.5)
DENSITY = 1.0 / math.sqrt(2.0 * math.pi)


def matmul(left, right):
    return jnp.dot(left, right, preferred_element_type=jnp.float32)


def contract_rows(left, right):
    return lax.dot_general(
        left, right, (((0,), (0,)), ((), ())), preferred_element_type=jnp.float32
    )


def times_transposed(left, right):
    return lax.dot_general(
        left, right, (((1,), (1,)), ((), ())), preferred_element_type=jnp.float32
    )


def split_low(values):
    high_part = values.astype(jnp.bfloat16)
    rest_part = (values - high_part.astype(jnp.float32)).astype(jnp.bfloat16)
    return (high_part, rest_part)


def normalize(values):
    average = jnp.mean(values, axis=-1, keepdims=True)
    centred = values - average
    variance = jnp.mean(centred * centred, axis=-1, keepdims=True)
    scale = lax.rsqrt(variance + EPS)
    return (centred * scale, scale)


def norm_backward(grad, unit, scale, gain):
    d_unit = grad * gain
    mean_one = jnp.mean(d_unit, axis=-1, keepdims=True)
    mean_two = jnp.mean(d_unit * unit, axis=-1, keepdims=True)
    d_values = (d_unit - mean_one - unit * mean_two) * scale
    return (
        d_values,
        jnp.sum(grad * unit, axis=0, keepdims=True),
        jnp.sum(grad, axis=0, keepdims=True),
    )


def gelu_pair(values):
    cumulative = 0.5 + 0.5 * lax.erf(values * ROOT_HALF)
    density = DENSITY * jnp.exp(-0.5 * values * values)
    return (values * cumulative, cumulative + values * density)


def depthwise(field, kernel_taps, kernel_width):
    margin = kernel_width // 2
    padded = jnp.pad(field, ((0, 0), (margin, margin), (margin, margin), (0, 0)))
    summed = jnp.zeros_like(field)
    for kernel_row in range(kernel_width):
        for kernel_col in range(kernel_width):
            window = padded[:, kernel_row : kernel_row + GRID, kernel_col : kernel_col + GRID, :]
            summed = summed + window * kernel_taps[kernel_row * kernel_width + kernel_col]
    return summed


def depthwise_taps(field, grad, kernel_width):
    margin = kernel_width // 2
    padded = jnp.pad(field, ((0, 0), (margin, margin), (margin, margin), (0, 0)))
    rows = []
    for kernel_row in range(kernel_width):
        for kernel_col in range(kernel_width):
            window = padded[:, kernel_row : kernel_row + GRID, kernel_col : kernel_col + GRID, :]
            rows.append(jnp.sum(window * grad, axis=(0, 1, 2)))
    return jnp.stack(rows)


def level_taps(kernel_block, level_index):
    kernel_width = KERNEL_SIZES[level_index]
    first_tap = KERNEL_STARTS[level_index]
    return kernel_block[first_tap : first_tap + kernel_width * kernel_width]


def focal_forward(context, gates, kernel_block, validity):
    images = validity.shape[0] // IMAGE_ROWS
    grid = lambda a: a.reshape(images, GRID, GRID, a.shape[-1])
    current = grid(context)
    gate_grid = grid(gates)
    valid_grid = grid(validity)
    summed = jnp.zeros_like(current)
    fields = [current]
    slopes = []
    for level_index in range(3):
        taps = level_taps(kernel_block, level_index)
        current, slope = gelu_pair(depthwise(current, taps, KERNEL_SIZES[level_index]))
        summed = summed + current * gate_grid[..., level_index : level_index + 1]
        fields.append(current)
        slopes.append(slope)
    valid_total = jnp.sum(valid_grid, axis=(1, 2), keepdims=True)
    pooled, pooled_slope = gelu_pair(
        jnp.sum(current * valid_grid, axis=(1, 2), keepdims=True) / valid_total
    )
    summed = summed + pooled * gate_grid[..., 3:4]
    return (
        summed.reshape(context.shape).astype(jnp.bfloat16),
        (fields, slopes, pooled, pooled_slope / valid_total),
    )


def focal_backward(d_summed, gates, kernel_block, validity, saved):
    fields, slopes, pooled, pooled_slope = saved
    images = validity.shape[0] // IMAGE_ROWS
    grid = lambda a: a.reshape(images, GRID, GRID, a.shape[-1])
    d_sum = grid(d_summed)
    gate_grid = grid(gates)
    valid_grid = grid(validity)
    d_pooled = jnp.sum(d_sum * gate_grid[..., 3:4], axis=(1, 2), keepdims=True)
    d_field = d_pooled * pooled_slope * valid_grid
    gate_cols = [None, None, None, jnp.sum(d_sum * pooled, axis=-1, keepdims=True)]
    tap_rows = [None, None, None]
    for level_index in reversed(range(3)):
        width = KERNEL_SIZES[level_index]
        gate_cols[level_index] = jnp.sum(d_sum * fields[level_index + 1], axis=-1, keepdims=True)
        d_pre = (d_field + d_sum * gate_grid[..., level_index : level_index + 1]) * slopes[
            level_index
        ]
        tap_rows[level_index] = depthwise_taps(fields[level_index], d_pre, width)
        d_field = depthwise(d_pre, level_taps(kernel_block, level_index)[::-1], width)
    d_gates = jnp.concatenate(gate_cols, axis=-1).reshape(gates.shape)
    return (d_field.reshape(d_summed.shape), d_gates, jnp.concatenate(tap_rows, axis=0))


class Shares:
    def __init__(self, local_rows, chan_size):
        self.count = max(1, IMAGE_ROWS // local_rows)
        self.groups = [
            list(range(first, first + self.count)) for first in range(0, chan_size, self.count)
        ]

    def to_images(self, values):
        if self.count == 1:
            return values
        return lax.all_to_all(
            values, "chan", 1, 0, axis_index_groups=self.groups, tiled=True
        )

    def to_rows(self, values):
        if self.count == 1:
            return values
        return lax.all_to_all(
            values, "chan", 0, 1, axis_index_groups=self.groups, tiled=True
        )

    def all_rows(self, values):
        if self.count == 1:
            return values
        return lax.all_gather(
            values, "chan", axis=0, axis_index_groups=self.groups, tiled=True
        )

    def sum_rows(self, values):
        if self.count == 1:
            return values
        return lax.psum_scatter(
            values, "chan", scatter_dimension=0, axis_index_groups=self.groups, tiled=True
        )

    def channels(self, values):
        if self.count == 1:
            return values
        size = values.shape[1] // self.count
        place = lax.axis_index("chan") % self.count
        return lax.dynamic_slice_in_dim(values, place * size, size, 1)

    def spread(self, values):
        if self.count == 1:
            return values
        size = values.shape[1]
        place = lax.axis_index("chan") % self.count
        whole = jnp.zeros((values.shape[0], size * self.count), values.dtype)
        return lax.dynamic_update_slice_in_dim(whole, values, place * size, 1)


def pack(parts, block_index):
    focal, mixer, mlp = parts
    return (
        jnp.concatenate(
            [
                focal[block_index, :, 0].T,
                focal[block_index, :, 1].T,
                mixer[block_index, 0].T,
                mixer[block_index, 1].T,
            ],
            axis=0,
        ),
        jnp.concatenate([mlp[block_index, 0].T, mlp[block_index, 1].T], axis=0),
    )


def gather_weights(packed, counts):
    size = lax.axis_size("chan")
    gathered = lax.all_gather(packed, "chan", axis=0, tiled=False)
    pieces = []
    start = 0
    for count in counts:
        pieces.append(
            gathered[:, start : start + count].reshape(size * count, packed.shape[-1])
        )
        start += count
    return pieces


def scatter_grads(grads):
    size = lax.axis_size("chan")
    stacked = jnp.concatenate(
        [grad.astype(jnp.bfloat16).reshape(size, -1, grad.shape[-1]) for grad in grads], axis=1
    )
    mine = lax.psum_scatter(stacked, "chan", scatter_dimension=0, tiled=False)
    return lax.psum(mine, "dp").astype(jnp.float32)


def nesterov(weight, moment, gradient, rate):
    new_moment = MOMENTUM * moment + gradient
    new_weight = weight - rate * (gradient + MOMENTUM * new_moment)
    return (new_weight, new_moment)


def block_forward(residual, vecs, focal_pieces, mlp_pieces, kernel_block, keep, validity, shares):
    query_w, key_w, mix_w, proj_w = focal_pieces
    up_w, down_w = mlp_pieces
    unit_one, scale_one = normalize(residual)
    first = (unit_one * vecs[0] + vecs[1]).astype(jnp.bfloat16)
    query = times_transposed(first, query_w)
    context = times_transposed(first, key_w)
    gates = times_transposed(first, vecs[6:10].astype(jnp.bfloat16))
    gates = shares.all_rows(gates)
    context_low, levels = focal_forward(
        shares.to_images(context), gates, shares.channels(kernel_block), validity
    )
    context_low = shares.to_rows(context_low)
    modulator = times_transposed(context_low, mix_w)
    product = (query * modulator).astype(jnp.bfloat16)
    middle = residual + keep[:, 0:1] * (matmul(product, proj_w) + vecs[4])
    unit_two, scale_two = normalize(middle)
    second = (unit_two * vecs[2] + vecs[3]).astype(jnp.bfloat16)
    hidden, slope = gelu_pair(times_transposed(second, up_w))
    hidden = hidden.astype(jnp.bfloat16)
    output = middle + keep[:, 1:2] * (matmul(hidden, down_w) + vecs[5])
    saved = (
        (unit_one, scale_one, first, query, gates),
        (context_low, levels, modulator, product),
        (unit_two, scale_two, second, hidden, slope),
    )
    return (output, saved)


def mlp_backward(d_residual, saved, vecs, mlp_pieces, keep):
    unit_two, scale_two, second, hidden, slope = saved
    up_w, down_w = mlp_pieces
    d_down = d_residual * keep[:, 1:2]
    d_low = d_down.astype(jnp.bfloat16)
    grad_down = contract_rows(hidden, d_low)
    d_pre = (times_transposed(d_low, down_w) * slope).astype(jnp.bfloat16)
    grad_up = contract_rows(d_pre, second)
    d_middle, grad_gain, grad_shift = norm_backward(
        matmul(d_pre, up_w), unit_two, scale_two, vecs[2]
    )
    bias = jnp.sum(d_down, axis=0, keepdims=True)
    return (d_middle + d_residual, (grad_up, grad_down), (grad_gain, grad_shift, bias))


def focal_block_backward(
    d_middle, saved_one, saved_two, vecs, focal_pieces, kernel_block, keep, validity, shares
):
    unit_one, scale_one, first, query, gates = saved_one
    context_low, levels, modulator, product = saved_two
    query_w, key_w, mix_w, proj_w = focal_pieces
    d_proj = d_middle * keep[:, 0:1]
    d_low = d_proj.astype(jnp.bfloat16)
    grad_proj = contract_rows(product, d_low)
    d_product = times_transposed(d_low, proj_w)
    d_query = (d_product * modulator).astype(jnp.bfloat16)
    d_modulator = (d_product * query).astype(jnp.bfloat16)
    grad_mix = contract_rows(d_modulator, context_low)
    d_context_sum = shares.to_images(matmul(d_modulator, mix_w))
    d_context, d_gates, grad_kernel = focal_backward(
        d_context_sum, gates, shares.channels(kernel_block), validity, levels
    )
    d_context = shares.to_rows(d_context.astype(jnp.bfloat16))
    d_gates = shares.sum_rows(d_gates)
    grad_kernel = shares.spread(grad_kernel)
    gate_high, gate_rest = split_low(d_gates)
    gate_low = vecs[6:10].astype(jnp.bfloat16)
    grad_gate = contract_rows(gate_high, first) + contract_rows(gate_rest, first)
    grad_query = contract_rows(d_query, first)
    grad_key = contract_rows(d_context, first)
    d_first = (
        matmul(d_query, query_w)
        + matmul(d_context, key_w)
        + matmul(gate_high, gate_low)
        + matmul(gate_rest, gate_low)
    )
    d_input, grad_gain, grad_shift = norm_backward(d_first, unit_one, scale_one, vecs[0])
    bias = jnp.sum(d_proj, axis=0, keepdims=True)
    return (
        d_input + d_middle,
        (grad_query, grad_key, grad_mix, grad_proj),
        grad_kernel,
        (grad_gain, grad_shift, bias, grad_gate),
    )


def shards(
    patches,
    valid_mask,
    target_mask,
    keep_mask,
    embed_weight,
    embed_moment,
    head_weight,
    head_moment,
    vectors,
    vector_moment,
    vector_average,
    focal_input,
    focal_moment,
    focal_average,
    mixers,
    mixer_moment,
    mixer_average,
    mlp_weights,
    mlp_moment,
    mlp_average,
    kernels,
    kernel_moment,
    kernel_average,
):
    local_rows = patches.shape[0]
    group_rows = valid_mask.shape[0]
    chan_size = lax.axis_size("chan")
    own = focal_input.shape[-1]
    own_hidden = mlp_weights.shape[-1]
    shares = Shares(local_rows, chan_size)
    outer = 10 * BLOCKS
    first_row = lax.axis_index("chan") * local_rows
    image_row = first_row // IMAGE_ROWS * IMAGE_ROWS
    image_rows = max(local_rows, IMAGE_ROWS)
    validity = valid_mask.astype(jnp.float32)
    valid_images = lax.dynamic_slice_in_dim(validity, image_row, image_rows)[:, None]
    valid_local = lax.dynamic_slice_in_dim(validity, first_row, local_rows)[:, None]
    masked_local = lax.dynamic_slice_in_dim(target_mask, first_row, local_rows).astype(jnp.float32)[
        :, None
    ]
    loss_weight = masked_local * valid_local
    group_count = jnp.sum(validity * target_mask.astype(jnp.float32))
    counted = lax.psum(group_count, "dp")
    denominator = counted * PATCH_IN
    keep_rows = jnp.repeat(keep_mask.astype(jnp.float32) / KEEP_RATE, IMAGE_ROWS, axis=0)
    keep_local = lax.dynamic_slice_in_dim(keep_rows, first_row, local_rows)

    low = tuple(part.astype(jnp.bfloat16) for part in (focal_input, mixers, mlp_weights))
    focal_pieces = []
    mlp_pieces = []
    for block_index in range(BLOCKS):
        focal_rows, mlp_rows = pack(low, block_index)
        focal_pieces.append(gather_weights(focal_rows, [own] * 4))
        mlp_pieces.append(gather_weights(mlp_rows, [own_hidden] * 2))
    kernels_full = lax.all_gather(kernels, "chan", axis=2, tiled=True)

    embed_low = embed_weight.astype(jnp.bfloat16)
    embed_full = matmul(patches, embed_low) + vectors[outer]
    embed_unit, embed_scale = normalize(embed_full)
    start_state = embed_unit * vectors[outer + 1] + vectors[outer + 2]
    residual = start_state * (1.0 - masked_local) + vectors[outer + 5] * masked_local
    saved_blocks = []
    for block_index in range(BLOCKS):
        residual, saved = block_forward(
            residual,
            vectors[10 * block_index : 10 * block_index + 10],
            focal_pieces[block_index],
            mlp_pieces[block_index],
            kernels_full[block_index],
            keep_local[:, block_index],
            valid_images,
            shares,
        )
        saved_blocks.append(saved)
    final_unit, final_scale = normalize(residual)
    final_low = (final_unit * vectors[outer + 3] + vectors[outer + 4]).astype(jnp.bfloat16)
    head_low = head_weight.astype(jnp.bfloat16)
    error = matmul(final_low, head_low) - patches.astype(jnp.float32)
    loss_part = jnp.sum(loss_weight * error * error) / denominator
    d_prediction = (2.0 * loss_weight * error / denominator).astype(jnp.bfloat16)
    grad_head = contract_rows(final_low, d_prediction)
    d_final = times_transposed(d_prediction, head_low)
    d_residual, grad_final_gain, grad_final_shift = norm_backward(
        d_final, final_unit, final_scale, vectors[outer + 3]
    )
    vector_parts = [None] * BLOCKS
    focal_grads = [None] * BLOCKS
    mlp_grads = [None] * BLOCKS
    kernel_parts = [None] * BLOCKS
    for block_index in reversed(range(BLOCKS)):
        vecs = vectors[10 * block_index : 10 * block_index + 10]
        keep = keep_local[:, block_index]
        saved_one, saved_two, saved_three = saved_blocks[block_index]
        d_middle, grads, (gain_two, shift_two, mlp_bias) = mlp_backward(
            d_residual, saved_three, vecs, mlp_pieces[block_index], keep
        )
        mlp_grads[block_index] = scatter_grads(grads)
        d_residual, grads, kernel_parts[block_index], (gain_one, shift_one, proj_bias, gate) = (
            focal_block_backward(
                d_middle,
                saved_one,
                saved_two,
                vecs,
                focal_pieces[block_index],
                kernels_full[block_index],
                keep,
                valid_images,
                shares,
            )
        )
        focal_grads[block_index] = scatter_grads(grads)
        vector_parts[block_index] = jnp.concatenate(
            [gain_one, shift_one, gain_two, shift_two, proj_bias, mlp_bias, gate], axis=0
        )
    d_start = d_residual * (1.0 - masked_local)
    grad_token = jnp.sum(d_residual * masked_local, axis=0, keepdims=True)
    d_embed, grad_embed_gain, grad_embed_shift = norm_backward(
        d_start, embed_unit, embed_scale, vectors[outer + 1]
    )
    grad_embed = contract_rows(patches, d_embed.astype(jnp.bfloat16))
    grad_vectors = jnp.concatenate(
        vector_parts
        + [
            jnp.sum(d_embed, axis=0, keepdims=True),
            grad_embed_gain,
            grad_embed_shift,
            grad_final_gain,
            grad_final_shift,
            grad_token,
        ],
        axis=0,
    )
    both = ("dp", "chan")
    grad_embed = lax.psum(grad_embed.astype(jnp.bfloat16), both).astype(jnp.float32)
    grad_head = lax.psum(grad_head.astype(jnp.bfloat16), both).astype(jnp.float32)
    grad_vectors, grad_kernel, loss = lax.psum(
        (grad_vectors, jnp.stack(kernel_parts), loss_part), both
    )
    grad_kernel = lax.dynamic_slice_in_dim(
        grad_kernel, lax.axis_index("chan") * own, own, 2
    )
    focal_stack = jnp.stack(focal_grads).reshape(BLOCKS, 4, own, -1)
    grad_focal = jnp.transpose(focal_stack[:, :2], (0, 3, 1, 2))
    grad_mixer = jnp.transpose(focal_stack[:, 2:], (0, 1, 3, 2))
    grad_mlp = jnp.transpose(
        jnp.stack(mlp_grads).reshape(BLOCKS, 2, own_hidden, -1), (0, 1, 3, 2)
    )
    rate = 0.2 * math.sqrt(group_rows * lax.axis_size("dp"))
    new_embed, new_embed_moment = nesterov(embed_weight, embed_moment, grad_embed, rate)
    new_head, new_head_moment = nesterov(head_weight, head_moment, grad_head, rate)
    results = []
    for weight, moment, average, gradient in (
        (vectors, vector_moment, vector_average, grad_vectors),
        (focal_input, focal_moment, focal_average, grad_focal),
        (mixers, mixer_moment, mixer_average, grad_mixer),
        (mlp_weights, mlp_moment, mlp_average, grad_mlp),
        (kernels, kernel_moment, kernel_average, grad_kernel),
    ):
        new_weight, new_moment = nesterov(weight, moment, gradient, rate)
        results.extend(
            (new_weight, new_moment, AVERAGE * average + (1.0 - AVERAGE) * new_weight)
        )
    return (loss, new_embed, new_embed_moment, new_head, new_head_moment, *results)


def solution(mesh):
    split = P(None, None, None, "chan")
    taps = P(None, None, "chan")
    return jax.shard_map(
        shards,
        mesh=mesh,
        in_specs=(P(("dp", "chan"), None), P("dp"), P("dp"), P("dp", None, None))
        + (P(),) * 7
        + (split,) * 9
        + (taps,) * 3,
        out_specs=(P(),) * 8 + (split,) * 9 + (taps,) * 3,
        check_vma=False,
    )
```

time: 1630 us -> 1020 us (0.63)
  waiting for transfers between devices: 1060 us -> 578 us
  other arithmetic: 289 us -> 86.4 us
  local copies, waits for them, and re-layouts: 66.8 us -> 201 us
  matrix products: 89.7 us -> 40.8 us
    all_gather x10 -> x4, waiting for transfers between devices: 403 us -> 86.3 us  [gather_weights(): gathered = lax.all_gather(packed, 'chan', axis=0, tiled=False)]
    reduce_scatter x10 -> x4, waiting for transfers between devices: 534 us -> 279 us  [scatter_grads(): mine = lax.psum_scatter(stacked, 'chan', scatter_dimension=0, tiled=False)]
    another operation x6 -> x166, local copies, waits for them, and re-layouts: 2.92 us -> 115 us  [depthwise_taps(): return jnp.stack(rows)]
    psum x2 -> x3, waiting for transfers between devices: 119 us -> 213 us  [the longest x1 137 us: shards(): lax.psum(grad_embed.astype(jnp.bfloat16), both).astype(jnp.float32)]
    reduce_sum x47 -> x29, other arithmetic: 129 us -> 45.3 us  [the longest x12 28 us: depthwise_taps(): rows.append(jnp.sum(window * grad, axis=(0, 1, 2)))]
    mul x19 -> x8, other arithmetic: 78.6 us -> 12.2 us  [the longest x6 10.9 us: gelu_pair(): return (values * cumulative, cumulative + values * density)]
    add_any x14 -> x0, other arithmetic: 47.7 us -> none  [the longest x6 45.2 us: depthwise(): padded[:, kernel_row:kernel_row + GRID, kernel_col:kernel_col + GRID, :]]
    psum x3 -> x2, blocking collectives: 91.1 us -> 46.6 us  [the longest x1 40 us: shards(): lax.psum((grad_vectors, jnp.stack(kernel_parts), loss_part), both)]
  transfers between devices with their start and end apart: 22 -> 11, of which waited for: 22 -> 10; matrix products, arithmetic and copies ran while one was open for 6% -> 11% of each run, Pallas kernels for 0% -> 0%
where the time goes in v1:
time: 1020 us; the launch traced here: 1010 us
  waiting for transfers between devices  578 us (57%)
  local copies, waits for them, and re-layouts  201 us (20%)
  other arithmetic  86.4 us (8%)
  blocking collectives  79.8 us (8%)
  matrix products  40.8 us (4%)
  between operations  20.1 us (2%)
    reduce_scatter x4, waiting for transfers between devices, scatter_grads(): mine = lax.psum_scatter(stacked, 'chan', scatter_dimension=0, tiled=False)  279 us
    psum x1, waiting for transfers between devices, shards(): lax.psum(grad_embed.astype(jnp.bfloat16), both).astype(jnp.float32)  137 us
    another operation x166, local copies, waits for them, and re-layouts, depthwise_taps(): return jnp.stack(rows)  115 us
    all_gather x4, waiting for transfers between devices, gather_weights(): gathered = lax.all_gather(packed, 'chan', axis=0, tiled=False)  86.3 us
    psum x1, waiting for transfers between devices, shards(): lax.psum((grad_vectors, jnp.stack(kernel_parts), loss_part), both)  49 us
    psum x1, blocking collectives, shards(): lax.psum((grad_vectors, jnp.stack(kernel_parts), loss_part), both)  40 us
    all_gather x1, blocking collectives, shards(): kernels_full = lax.all_gather(kernels, 'chan', axis=2, tiled=True)  33.1 us
    reduce_sum x12, other arithmetic, depthwise_taps(): rows.append(jnp.sum(window * grad, axis=(0, 1, 2)))  28 us
  transfers between devices with their start and end apart: 11, of which 10 were waited for; matrix products, arithmetic and copies ran while one was open for 11% of the time, Pallas kernels for 0%

profile of v1, /device:TPU:0, one launch (start us, length us, event | category | flops | bytes accessed | tf_op | source)
XLA Modules:
  0.0 1006.5 jit_solution(10225679307886474186)
XLA Ops:
  12.7 33.1 %all_gather.29 = f32[2,83,384]{1,2,0:T(8,128)S(1)} all-gather(f32[2,83,48]{1,2,0:T(8,128)S(1)} %copy-done.93), channel_id=1, replica_groups=mesh['dp'=4,'chan'=8] {'chan'}, dimensions={2}, use_global_device_ids=true | all-gather | bytes 286848 | tf_op jit(solution)/shard_map/all_gather | solution.py:383
  60.5 3.1 slice_reduce_fusion.36
  70.3 6.6 psum.70
  88.9 4.5 multiply_reduce_fusion.194
  100.2 51.5 %all-gather.11.cloned.1.call-done = bf16[3072,384]{1,0:T(8,128)(2,1)} async-done(((bf16[384,384]{1,0:T(8,128)(2,1)}), bf16[3072,384]{1,0:T(8,128)(2,1)}) %all-gather.11.cloned.1.call-update) | async-done | bytes 2359312 | tf_op jit(solution)/shard_map/all_gather | solution.py:217
  164.0 4.6 multiply_reduce_fusion.191
  171.0 33.9 %all-gather.15.cloned.1.call-done = bf16[3072,384]{1,0:T(8,128)(2,1)} async-done(((bf16[384,384]{1,0:T(8,128)(2,1)}), bf16[3072,384]{1,0:T(8,128)(2,1)}) %all-gather.15.cloned.1.call-update) | async-done | bytes 2359312 | tf_op jit(solution)/shard_map/all_gather | solution.py:217
  231.7 6.4 multiply_reduce_fusion.49
  239.2 3.2 multiply_reduce_fusion.74
  264.6 5.8 multiply_reduce_fusion.132
  271.0 3.5 multiply_reduce_fusion.157
  390.8 6.7 concatenate.81
  397.5 14.6 %concatenate.80 = f32[83,384]{1,0:T(8,128)} concatenate(f32[1,384]{1,0:T(1,128)} %stack.534, f32[1,384]{1,0:T(1,128)} %stack.535, f32[1,384]{1,0:T(1,128)} %stack.536, f32[1,384]{1,0:T(1,128)} %stack.537, f32[1,384]{1,0:T(1,128)} %stack.538, f32[1,384]{1,0:T(1,128)} %stack.539, f32[1,384]{1,0:T(1,128)} %stack.540, f32[1,384]{1,0:T(1,128)} %stack.541, f32[1,384]{1,0:T(1,128)} %stack.542, ...), dimensions={0} | concatenate | bytes 254976 | tf_op jit(solution)/shard_map/concatenate | solution.py:145
  447.8 40.0 %all-reduce.12 = (f32[]{:T(128)}, f32[26,384]{1,0:T(8,128)S(1)}) all-reduce(f32[]{:T(128)S(6)} %div.167, f32[26,384]{1,0:T(8,128)S(1)} %concatenate.75), channel_id=1, replica_groups=mesh['dp'=4,'chan'=8] {'dp','chan'}, use_global_device_ids=true, to_apply=%region_18.19 | all-reduce | flops 9985 | bytes 79880 | tf_op jit(solution)/shard_map/psum | solution.py:464
  488.5 49.0 %all-reduce.19.cloned.1.call-done = f32[2,83,384]{2,1,0:T(8,128)} async-done(((f32[2,83,384]{2,1,0:T(8,128)}), f32[2,83,384]{2,1,0:T(8,128)}) %all-reduce.19.cloned.1.call-update) | async-done | bytes 254992 | tf_op jit(solution)/shard_map/psum | solution.py:464
  540.6 66.6 %reduce-scatter.7.cloned.1.call-done = bf16[1,192,384]{2,1,0:T(8,128)(2,1)} async-done(((bf16[8,192,384]{2,1,0:T(8,128)(2,1)}), bf16[1,192,384]{2,1,0:T(8,128)(2,1)}) %reduce-scatter.7.cloned.1.call-update) | async-done | bytes 147472 | tf_op jit(solution)/shard_map/reduce_scatter | solution.py:233
  607.2 67.6 %reduce-scatter.5.cloned.1.call-done = bf16[1,192,384]{2,1,0:T(8,128)(2,1)} async-done(((bf16[8,192,384]{2,1,0:T(8,128)(2,1)}), bf16[1,192,384]{2,1,0:T(8,128)(2,1)}) %reduce-scatter.5.cloned.1.call-update) | async-done | bytes 147472 | tf_op jit(solution)/shard_map/reduce_scatter | solution.py:233
  674.8 72.3 %reduce-scatter.11.cloned.1.call-done = bf16[1,384,384]{2,1,0:T(8,128)(2,1)} async-done(((bf16[8,384,384]{2,1,0:T(8,128)(2,1)}), bf16[1,384,384]{2,1,0:T(8,128)(2,1)}) %reduce-scatter.11.cloned.1.call-update) | async-done | bytes 294928 | tf_op jit(solution)/shard_map/reduce_scatter | solution.py:233
  747.1 72.2 %reduce-scatter.9.cloned.1.call-done = bf16[1,384,384]{2,1,0:T(8,128)(2,1)} async-done(((bf16[8,384,384]{2,1,0:T(8,128)(2,1)}), bf16[1,384,384]{2,1,0:T(8,128)(2,1)}) %reduce-scatter.9.cloned.1.call-update) | async-done | bytes 294928 | tf_op jit(solution)/shard_map/reduce_scatter | solution.py:233
  819.3 137.3 %all-reduce.21.cloned.1.call-done = (bf16[768,384]{0,1:T(8,128)(2,1)}, bf16[384,768]{1,0:T(8,128)(2,1)}) async-done(((bf16[768,384]{0,1:T(8,128)(2,1)}, bf16[384,768]{1,0:T(8,128)(2,1)}), (bf16[768,384]{0,1:T(8,128)(2,1)}, bf16[384,768]{1,0:T(8,128)(2,1)})) %all-reduce.21.cloned.1.call-update) | async-done | bytes 1179664 | tf_op jit(solution)/shard_map/psum | solution.py:462
  956.6 2.7 convert_add_fusion.3
  959.4 2.7 copy.53
  963.9 3.0 fusion.22
  967.0 26.7 %all-reduce.23.cloned.1.call-done = (bf16[1,4,48,384]{3,2,1,0:T(8,128)(2,1)}, bf16[1,4,48,384]{3,2,1,0:T(8,128)(2,1)}, bf16[1,2,192,384]{3,2,1,0:T(8,128)(2,1)}, bf16[1,2,192,384]{3,2,1,0:T(8,128)(2,1)}) async-done(((bf16[1,4,48,384]{3,2,1,0:T(8,128)(2,1)}, bf16[1,4,48,384]{3,2,1,0:T(8,128)(2,1)}, bf16[1,2,192,384]{3,2,1,0:T(8,128)(2,1)}, bf16[1,2,192,384]{3,2,1,0:T(8,128)(2,1)}), ...) | async-done | bytes 884752 | tf_op jit(solution)/shard_map/psum | solution.py:234
  (1094 shorter events, 268.8 us)
Async XLA Ops:
  7.2 75.4 %all-gather.9.cloned.1.call-start = ((), (), s32[]{:S(2)}) async-start(), calls=%async_computation.9 | async-start | bytes 1327104 | tf_op jit(solution)/shard_map/all_gather | solution.py:217
  10.1 88.0 %all-gather.13.cloned.1.call-start = ((), (), s32[]{:S(2)}) async-start(), calls=%async_computation.11 | async-start | bytes 1327104 | tf_op jit(solution)/shard_map/all_gather | solution.py:217
  10.8 140.8 %all-gather.11.cloned.1.call-start = ((), (), s32[]{:S(2)}) async-start(), calls=%async_computation.10 | async-start | bytes 2654208 | tf_op jit(solution)/shard_map/all_gather | solution.py:217
  11.8 193.1 %all-gather.15.cloned.1.call-start = ((), (), s32[]{:S(2)}) async-start(), calls=%async_computation.12 | async-start | bytes 2654208 | tf_op jit(solution)/shard_map/all_gather | solution.py:217
  12.6 524.9 %all-reduce.19.cloned.1.call-start = ((), (), s32[]{:S(2)}) async-start(), calls=%async_computation.8 | async-start | bytes 540672 | tf_op jit(solution)/shard_map/psum | solution.py:464
  70.2 83.3 %copy-start.121 = (f32[384]{0:T(512)}, f32[384]{0:T(512)S(1)}, u32[]{:S(2)}) copy-start(f32[384]{0:T(512)S(1)} %get-tuple-element.436) | copy-start | bytes 4612
  70.2 87.3 %copy-start.112 = (f32[384]{0:T(512)}, f32[384]{0:T(512)S(1)}, u32[]{:S(2)}) copy-start(f32[384]{0:T(512)S(1)} %get-tuple-element.433) | copy-start | bytes 4612
  70.3 87.5 %copy-start.95 = (bf16[26,384]{1,0:T(8,128)(2,1)}, bf16[26,384]{1,0:T(8,128)(2,1)S(1)}, u32[]{:S(2)}) copy-start(bf16[26,384]{1,0:T(8,128)(2,1)S(1)} %convert.11) | copy-start | bytes 59908
  260.2 157.6 %copy-start.49 = (bf16[256,384]{1,0:T(8,128)(2,1)}, bf16[256,384]{1,0:T(8,128)(2,1)S(1)}, u32[]{:S(2)}) copy-start(bf16[256,384]{1,0:T(8,128)(2,1)S(1)} %get-tuple-element.533) | copy-start | bytes 589828
  274.8 65.9 %copy-start.308 = (f32[384]{0:T(512)S(1)}, f32[384]{0:T(512)}, u32[]{:S(2)}) copy-start(f32[384]{0:T(512)} %get-tuple-element.157) | copy-start | bytes 4612
  274.8 66.5 %copy-start.307 = (f32[384]{0:T(512)S(1)}, f32[384]{0:T(512)}, u32[]{:S(2)}) copy-start(f32[384]{0:T(512)} %get-tuple-element.156) | copy-start | bytes 4612
  274.9 67.0 %copy-start.306 = (f32[384]{0:T(512)S(1)}, f32[384]{0:T(512)}, u32[]{:S(2)}) copy-start(f32[384]{0:T(512)} %get-tuple-element.155) | copy-start | bytes 4612
  274.9 67.6 %copy-start.305 = (f32[384]{0:T(512)S(1)}, f32[384]{0:T(512)}, u32[]{:S(2)}) copy-start(f32[384]{0:T(512)} %get-tuple-element.154) | copy-start | bytes 4612
  276.1 137.7 %copy-start.72 = (bf16[384,384]{1,0:T(8,128)(2,1)S(1)}, bf16[384,384]{1,0:T(8,128)(2,1)}, u32[]{:S(2)}) copy-start(bf16[384,384]{1,0:T(8,128)(2,1)} %convolution_convert_fusion.6) | copy-start | bytes 884740
  276.1 137.7 %copy-start.73 = (bf16[384,384]{1,0:T(8,128)(2,1)S(1)}, bf16[384,384]{1,0:T(8,128)(2,1)}, u32[]{:S(2)}) copy-start(bf16[384,384]{1,0:T(8,128)(2,1)} %convolution_convert_fusion.9) | copy-start | bytes 884740
  413.8 193.5 %reduce-scatter.7.cloned.1.call-start = ((), (), s32[]{:S(2)}) async-start(), calls=%async_computation.5 | async-start | bytes 1327104 | tf_op jit(solution)/shard_map/reduce_scatter | solution.py:233
  416.1 258.8 %reduce-scatter.5.cloned.1.call-start = ((), (), s32[]{:S(2)}) async-start(), calls=%async_computation.4 | async-start | bytes 1327104 | tf_op jit(solution)/shard_map/reduce_scatter | solution.py:233
  419.8 327.3 %reduce-scatter.11.cloned.1.call-start = ((), (), s32[]{:S(2)}) async-start(), calls=%async_computation.7 | async-start | bytes 2654208 | tf_op jit(solution)/shard_map/reduce_scatter | solution.py:233
  424.6 394.7 %reduce-scatter.9.cloned.1.call-start = ((), (), s32[]{:S(2)}) async-start(), calls=%async_computation.6 | async-start | bytes 2654208 | tf_op jit(solution)/shard_map/reduce_scatter | solution.py:233
  430.1 526.6 %all-reduce.21.cloned.1.call-start = ((), (), s32[]{:S(2)}) async-start(), calls=%async_computation.13 | async-start | bytes 2359296 | tf_op jit(solution)/shard_map/psum | solution.py:462
  447.4 90.1 %copy-start.83 = (f32[2,83,48]{2,1,0:T(8,128)S(1)}, f32[2,83,48]{2,1,0:T(8,128)}, u32[]{:S(2)}) copy-start(f32[2,83,48]{2,1,0:T(8,128)} %copy.52) | copy-start | bytes 95620
  447.4 90.1 %copy-start.84 = (f32[2,83,48]{2,1,0:T(8,128)S(1)}, f32[2,83,48]{2,1,0:T(8,128)}, u32[]{:S(2)}) copy-start(f32[2,83,48]{2,1,0:T(8,128)} %copy.50) | copy-start | bytes 95620
  447.4 546.2 %all-reduce.23.cloned.1.call-start = ((), (), s32[]{:S(2)}) async-start(), calls=%async_computation.14 | async-start | bytes 1769472 | tf_op jit(solution)/shard_map/psum | solution.py:234
  447.8 508.8 %copy-start.20 = (f32[768,384]{0,1:T(8,128)S(1)}, f32[768,384]{0,1:T(8,128)}, u32[]{:S(2)}) copy-start(f32[768,384]{0,1:T(8,128)} %copy.49) | copy-start | bytes 3538948
  (342 other events, 4046.0 us)
Sparse Core Ops, SparseCore 0:
  10.8 44.5 all-gather.8
  58.1 39.8 all-gather.12
  100.8 50.8 all-gather.10
  154.3 50.6 all-gather.14
  413.9 123.5 all-reduce.18
  541.7 65.5 reduce-scatter.6
  611.6 63.1 reduce-scatter.4
  678.7 68.3 reduce-scatter.10
  751.0 68.2 reduce-scatter.8
  826.2 130.3 all-reduce.20
  959.2 34.3 all-reduce.22

commit v2 on v1

v2 whole, which is shorter than its diff:
```python
import math

import jax
import jax.numpy as jnp
from jax import lax
from jax.experimental import pallas as pl
from jax.experimental.pallas import tpu as pltpu
from jax.sharding import PartitionSpec as P

PATCH_IN = 768
GRID = 16
BLOCKS = 2
IMAGE_ROWS = GRID * GRID
LANES = 128

EPS = 1e-05
MOMENTUM = 0.9
AVERAGE = 0.5
KEEP_RATE = 0.8
KERNEL_SIZES = (3, 5, 7)
KERNEL_STARTS = (0, 9, 34)
ROOT_HALF = math.sqrt(0.5)
DENSITY = 1.0 / math.sqrt(2.0 * math.pi)
VMEM_LIMIT = 24 << 20
F32 = jnp.float32
BF16 = jnp.bfloat16


def matmul(left, right):
    return jnp.dot(left, right, preferred_element_type=F32)


def contract_rows(left, right):
    return lax.dot_general(left, right, (((0,), (0,)), ((), ())), preferred_element_type=F32)


def times_transposed(left, right):
    return lax.dot_general(left, right, (((1,), (1,)), ((), ())), preferred_element_type=F32)


def normalize(values):
    average = jnp.mean(values, axis=-1, keepdims=True)
    centred = values - average
    variance = jnp.mean(centred * centred, axis=-1, keepdims=True)
    scale = lax.rsqrt(variance + EPS)
    return (centred * scale, scale)


def norm_backward(grad, unit, scale, gain):
    d_unit = grad * gain
    mean_one = jnp.mean(d_unit, axis=-1, keepdims=True)
    mean_two = jnp.mean(d_unit * unit, axis=-1, keepdims=True)
    return (d_unit - mean_one - unit * mean_two) * scale


def column_sum(values):
    return jnp.sum(values, axis=0, keepdims=True)


def gelu_pair(values):
    cumulative = 0.5 + 0.5 * lax.erf(values * ROOT_HALF)
    density = DENSITY * jnp.exp(-0.5 * values * values)
    return (values * cumulative, cumulative + values * density)


def nesterov(weight, moment, gradient, rate):
    new_moment = MOMENTUM * moment + gradient
    new_weight = weight - rate * (gradient + MOMENTUM * new_moment)
    return (new_weight, new_moment)


def after(value, *others):
    return lax.optimization_barrier((value, others))[0]


class Links:
    def __init__(self):
        chan = lax.axis_size("chan")
        self.ny = 1 << ((chan.bit_length() - 1) // 2)
        self.nz = chan // self.ny
        self.nc = 2
        self.nx = lax.axis_size("dp") // self.nc
        self.chan = chan
        self.place = lax.axis_index("chan")
        self.z = self.place // self.ny
        self.y = self.place % self.ny
        group = lax.axis_index("dp")
        self.x = group // self.nc
        self.core = group % self.nc
        self.sizes = {"z": self.nz, "y": self.ny, "x": self.nx}

    def bits(self, axis):
        return [1 << k for k in reversed(range((self.sizes[axis] - 1).bit_length()))]

    def swap(self, values, axis, step):
        if axis in ("z", "y"):
            step = step * self.ny if axis == "z" else step
            return lax.ppermute(values, "chan", [(i, i ^ step) for i in range(self.chan)])
        step = step * self.nc if axis == "x" else step
        return lax.ppermute(values, "dp", [(i, i ^ step) for i in range(self.nx * self.nc)])

    def swap_core(self, values):
        return self.swap(values, "core", 1)

    def cross_x(self, values):
        total = values
        for step in self.bits("x"):
            low = total.astype(values.dtype)
            total = low.astype(F32) + self.swap(low, "x", step).astype(F32)
        return total.astype(F32)

    def mask_of(self, axis, step):
        return tuple(step if name == axis else 0 for name in ("z", "y", "x"))

    def here(self):
        return jnp.stack([self.core, self.place, self.x]).astype(jnp.int32)

    def slots(self, masks, split_x):
        places = []
        for mask_z, mask_y, mask_x in masks:
            place = (self.z ^ mask_z) * self.ny + (self.y ^ mask_y)
            places.append(place * self.nx + (self.x ^ mask_x) if split_x else place)
        return jnp.stack([self.core, self.place] + places).astype(jnp.int32)

    def open_sum(self, kept, received, parts=1):
        chan, rows, width = kept.shape
        bits = [2] * ((chan * parts).bit_length() - 1)
        return [term.reshape(*bits, rows // parts, width) for term in (kept, received)]

    def exchange(self, terms, axis, level):
        dims = terms[0].ndim - 2
        at = len(self.bits("z")) - 1 - level if axis == "z" else dims - 1
        index = self.index_on(axis) >> level & 1

        def pick(term, which):
            return lax.dynamic_index_in_dim(term, which, at, keepdims=False)

        sent = total([pick(term, 1 - index) for term in terms])

        def finish(received):
            return [pick(term, index) for term in terms] + [received]

        return ((sent, axis, 1 << level), finish)

    def index_on(self, axis):
        return self.y if axis == "y" else self.z if axis == "z" else self.x

    def early(self, terms, axis):
        levels = len(self.bits(axis))
        for level in range(levels - 1):
            move, finish = self.exchange(terms, axis, level)
            terms = finish(self.swap(*move))
        return self.exchange(terms, axis, levels - 1)

    def regather_x(self, rows):
        *steps, last = reversed(self.bits("x"))
        for step in steps:
            rows = self.beside_x(rows, self.swap(rows, "x", step), step)
        return ((rows, "x", last), lambda received: self.beside_x(rows, received, last))

    def beside_x(self, rows, received, step):
        first = jnp.concatenate([rows, received])
        second = jnp.concatenate([received, rows])
        return jnp.where(self.x & step == 0, first, second)

    def both_halves(self, summed):
        other = self.swap_core(summed)
        first = self.core == 0
        return (jnp.where(first, summed, other), jnp.where(first, other, summed))


def join(left, right):
    return tuple(a ^ b for a, b in zip(left, right))


def total(terms):
    result = terms[0].astype(F32)
    for term in terms[1:]:
        result = result + term.astype(F32)
    return result.astype(BF16)


class Gather:
    def __init__(self, links, own):
        self.links = links
        self.stack = own[None]
        self.masks = [(0, 0, 0)]
        self.parts = None

    def moves(self, axis, step):
        return [(self.stack, axis, step)]

    def take(self, received, axis, step, keep_apart=False):
        if keep_apart:
            self.parts = [self.stack, received]
        else:
            self.stack = jnp.concatenate([self.stack, received], axis=0)
        extra = self.links.mask_of(axis, step)
        self.masks = self.masks + [join(mask, extra) for mask in self.masks]

    def early(self, axis):
        *steps, last = self.links.bits(axis)
        for step in steps:
            self.take(self.links.swap(self.stack, axis, step), axis, step)
        return (axis, last)

    def direct(self):
        return [(self.stack, "z", step) for step in range(1, self.links.nz)]

    def take_direct(self, received):
        self.stack = jnp.concatenate([self.stack] + received, axis=0)
        self.masks = [self.links.mask_of("z", step) for step in range(self.links.nz)]


class Pieces:
    def __init__(self, where, near, far, matrices):
        self.where = where
        self.near = near
        self.far = far
        self.matrices = matrices
        self.slots = where.shape[0] - 2
        self.width = near[0].shape[-1]

    def rows(self, name):
        return self.matrices[name][2] * self.slots

    def arrays(self):
        return [*self.near, *self.far]

    def copies(self, name, where, parts, target, sems):
        half, first, count = self.matrices[name]
        near, far = parts[: len(self.near)], parts[len(self.near) :]
        pairs = []
        slot = 0
        for near_part, far_part in zip(near, far):
            for d in range(near_part.shape[0]):
                at = pl.multiple_of(where[2 + slot] * count, 8)
                room = target.at[pl.ds(at, count), :]
                rows = pl.ds(first, count)
                pairs.append(
                    (
                        pltpu.make_async_copy(near_part.at[d, rows, :], room, sems.at[slot]),
                        pltpu.make_async_copy(far_part.at[d, rows, :], room, sems.at[slot]),
                    )
                )
                slot += 1
        mine = where[0] == half

        def start():
            @pl.when(mine)
            def _():
                for pair in pairs:
                    pair[0].start()

            @pl.when(jnp.logical_not(mine))
            def _():
                for pair in pairs:
                    pair[1].start()

        def wait():
            for pair in pairs:
                pair[0].wait()

        return (start, wait)


class Room:
    def __init__(self):
        self.refs = {}
        self.waits = {}
        self.flushes = []
        self.pending = []

    def __getitem__(self, key):
        wait = self.waits.pop(key, None)
        if wait is not None:
            wait()
        return self.refs[key]

    def __getattr__(self, key):
        return self[key]

    def flush(self, *refs):
        rest = []
        for ref, copy in self.flushes:
            if any(ref is one for one in refs):
                copy.start()
                self.pending.append(copy)
            else:
                rest.append((ref, copy))
        self.flushes = rest

    def finish(self):
        self.flush(*[ref for ref, _copy in self.flushes])
        for copy in self.pending:
            copy.wait()


class Box(dict):
    __getattr__ = dict.__getitem__


class View:
    def __init__(self, room, names):
        self.room = room
        self.names = names

    def __getattr__(self, key):
        return self.room[self.names.get(key, key)]

    def flush(self, *refs):
        self.room.flush(*refs)


def renamed(stage, **names):
    def call(room):
        stage(View(room, names))

    call.__name__ = stage.__name__
    return call


HOLD, FETCH, SCALAR = range(3)


def run_kernel(stages, inputs, outputs, temps=(), weights=(), pinned=True):
    temps = dict(temps)
    operands, in_specs, scratch, plan = [], [], [], []

    def scratch_for(shape):
        scratch.append(shape)
        return len(scratch) - 1

    for key, (array, mode) in inputs.items():
        operands.append(array)
        if mode == HOLD:
            in_specs.append(pl.BlockSpec(memory_space=pltpu.VMEM))
            plan.append((key, mode, None))
        elif mode == SCALAR:
            in_specs.append(pl.BlockSpec(memory_space=pltpu.SMEM))
            plan.append((key, mode, None))
        else:
            operands[-1] = pltpu.with_memory_space_constraint(array, pltpu.HBM)
            in_specs.append(pl.BlockSpec(memory_space=pltpu.HBM))
            place = scratch_for(pltpu.VMEM(array.shape, array.dtype))
            plan.append((key, mode, (place, scratch_for(pltpu.SemaphoreType.DMA))))
    loads = []
    for pieces, names in weights:
        first = len(operands)
        operands.append(pieces.where)
        in_specs.append(pl.BlockSpec(memory_space=pltpu.SMEM))
        for array in pieces.arrays():
            if pinned:
                array = pltpu.with_memory_space_constraint(array, pltpu.HBM)
            operands.append(array)
            in_specs.append(pl.BlockSpec(memory_space=pltpu.HBM if pinned else pl.ANY))
        for matrix in names:
            place = scratch_for(pltpu.VMEM((pieces.rows(matrix), pieces.width), BF16))
            sems = scratch_for(pltpu.SemaphoreType.DMA((pieces.slots,)))
            loads.append((matrix, pieces, first, place, sems))
    out_specs, out_shapes, out_plan = [], [], []
    for key, (shape, dtype, mode) in outputs.items():
        if mode == HOLD:
            out_specs.append(pl.BlockSpec(memory_space=pltpu.VMEM))
            out_shapes.append(jax.ShapeDtypeStruct(shape, dtype))
            out_plan.append((key, None))
        else:
            out_specs.append(pl.BlockSpec(memory_space=pltpu.HBM))
            out_shapes.append(pltpu.HBM(shape, dtype))
            place = scratch_for(pltpu.VMEM(shape, dtype))
            out_plan.append((key, (place, scratch_for(pltpu.SemaphoreType.DMA))))
    temp_plan = [(key, scratch_for(shape)) for key, shape in temps.items()]

    def body(*refs):
        ins = refs[: len(operands)]
        outs = refs[len(operands) : len(operands) + len(out_specs)]
        rooms = refs[len(operands) + len(out_specs) :]
        room = Room()
        for ref, (key, mode, more) in zip(ins, plan):
            if mode == FETCH:
                place, sem = more
                copy = pltpu.make_async_copy(ref, rooms[place], rooms[sem])
                copy.start()
                room.refs[key] = rooms[place]
                room.waits[key] = copy.wait
            else:
                room.refs[key] = ref
        for matrix, pieces, first, place, sems in loads:
            where = ins[first]
            parts = ins[first + 1 : first + 1 + len(pieces.arrays())]
            start, wait = pieces.copies(matrix, where, parts, rooms[place], rooms[sems])
            start()
            room.refs[matrix] = rooms[place]
            room.waits[matrix] = wait
            room.refs.update(where=where)
        for ref, (key, more) in zip(outs, out_plan):
            if more is None:
                room.refs[key] = ref
            else:
                place, sem = more
                room.refs[key] = rooms[place]
                copy = pltpu.make_async_copy(rooms[place], ref, rooms[sem])
                room.flushes.append((rooms[place], copy))
        for key, place in temp_plan:
            room.refs[key] = rooms[place]
        for stage in stages:
            stage(room)
        for key in list(room.waits):
            room[key]
        room.finish()

    results = pl.pallas_call(
        body,
        name=stages[-1].__name__,
        in_specs=in_specs,
        out_specs=out_specs,
        out_shape=out_shapes,
        scratch_shapes=scratch,
        compiler_params=pltpu.CompilerParams(vmem_limit_bytes=VMEM_LIMIT),
    )(*operands)
    return Box(zip(outputs, results))


MASKED, COUNTED, VALID, KEEP = 0, 1, 2, 3


def column(room, index):
    return room.columns[:, index : index + 1]


def keep_of(room, block, branch):
    return column(room, KEEP + 2 * block + branch)


def vector(room, row):
    return room.vectors[row : row + 1, :]


def low_gates(room, block):
    return room.vectors[10 * block + 6 : 10 * block + 10, :].astype(BF16)


def correlate(padded, taps, level, flip):
    width = KERNEL_SIZES[level]
    first = KERNEL_STARTS[level]
    margin = width // 2
    lanes = padded.shape[-1]
    sums = [None] * GRID
    for dx in range(width):
        weights = []
        for dy in range(width):
            tap = dy * width + dx
            if flip:
                tap = width * width - 1 - tap
            weights.append(jnp.broadcast_to(taps[first + tap : first + tap + 1, :], (GRID, lanes)))
        for row in range(GRID):
            window = padded[row, 8 - margin + dx : 8 - margin + dx + GRID, :]
            for dy in range(width):
                out = row - dy + margin
                if 0 <= out < GRID:
                    term = window * weights[dy]
                    sums[out] = term if sums[out] is None else sums[out] + term
    return sums


def correlate_taps(padded, grads, d_taps, at_lanes, level):
    width = KERNEL_SIZES[level]
    first = KERNEL_STARTS[level]
    margin = width // 2
    for dx in range(width):
        sums = [None] * width
        for row in range(GRID):
            window = padded[row, 8 - margin + dx : 8 - margin + dx + GRID, :]
            for dy in range(width):
                out = row - dy + margin
                if 0 <= out < GRID:
                    term = window * grads[out]
                    sums[dy] = term if sums[dy] is None else sums[dy] + term
        for dy in range(width):
            tap = first + dy * width + dx
            d_taps[tap : tap + 1, at_lanes] = column_sum(sums[dy])


def clear_margins(padded):
    lanes = padded.shape[-1]
    for row in range(GRID):
        padded[row, 0:8, :] = jnp.zeros((8, lanes), F32)
        padded[row, 8 + GRID : 16 + GRID, :] = jnp.zeros((8, lanes), F32)


def rows_at(row):
    return slice(row * GRID, (row + 1) * GRID)


def gate_part(gates, row, level, lanes):
    part = gates[rows_at(row), level * LANES : (level + 1) * LANES]
    return part if lanes == LANES else part[:, 0:1]


def lane_range(group, groups, lanes):
    if groups == 1:
        return slice(0, lanes)
    return pl.ds(pl.multiple_of(group * lanes, lanes), lanes)


def tap_room(tap_count):
    return -(-tap_count // 8) * 8


def split_three(values):
    high = values.astype(BF16)
    rest = values - high.astype(F32)
    middle = rest.astype(BF16)
    return (high, middle, (rest - middle.astype(F32)).astype(BF16))


def pack_rows(here, sources, taps, parts):
    width = sources[0][0].shape[3]
    counts = [array.shape[2] // parts for array, _block in sources]
    rows = sum(counts) + (0 if taps is None else taps.shape[1])

    def body(here_ref, *refs):
        wide_refs = refs[: len(sources)]
        rest = refs[len(sources) :]
        out_ref = rest[0] if taps is None else rest[1]
        buffers = rest[-1 - len(sources) : -1]
        sems = rest[-1]
        copies = []
        for at, (ref, (_array, block)) in enumerate(zip(wide_refs, sources)):
            source = ref.at[block, here_ref[0]]
            if parts > 1:
                first = pl.multiple_of(here_ref[2] * counts[at], 8)
                source = source.at[pl.ds(first, counts[at]), :]
            copies.append(pltpu.make_async_copy(source, buffers[at], sems.at[at]))
            copies[-1].start()
        row = sum(counts)
        if taps is not None:
            own, count = taps.shape[1:]
            out_ref[row : row + own, :] = jnp.zeros((own, width), BF16)
            splits = [split_three(rest[0][b]) for b in range(BLOCKS)]
            wide = (splits[0][0], splits[1][0], splits[0][1])
            thin = (splits[1][1], splits[0][2], splits[1][2])
            for chosen, at_core in ((wide, 0), (thin, 1)):

                @pl.when(here_ref[0] == at_core)
                def _():
                    for index, part in enumerate(chosen):
                        at = index * LANES
                        out_ref[row : row + own, at : at + count] = part

        row = 0
        for copy, buffer, count in zip(copies, buffers, counts):
            copy.wait()
            out_ref[row : row + count, :] = buffer[...].astype(BF16)
            row += count

    extra = [] if taps is None else [taps]
    return pl.pallas_call(
        body,
        name=pack_rows.__name__,
        in_specs=[pl.BlockSpec(memory_space=pltpu.SMEM)]
        + [pl.BlockSpec(memory_space=pltpu.HBM) for _ in sources]
        + [pl.BlockSpec(memory_space=pltpu.VMEM) for _ in extra],
        out_specs=pl.BlockSpec(memory_space=pltpu.VMEM),
        out_shape=jax.ShapeDtypeStruct((rows, width), BF16),
        scratch_shapes=[pltpu.VMEM((count, width), F32) for count in counts]
        + [pltpu.SemaphoreType.DMA((len(sources),))],
        compiler_params=pltpu.CompilerParams(vmem_limit_bytes=VMEM_LIMIT),
    )(
        here,
        *[pltpu.with_memory_space_constraint(array, pltpu.HBM) for array, _block in sources],
        *extra,
    )


def taps_stage(tap_count, groups, lanes):
    room_rows = tap_room(tap_count)
    used = BLOCKS * room_rows

    def join_taps(room):
        wide = room.wide[...]
        thin = room.thin[...]
        shape = (used, wide.shape[1])
        row = lax.broadcasted_iota(jnp.int32, shape, 0)
        lane = lax.broadcasted_iota(jnp.int32, shape, 1)
        upper = row >= room_rows
        tap = jnp.where(upper, row - room_rows, row)
        tap = jnp.where(tap < tap_count, tap, -8 * LANES)

        def chosen(lower_places, upper_places):
            marks = jnp.zeros(shape, F32)
            for places, side in ((lower_places, False), (upper_places, True)):
                for place in places:
                    hit = jnp.logical_and(lane == tap + place * LANES, upper == side)
                    marks = jnp.where(hit, 1.0, marks)
            return marks.astype(BF16)

        taps = times_transposed(chosen((0, 2), (1,)), wide)
        taps = taps + times_transposed(chosen((1,), (0, 2)), thin)
        for b in range(BLOCKS):
            for j in range(groups):
                room.taps[b, j] = taps[
                    b * room_rows : (b + 1) * room_rows, j * lanes : (j + 1) * lanes
                ]

    return join_taps


def inputs_stage(block, groups, lanes):
    def focal_inputs(room):
        unit, _scale = normalize(room.x[...])
        first = unit * vector(room, 10 * block) + vector(room, 10 * block + 1)
        first = first.astype(BF16)
        width = first.shape[1]
        gate_low = low_gates(room, block)
        for level in range(4):
            spread = jnp.broadcast_to(gate_low[level : level + 1], (LANES, width))
            room.gates[:, level * LANES : (level + 1) * LANES] = times_transposed(
                first, spread
            )
        key = room.key
        for j in range(groups):
            room.context[j] = times_transposed(first, key[j * lanes : (j + 1) * lanes, :])
        room.query_out[...] = times_transposed(first, room.query[...])
        room.flush(room.gates, room.context, room.query_out)

    return focal_inputs


def focal_stage(block, groups, lanes):
    def focal_levels(room):
        padded = room.padded
        taps, context, gates, low, pool = room.taps, room.context, room.gates, room.low, room.pool
        fields = [room.k1, room.k2, room.k3]
        slopes = [room.s1, room.s2, room.s3]
        clear_margins(padded)
        valid = room.image_columns[:, VALID : VALID + 1]
        valid_total = column_sum(valid)

        def group(j, carry):
            tap = taps.at[block, j]
            for row in range(GRID):
                padded[row, 8 : 8 + GRID, :] = context[j, rows_at(row), :]
            for level in range(3):
                sums = correlate(padded, tap, level, False)
                for row in range(GRID):
                    value, slope = gelu_pair(sums[row])
                    fields[level][j, rows_at(row), :] = value
                    slopes[level][j, rows_at(row), :] = slope
                    if level < 2:
                        padded[row, 8 : 8 + GRID, :] = value
            mean = column_sum(fields[2][j] * valid) / valid_total
            pooled, pooled_slope = gelu_pair(mean)
            pool[j, 0:1, :] = pooled
            pool[j, 1:2, :] = pooled_slope / valid_total
            pool[j, 2:8, :] = jnp.zeros((6, lanes), F32)
            at = lane_range(j, groups, lanes)
            for row in range(GRID):
                summed = pooled * gate_part(gates, row, 3, lanes)
                for level in range(3):
                    summed = summed + fields[level][j, rows_at(row), :] * gate_part(
                        gates, row, level, lanes
                    )
                low[rows_at(row), at] = summed.astype(BF16)
            return carry

        if groups > 1:
            lax.fori_loop(0, groups, group, 0)
        else:
            group(0, 0)
        room.flush(room.k1, room.k2, room.k3, room.s1, room.s2, room.s3, room.pool, room.low)

    return focal_levels


def mix_stage(block):
    def mix_forward(room):
        modulator = times_transposed(room.low[...], room.mix[...])
        room.mod[...] = modulator
        room.flush(room.mod)
        product = (room.query_out[...] * modulator).astype(BF16)
        branch = matmul(product, room.proj[...]) + vector(room, 10 * block + 4)
        room.middle[...] = room.x[...] + keep_of(room, block, 0) * branch

    return mix_forward


def mlp_stage(block):
    def mlp_forward(room):
        middle = room.middle[...]
        unit, _scale = normalize(middle)
        second = unit * vector(room, 10 * block + 2) + vector(room, 10 * block + 3)
        second = second.astype(BF16)
        up = room.up
        step = up.shape[0] // 4
        for part in range(4):
            at = slice(part * step, (part + 1) * step)
            value, slope = gelu_pair(times_transposed(second, up[at, :]))
            room.hidden[:, at] = value.astype(BF16)
            room.slope[:, at] = slope
        room.flush(room.hidden, room.slope)
        lowered = matmul(room.hidden[...], room.down[...]) + vector(room, 10 * block + 5)
        room.out[...] = middle + keep_of(room, block, 1) * lowered

    return mlp_forward


def embed_stage(room):
    outer = 10 * BLOCKS
    embedded = matmul(room.patches[...], room.embed[...].astype(BF16))
    embedded = embedded + vector(room, outer)
    room.embedded[...] = embedded
    room.flush(room.embedded)
    unit, _scale = normalize(embedded)
    mask = column(room, MASKED)
    state = unit * vector(room, outer + 1) + vector(room, outer + 2)
    room.x[...] = state * (1.0 - mask) + vector(room, outer + 5) * mask


def store_halves(core, kept, sent, at, first, second):
    chan, _rows, width = kept.shape
    rows = first.shape[0] // chan
    first = first.reshape(chan, rows, width).astype(BF16)
    second = second.reshape(chan, rows, width).astype(BF16)

    @pl.when(core == 0)
    def _():
        kept[:, at : at + rows, :] = first
        sent[:, at : at + rows, :] = second

    @pl.when(core != 0)
    def _():
        kept[:, at : at + rows, :] = second
        sent[:, at : at + rows, :] = first


def head_stage(room):
    outer = 10 * BLOCKS
    gain = vector(room, outer + 3)
    unit, scale = normalize(room.x[...])
    low = (unit * gain + vector(room, outer + 4)).astype(BF16)
    head_low = room.head[...].astype(BF16)
    error = matmul(low, head_low) - room.patches[...].astype(F32)
    denom = room.denom[0, 0]
    weighted = column(room, COUNTED) * error
    loss = column_sum(jnp.sum(weighted * error, axis=-1, keepdims=True)) / denom
    d_pred = (2.0 * weighted / denom).astype(BF16)
    grad = contract_rows(low, d_pred)
    half = grad.shape[1] // 2
    core = room.where[0]
    store_halves(core, room.kept, room.sent, 0, grad[:, :half], grad[:, half:])
    room.flush(room.kept, room.sent)
    d_final = times_transposed(d_pred, head_low)
    room.d_out[...] = norm_backward(d_final, unit, scale, gain)
    sums = room.sums
    width = low.shape[1]
    sums[0:1, :] = column_sum(d_final * unit)
    sums[1:2, :] = column_sum(d_final)
    sums[2:3, :] = jnp.broadcast_to(loss, (1, width))
    sums[3:8, :] = jnp.zeros((5, width), F32)


def mlp_back_stage(block):
    def mlp_backward(room):
        d_residual = room.d_in[...]
        d_down = d_residual * keep_of(room, block, 1)
        d_low = d_down.astype(BF16)
        unit, scale = normalize(room.middle[...])
        gain = vector(room, 10 * block + 2)
        second = (unit * gain + vector(room, 10 * block + 3)).astype(BF16)
        grad_down = contract_rows(room.hidden[...], d_low)
        d_pre = (times_transposed(d_low, room.down[...]) * room.slope[...]).astype(BF16)
        grad_up = contract_rows(d_pre, second)
        core = room.where[0]
        store_halves(core, room.kept, room.sent, 0, grad_up, grad_down)
        room.flush(room.sent, room.kept)
        d_second = matmul(d_pre, room.up[...])
        room.d_out[...] = d_residual + norm_backward(d_second, unit, scale, gain)
        sums = room.sums
        width = d_low.shape[1]
        sums[0:1, :] = column_sum(d_second * unit)
        sums[1:2, :] = column_sum(d_second)
        sums[2:3, :] = column_sum(d_down)
        sums[3:8, :] = jnp.zeros((5, width), F32)

    return mlp_backward


def mix_back_stage(block, groups, lanes):
    def mix_backward(room):
        d_proj = room.d_in[...] * keep_of(room, block, 0)
        d_low = d_proj.astype(BF16)
        d_product = times_transposed(d_low, room.proj[...])
        modulator = room.mod[...]
        query = room.query_out[...]
        d_mod = (d_product * query).astype(BF16)
        mix = room.mix
        for j in range(groups):
            room.d_sum[j] = matmul(d_mod, mix[:, j * lanes : (j + 1) * lanes])
        room.d_query[...] = (d_product * modulator).astype(BF16)
        product = (query * modulator).astype(BF16)
        grad_proj = contract_rows(product, d_low)
        grad_mix = contract_rows(d_mod, room.low[...])
        core = room.where[0]
        store_halves(core, room.kept, room.sent, 0, grad_mix, grad_proj)
        sums = room.sums
        width = d_low.shape[1]
        sums[0:1, :] = column_sum(d_proj)
        sums[1:8, :] = jnp.zeros((7, width), F32)

    return mix_backward


def focal_back_stage(block, groups, lanes):
    def levels_backward(room):
        padded = room.padded
        d_padded = room.d_padded
        clear_margins(padded)
        clear_margins(d_padded)
        d_all, gates, taps, pool = room.d_sum, room.gates, room.taps, room.pool
        fields = [room.context, room.k1, room.k2, room.k3]
        slopes = [room.s1, room.s2, room.s3]
        d_context, d_gates, d_taps = room.d_context, room.d_gates, room.d_taps
        valid = room.image_columns[:, VALID : VALID + 1]
        d_gates[...] = jnp.zeros(d_gates.shape, F32)
        d_taps[...] = jnp.zeros(d_taps.shape, F32)

        def fold(values):
            if lanes == LANES:
                return values
            summed = jnp.sum(values, axis=-1, keepdims=True) / LANES
            return jnp.broadcast_to(summed, (values.shape[0], LANES))

        def group(j, carry):
            tap = taps.at[block, j]
            at = lane_range(j, groups, lanes)
            d_pooled = jnp.zeros((1, lanes), F32)
            for row in range(GRID):
                d_pooled = d_pooled + column_sum(
                    d_all[j, rows_at(row), :] * gate_part(gates, row, 3, lanes)
                )
            d_mean = d_pooled * pool[j, 1:2, :]
            d_field = [d_mean * valid[rows_at(row)] for row in range(GRID)]
            for level in (2, 1, 0):
                d_pre = []
                for row in range(GRID):
                    here = rows_at(row)
                    grad = d_field[row] + d_all[j, here, :] * gate_part(gates, row, level, lanes)
                    grad = grad * slopes[level][j, here, :]
                    d_pre.append(grad)
                    d_padded[row, 8 : 8 + GRID, :] = grad
                    padded[row, 8 : 8 + GRID, :] = fields[level][j, here, :]
                correlate_taps(padded, d_pre, d_taps, at, level)
                d_field = correlate(d_padded, tap, level, True)
            for row in range(GRID):
                d_context[rows_at(row), at] = d_field[row].astype(BF16)
            whole = d_all[j]
            for level in range(3):
                here = slice(level * LANES, (level + 1) * LANES)
                d_gates[:, here] = d_gates[:, here] + fold(whole * fields[level + 1][j])
            here = slice(3 * LANES, 4 * LANES)
            d_gates[:, here] = d_gates[:, here] + fold(whole * pool[j, 0:1, :])
            return carry

        if groups > 1:
            lax.fori_loop(0, groups, group, 0)
        else:
            group(0, 0)
        room.flush(room.d_taps)

    return levels_backward


def inputs_back_stage(block):
    def inputs_backward(room):
        unit, scale = normalize(room.x[...])
        gain = vector(room, 10 * block)
        first_wide = (unit * gain + vector(room, 10 * block + 1)).astype(BF16)
        first = first_wide
        first_wide = first.astype(F32)
        rows, width = first.shape
        gate_low = low_gates(room, block).astype(F32)
        sums = room.input_sums
        sums[...] = jnp.zeros((8, width), F32)
        d_first = jnp.zeros((rows, width), F32)
        d_gates = room.d_gates
        for level in range(4):
            here = slice(level * LANES, (level + 1) * LANES)
            col = jnp.sum(d_gates[:, here], axis=-1, keepdims=True)
            d_first = d_first + col * gate_low[level : level + 1]
            sums[2 + level : 3 + level, :] = column_sum(col * first_wide)
        d_query = room.d_query[...]
        d_context = room.d_context[...]
        d_first = d_first + matmul(d_query, room.query[...])
        d_first = d_first + matmul(d_context, room.key[...])
        room.d_out[...] = room.d_in[...] + norm_backward(d_first, unit, scale, gain)
        sums[0:1, :] = column_sum(d_first * unit)
        sums[1:2, :] = column_sum(d_first)
        grad_query = contract_rows(d_query, first)
        grad_key = contract_rows(d_context, first)
        kept, sent = room.kept, room.sent
        core = room.where[0]
        store_halves(core, kept, sent, 0, grad_query, grad_key)
        at = width // kept.shape[0]
        kept[:, at : 2 * at, :] = room.more_kept[...]
        sent[:, at : 2 * at, :] = room.more_sent[...]

    return inputs_backward


def sums_start(tap_count):
    return BLOCKS * tap_room(tap_count)


def small_rows_for(tap_count, chan):
    used = sums_start(tap_count) + 8 * (2 + 3 * BLOCKS)
    return -(-used // (16 * chan)) * (16 * chan)


def embed_back_stage(tap_count, sum_keys, tap_keys, first_row):
    outer = 10 * BLOCKS

    def embed_backward(room):
        mask = column(room, MASKED)
        d_residual = room.d_out[...]
        d_start = d_residual * (1.0 - mask)
        unit, scale = normalize(room.embedded[...])
        d_embed = norm_backward(d_start, unit, scale, vector(room, outer + 1))
        small = room.small
        small[...] = jnp.zeros(small.shape, F32)
        for b, key in enumerate(tap_keys):
            at = b * tap_room(tap_count)
            taps = room.d_taps if key is None else room[key]
            small[at : at + taps.shape[0], :] = taps[...]
        at = sums_start(tap_count)
        small[at : at + 1, :] = column_sum(d_embed)
        small[at + 1 : at + 2, :] = column_sum(d_start * unit)
        small[at + 2 : at + 3, :] = column_sum(d_start)
        small[at + 3 : at + 4, :] = column_sum(d_residual * mask)
        for key in sum_keys:
            at += 8
            sums = room.input_sums if key is None else room[key]
            small[at : at + 8, :] = sums[...]
        grad = contract_rows(room.patches[...], d_embed.astype(BF16))
        core = room.where[0]
        kept, sent = room.kept, room.sent
        half = grad.shape[0] // 2
        row = first_row
        store_halves(core, kept, sent, row, grad[:half], grad[half:])
        row += half // kept.shape[0]
        half = small.shape[0] // 2
        store_halves(core, kept, sent, row, small[:half], small[half:])

    return embed_backward


def update_head_stage(rate):
    def update_head(room):
        half = room.weight.shape[1] // 2
        for index in range(2):
            here = slice(index * half, (index + 1) * half)
            new_weight, new_moment = nesterov(
                room.weight[:, here],
                room.moment[:, here],
                (room.head0, room.head1)[index][...].astype(F32),
                rate,
            )
            room.new_weight[:, here] = new_weight
            room.new_moment[:, here] = new_moment

    return update_head


def update_shared_stage(tap_count, own, rate):
    def update_shared(room):
        half = room.embed0.shape[0]
        for index in range(2):
            here = slice(index * half, (index + 1) * half)
            gradient = (room.embed0, room.embed1)[index][...].astype(F32)
            new_weight, new_moment = nesterov(
                room.weight[here, :], room.moment[here, :], gradient, rate
            )
            room.new_weight[here, :] = new_weight
            room.new_moment[here, :] = new_moment
        room.flush(room.new_weight, room.new_moment)
        small = jnp.concatenate([room.small0[...], room.small1[...]], axis=0)
        grads = small.astype(F32)
        width = small.shape[1]

        def sum_row(index, row):
            at = sums_start(tap_count) + 8 * index + row
            return grads[at : at + 1]

        rows = []
        for b in range(BLOCKS):
            inputs_at, mlp_at, mix_at = 1 + 3 * b, 2 + 3 * b, 3 + 3 * b
            rows += [sum_row(inputs_at, 0), sum_row(inputs_at, 1)]
            rows += [sum_row(mlp_at, 0), sum_row(mlp_at, 1)]
            rows += [sum_row(mix_at, 0), sum_row(mlp_at, 2)]
            rows += [sum_row(inputs_at, 2 + level) for level in range(4)]
        head_at = 1 + 3 * BLOCKS
        rows += [sum_row(0, 0), sum_row(0, 1), sum_row(0, 2)]
        rows += [sum_row(head_at, 0), sum_row(head_at, 1), sum_row(0, 3)]
        packed = room.packed
        for at, row in enumerate(rows):
            packed[at : at + 1, :] = row
        gradient = packed[0 : len(rows), :]
        new_weight, new_moment = nesterov(
            room.vectors[...], room.vector_moment[...], gradient, rate
        )
        room.new_vectors[...] = new_weight
        room.new_vector_moment[...] = new_moment
        room.new_vector_average[...] = (
            AVERAGE * room.vector_average[...] + (1.0 - AVERAGE) * new_weight
        )
        room.loss[...] = sum_row(head_at, 2)[:, 0:LANES]
        first = room.where[1] * own
        source = lax.broadcasted_iota(jnp.int32, (own, width), 1)
        wanted = first + lax.broadcasted_iota(jnp.int32, (own, width), 0)
        chosen = (source == wanted).astype(F32).astype(BF16)
        for b in range(BLOCKS):
            at = b * tap_room(tap_count)
            gradient = times_transposed(chosen, small[at : at + tap_room(tap_count)])
            gradient = gradient[:, :tap_count]
            new_weight, new_moment = nesterov(
                room.kernels[b], room.kernel_moment[b], gradient, rate
            )
            room.new_kernels[b] = new_weight
            room.new_kernel_moment[b] = new_moment
            room.new_kernel_average[b] = (
                AVERAGE * room.kernel_average[b] + (1.0 - AVERAGE) * new_weight
            )

    return update_shared


class Shares:
    def __init__(self, local_rows, chan_size):
        self.count = max(1, IMAGE_ROWS // local_rows)
        self.groups = [
            list(range(first, first + self.count)) for first in range(0, chan_size, self.count)
        ]

    def to_images(self, values):
        whole = lax.all_to_all(
            values[0], "chan", 1, 0, axis_index_groups=self.groups, tiled=True
        )
        return whole[None]

    def to_rows(self, values):
        return lax.all_to_all(values, "chan", 0, 1, axis_index_groups=self.groups, tiled=True)

    def all_rows(self, values):
        return lax.all_gather(
            values, "chan", axis=0, axis_index_groups=self.groups, tiled=True
        )

    def sum_rows(self, values):
        return lax.psum_scatter(
            values, "chan", scatter_dimension=0, axis_index_groups=self.groups, tiled=True
        )

    def channels(self, values):
        size = values.shape[-1] // self.count
        place = lax.axis_index("chan") % self.count
        return lax.dynamic_slice_in_dim(values, place * size, size, values.ndim - 1)

    def spread(self, values):
        size = values.shape[1]
        place = lax.axis_index("chan") % self.count
        whole = jnp.zeros((values.shape[0], size * self.count), values.dtype)
        return lax.dynamic_update_slice_in_dim(whole, values, place * size, 1)


def hold(array):
    return (array, HOLD)


def fetch(array):
    return (array, FETCH)


def fetch_all(made, names):
    return {name: fetch(made[name]) for name in names}


def shards(
    patches,
    valid_mask,
    target_mask,
    keep_mask,
    embed_weight,
    embed_moment,
    head_weight,
    head_moment,
    vectors,
    vector_moment,
    vector_average,
    focal_input,
    focal_moment,
    focal_average,
    mixers,
    mixer_moment,
    mixer_average,
    mlp_weights,
    mlp_moment,
    mlp_average,
    kernels,
    kernel_moment,
    kernel_average,
):
    links = Links()
    rows, patch_in = patches.shape
    group_rows = valid_mask.shape[0]
    own = focal_input.shape[-1]
    own_hidden = mlp_weights.shape[-1]
    hidden_width = own_hidden * links.chan
    tap_count = kernels.shape[1]
    width = vectors.shape[1]
    shares = Shares(rows, links.chan)
    shared = shares.count > 1
    channels = width // shares.count
    lanes = LANES if channels % LANES == 0 else channels
    groups = channels // lanes
    room_rows = tap_room(tap_count)
    split_x = own_hidden % (8 * links.nx) == 0 and links.nx > 1

    def together(values, moves):
        got = [links.swap(*move) for move in moves]
        return lax.optimization_barrier((values, got))

    def beside(call, gate, moves):
        made = call(after(gate, *[move[0] for move in moves]))
        made, got = together(dict(made), moves)
        return (Box(made), got)

    here = links.here()
    focal_rows = jnp.transpose(focal_input, (0, 2, 3, 1))
    mixer_rows = jnp.transpose(mixers, (0, 1, 3, 2))
    mlp_rows = jnp.transpose(mlp_weights, (0, 1, 3, 2))
    kernel_rows = jnp.transpose(kernels, (0, 2, 1))
    focal_layout = dict(
        query=(0, 0, own), mix=(0, own, own), key=(1, 0, own), proj=(1, own, own)
    )
    first_layout = dict(focal_layout, wide=(0, 2 * own, own), thin=(1, 2 * own, own))

    def mlp_layout(count):
        return dict(up=(0, 0, count), down=(1, 0, count))

    first_row = links.place * rows
    validity = valid_mask.astype(F32)
    masked = target_mask.astype(F32)
    keep_rows = jnp.repeat(
        keep_mask.reshape(keep_mask.shape[0], -1).astype(F32) / KEEP_RATE, IMAGE_ROWS, axis=0
    )
    table = jnp.concatenate(
        [
            masked[:, None],
            (masked * validity)[:, None],
            validity[:, None],
            keep_rows,
            jnp.zeros((group_rows, 1), F32),
        ],
        axis=1,
    )
    columns = lax.dynamic_slice_in_dim(table, first_row, rows)
    image_columns = columns
    if shared:
        image_columns = lax.dynamic_slice_in_dim(
            table, first_row // IMAGE_ROWS * IMAGE_ROWS, IMAGE_ROWS
        )
    group_count = jnp.broadcast_to(jnp.sum(validity * masked), (8, LANES))
    basic = dict(vectors=fetch(vectors), columns=fetch(columns))
    grid_columns = dict(image_columns=fetch(image_columns))

    whole = (rows, width)
    focal = [None] * BLOCKS
    mlp = [None] * BLOCKS
    focal[0] = Gather(
        links, pack_rows(here, [(focal_rows, 0), (mixer_rows, 0)], kernel_rows, 1)
    )
    moves = focal[0].direct()
    embedded = run_kernel(
        [embed_stage],
        dict(patches=fetch(patches), embed=fetch(embed_weight), **basic),
        dict(x=(whole, F32, HOLD), embedded=(whole, F32, FETCH)),
    )
    parts_x = links.nx if split_x else 1
    packed = pack_rows(here, [(mlp_rows, 0)], None, parts_x)
    (x, packed), got = together((embedded.x, packed), moves)
    focal[0].take_direct(got)
    mlp[0] = Gather(links, packed)
    z_first, *z_rest = links.bits("z")
    y_move = focal[0].early("y")
    (move,) = mlp[0].moves("z", z_first)
    packed = (
        pack_rows(here, [(focal_rows, 1), (mixer_rows, 1)], None, 1),
        pack_rows(here, [(mlp_rows, 1)], None, 1),
    )
    packed, got = together(packed, [move])
    mlp[0].take(got[0], "z", z_first)
    focal[1] = Gather(links, packed[0])
    mlp[1] = Gather(links, packed[1])

    def take_z(gather, received):
        for step, one in zip(z_rest, received):
            gather.take(one, "z", step)

    moves = [(mlp[0].stack, "z", step) for step in z_rest]
    moves += [(focal[0].stack, *y_move), (focal[1].stack, "z", z_first)]
    moves += [(group_count, "core", 1)]
    x, got = together(x, moves)
    take_z(mlp[0], got[:-3])
    focal[0].take(got[-3], *y_move, True)
    focal[1].take(got[-2], "z", z_first)
    group_count = group_count + got[-1]

    def twins(gather, values):
        values, got = together(values, [(part, "core", 1) for part in gather.parts])
        return (values, got)

    def pieces_of(gather, far, layout, split):
        return Pieces(links.slots(gather.masks, split), gather.parts, far, layout)

    y_move = mlp[0].early("y")
    x, far = twins(focal[0], after(x, mlp[0].stack, group_count))
    focal_pieces = [pieces_of(focal[0], far, first_layout, False), None]
    mlp_pieces = [None, None]

    field_shape = (groups, IMAGE_ROWS, lanes)
    field = (field_shape, F32, FETCH)
    padded = pltpu.VMEM((GRID, GRID + 16, lanes), F32)
    gates_out = dict(gates=((IMAGE_ROWS, 4 * LANES), F32, FETCH))
    focal_out = dict(k1=field, k2=field, k3=field, s1=field, s2=field, s3=field)
    focal_out.update(pool=((groups, 8, lanes), F32, FETCH))
    mixed_out = dict(mod=(whole, F32, FETCH), middle=(whole, F32, HOLD))
    query_out = dict(query_out=(whole, F32, FETCH))
    low_out = dict(low=(whole, BF16, FETCH))
    mlp_out = dict(
        hidden=((rows, hidden_width), BF16, FETCH), slope=((rows, hidden_width), F32, FETCH)
    )
    weights_in = dict(key=0, query=0, mix=0, proj=0)
    up_down = dict(up=0, down=0)
    taps_shape = (BLOCKS, groups, room_rows, lanes)

    def focal_apart(b, x, taps):
        pieces = focal_pieces[b]
        made = run_kernel(
            [inputs_stage(b, 1, width)],
            dict(x=hold(x), **basic),
            dict(
                gates=((rows, 4 * LANES), F32, FETCH),
                context=((1, rows, width), F32, FETCH),
                **query_out,
            ),
            {},
            [(pieces, dict(key=0, query=0))],
        )
        made.update(gates=shares.all_rows(made.gates), context=shares.to_images(made.context))
        made.update(
            run_kernel(
                [focal_stage(b, groups, lanes)],
                dict(
                    context=fetch(made.context),
                    gates=fetch(made.gates),
                    taps=fetch(taps),
                    **grid_columns,
                ),
                dict(low=((IMAGE_ROWS, channels), BF16, FETCH), **focal_out),
                dict(padded=padded),
            )
        )
        made.update(low=shares.to_rows(made.low))
        made.update(
            run_kernel(
                [mix_stage(b)],
                dict(
                    x=hold(x), low=fetch(made.low), query_out=fetch(made.query_out), **basic
                ),
                mixed_out,
                {},
                [(pieces, dict(mix=0, proj=0))],
            )
        )
        return made

    def focal_stages(b):
        return [inputs_stage(b, groups, lanes), focal_stage(b, groups, lanes), mix_stage(b)]

    focal_made_out = dict(
        context=field, **gates_out, **query_out, **focal_out, **low_out, **mixed_out
    )

    def first_focal(x):
        if shared:
            taps = run_kernel(
                [taps_stage(tap_count, 1, width)],
                {},
                dict(taps=((BLOCKS, 1, room_rows, width), F32, FETCH)),
                {},
                [(focal_pieces[0], dict(wide=0, thin=0))],
            ).taps
            taps = shares.channels(taps)
            return Box(focal_apart(0, x, taps), taps=taps)
        return run_kernel(
            [taps_stage(tap_count, groups, lanes)] + focal_stages(0),
            dict(x=hold(x), **basic, **grid_columns),
            dict(taps=(taps_shape, F32, FETCH), **focal_made_out),
            dict(padded=padded),
            [(focal_pieces[0], dict(wide=0, thin=0, **weights_in))],
            False,
        )

    moves = [(mlp[0].stack, *y_move)]
    moves += [(focal[1].stack, "z", step) for step in z_rest[:1]]
    moves += [(mlp[1].stack, "z", z_first)]
    x_first, *x_rest = links.bits("x")
    moves += [(group_count, "x", x_first)]
    saved = [Box(x=x), Box()]
    made, got = beside(first_focal, x, moves)
    saved[0].update(made)
    taps = made.taps
    mlp[0].take(got[0], *y_move, not split_x)
    take_z(focal[1], got[1:-2])
    mlp[1].take(got[-2], "z", z_first)
    counted = group_count + got[-1]
    for step in x_rest:
        counted = counted + links.swap(counted, "x", step)
    denominator = counted[0:1, 0:1] * PATCH_IN
    y_move = focal[1].early("y")
    moves = [(focal[1].stack, *y_move)]
    moves += [(mlp[1].stack, "z", step) for step in z_rest]
    if split_x:
        x_move = mlp[0].early("x")
        moves += [(mlp[0].stack, *x_move)]
    middle, got = together(saved[0].middle, moves)
    focal[1].take(got[0], *y_move, True)
    take_z(mlp[1], got[1 : 1 + len(z_rest)])
    if split_x:
        mlp[0].take(got[-1], *x_move, True)
    y_move = mlp[1].early("y")
    moves = [(part, "core", 1) for part in mlp[0].parts + focal[1].parts]
    middle, got = together(after(middle, mlp[1].stack), moves)
    mlp_pieces[0] = pieces_of(mlp[0], got[:2], mlp_layout(own_hidden // parts_x), split_x)
    focal_pieces[1] = pieces_of(focal[1], got[2:], focal_layout, False)

    def second_focal(middle):
        inputs = dict(middle=hold(middle), **basic)
        outputs = dict(out=(whole, F32, FETCH), **mlp_out)
        if shared:
            made = run_kernel(
                [mlp_stage(0)], inputs, outputs, {}, [(mlp_pieces[0], up_down)]
            )
            lower = Box(hidden=made.hidden, slope=made.slope)
            return Box(focal_apart(1, made.out, taps), x=made.out, lower=dict(lower))
        made = run_kernel(
            [renamed(mlp_stage(0), middle=0, out=1)]
            + [renamed(stage, x=1) for stage in focal_stages(1)],
            {0: hold(middle), **basic, **grid_columns, **dict(taps=fetch(taps))},
            {1: (whole, F32, FETCH), **mlp_out, **focal_made_out},
            dict(padded=padded),
            [(mlp_pieces[0], up_down), (focal_pieces[1], weights_in)],
        )
        lower = dict(hidden=made.hidden, slope=made.slope)
        upper = Box({key: made[key] for key in focal_made_out})
        upper.update(x=made[1], lower=lower)
        return upper

    made, got = beside(second_focal, middle, [(mlp[1].stack, *y_move)])
    mlp[1].take(got[0], *y_move, True)
    saved[0].update(made.lower)
    saved[1].update(made)
    middle, far = twins(mlp[1], saved[1].middle)
    mlp_pieces[1] = pieces_of(mlp[1], far, mlp_layout(own_hidden), False)

    sums_out = ((8, width), F32, FETCH)
    head_part = (links.chan, patch_in // (2 * links.chan), width)
    hidden_part = (links.chan, own_hidden, width)
    own_part = (links.chan, own, width)
    made = run_kernel(
        [
            renamed(mlp_stage(1), out=0),
            renamed(head_stage, x=0, d_out=1, kept=2, sent=3, sums=4),
            renamed(mlp_back_stage(1), d_in=1),
        ],
        {
            **dict(middle=hold(middle), patches=fetch(patches), head=fetch(head_weight)),
            **dict(denom=(denominator, SCALAR), **basic),
        },
        {
            2: (head_part, BF16, HOLD),
            3: (head_part, BF16, HOLD),
            4: sums_out,
            **dict(
                d_out=(whole, F32, HOLD),
                kept=(hidden_part, BF16, HOLD),
                sent=(hidden_part, BF16, HOLD),
                sums=sums_out,
            ),
        },
        {
            0: pltpu.VMEM(whole, F32),
            1: pltpu.VMEM(whole, F32),
            **dict(
                hidden=pltpu.VMEM((rows, hidden_width), BF16),
                slope=pltpu.VMEM((rows, hidden_width), F32),
            ),
        },
        [(mlp_pieces[1], up_down)],
    )
    head_sums = made[4]
    sums = [[None] * 3 for _ in range(BLOCKS)]
    sums[1][1] = made.sums
    d_middle = made.d_out
    embed_rows = patch_in // (2 * links.chan)
    small_rows = small_rows_for(tap_count, links.chan)

    def mix_back(b, d_middle):
        shape = (1, rows, width) if shared else field_shape
        return run_kernel(
            [mix_back_stage(b, shape[0], shape[2])],
            dict(
                d_in=hold(d_middle),
                **fetch_all(saved[b], dict(query_out=0, mod=0, low=0)),
                **basic,
            ),
            dict(
                d_query=(whole, BF16, HOLD),
                d_sum=(shape, F32, HOLD),
                kept=(own_part, BF16, HOLD),
                sent=(own_part, BF16, HOLD),
                sums=sums_out,
            ),
            {},
            [(focal_pieces[b], dict(proj=0, mix=0))],
        )

    def focal_back(b, d_sum, d_middle, mixed):
        final = b == 0
        kept = saved[b]
        names = dict(context=0, gates=0, k1=0, k2=0, k3=0, s1=0, s2=0, s3=0, pool=0)
        levels_in = dict(taps=fetch(taps), **fetch_all(kept, names), **grid_columns)
        levels_temps = dict(padded=padded, d_padded=padded)
        inputs = dict(
            d_in=hold(d_middle),
            d_query=hold(mixed.d_query),
            x=fetch(kept.x),
            more_kept=hold(mixed.kept),
            more_sent=hold(mixed.sent),
            **basic,
        )
        part_rows = 2 * own
        if final:
            part_rows += embed_rows + small_rows // (2 * links.chan)
        part = (links.chan, part_rows, width)
        outputs = dict(kept=(part, BF16, HOLD), sent=(part, BF16, HOLD))
        temps = {}
        stages = [inputs_back_stage(b)]
        if final:
            sum_keys = [None]
            for c in range(BLOCKS):
                for kind in range(3):
                    if sums[c][kind] is not None:
                        key = 3 * c + kind
                        sum_keys.append(key)
                        inputs[key] = fetch(sums[c][kind])
            head_key, taps_key = 3 * BLOCKS, 3 * BLOCKS + 1
            inputs[head_key] = fetch(head_sums)
            inputs[taps_key] = fetch(d_taps)
            sum_keys.append(head_key)
            inputs.update(patches=fetch(patches), embedded=fetch(embedded.embedded))
            stages.append(embed_back_stage(tap_count, sum_keys, [None, taps_key], 2 * own))
            temps.update(
                small=pltpu.VMEM((small_rows, width), F32),
                input_sums=pltpu.VMEM((8, width), F32),
                d_out=pltpu.VMEM(whole, F32),
            )
        else:
            outputs.update(d_out=(whole, F32, HOLD), input_sums=sums_out)
        weights = [(focal_pieces[b], dict(query=0, key=0))]
        if shared:
            levels = run_kernel(
                [focal_back_stage(b, groups, lanes)],
                dict(d_sum=fetch(shares.to_images(d_sum)), **levels_in),
                dict(
                    d_context=((IMAGE_ROWS, channels), BF16, FETCH),
                    d_gates=((IMAGE_ROWS, 4 * LANES), F32, FETCH),
                    d_taps=((room_rows, channels), F32, FETCH),
                ),
                levels_temps,
            )
            tap_grad = shares.spread(levels.d_taps)
            inputs.update(
                d_context=fetch(shares.to_rows(levels.d_context)),
                d_gates=fetch(shares.sum_rows(levels.d_gates)),
            )
            if final:
                inputs.update(d_taps=fetch(tap_grad))
            made = run_kernel(stages, inputs, outputs, temps, weights)
            return Box(made, d_taps=tap_grad)
        temps.update(
            d_context=pltpu.VMEM(whole, BF16),
            d_gates=pltpu.VMEM((rows, 4 * LANES), F32),
            **levels_temps,
        )
        tap_shape = (room_rows, width)
        if final:
            temps.update(d_taps=pltpu.VMEM(tap_shape, F32))
        else:
            outputs.update(d_taps=(tap_shape, F32, FETCH))
        return run_kernel(
            [focal_back_stage(b, groups, lanes)] + stages,
            dict(d_sum=hold(d_sum), **levels_in) | inputs,
            outputs,
            temps,
            weights,
        )

    def mlp_back(b, d_x):
        return run_kernel(
            [mlp_back_stage(b)],
            dict(d_in=hold(d_x), **fetch_all(saved[b], dict(hidden=0, slope=0, middle=0)), **basic),
            dict(
                d_out=(whole, F32, HOLD),
                kept=(hidden_part, BF16, HOLD),
                sent=(hidden_part, BF16, HOLD),
                sums=sums_out,
            ),
            {},
            [(mlp_pieces[b], dict(down=0, up=0))],
        )

    z_last = len(links.bits("z")) - 1

    def open_mlp(kept, received):
        terms = links.open_sum(kept, received, parts_x)
        return links.early(terms, "x") if split_x else links.early(terms, "y")

    mixed, got = beside(
        lambda gate: mix_back(1, gate), d_middle, [(made.sent, "core", 1), (made[3], "core", 1)]
    )
    sums[1][2] = mixed.sums
    mlp_move, mlp_finish = open_mlp(made.kept, got[0])
    head_move, head_finish = links.early(links.open_sum(made[2], got[1]), "y")
    made, got = beside(
        lambda gate: focal_back(1, gate, d_middle, mixed), mixed.d_sum, [mlp_move, head_move]
    )
    mlp_sum = mlp_finish(got[0])
    sums[1][0] = made.input_sums
    d_taps = made.d_taps
    focal_kept = made.kept
    mlp_move, mlp_finish = links.early(mlp_sum, "y") if split_x else links.exchange(
        mlp_sum, "z", 0
    )
    head_move, head_finish = links.exchange(head_finish(got[1]), "z", 0)
    made, got = beside(
        lambda gate: mlp_back(0, gate),
        made.d_out,
        [(made.sent, "core", 1), mlp_move, head_move],
    )
    sums[0][1] = made.sums
    mlp_one = mlp_finish(got[1])
    d_middle = made.d_out
    focal_move, focal_finish = links.early(links.open_sum(focal_kept, got[0]), "y")
    one_move, one_finish = links.exchange(mlp_one, "z", 0 if split_x else z_last)
    head_move, head_finish = links.exchange(head_finish(got[2]), "z", z_last)
    mlp_kept = made.kept
    mixed, got = beside(
        lambda gate: mix_back(0, gate),
        d_middle,
        [(made.sent, "core", 1), focal_move, one_move, head_move],
    )
    sums[0][2] = mixed.sums
    mlp_move, mlp_finish = open_mlp(mlp_kept, got[0])
    focal_move, focal_finish = links.exchange(focal_finish(got[1]), "z", 0)
    mlp_one = one_finish(got[2])
    head_low = total(head_finish(got[3]))
    if split_x:
        one_move, one_finish = links.exchange(mlp_one, "z", z_last)
    else:
        one_low = total(mlp_one)
        one_move = (one_low, "x", x_first)
    moves = [mlp_move, focal_move, one_move, (head_low, "x", x_first)]
    made, got = beside(lambda gate: focal_back(0, gate, d_middle, mixed), mixed.d_sum, moves)
    mlp_sum = mlp_finish(got[0])

    def rest_x(low, received):
        summed = low.astype(F32) + received.astype(F32)
        for step in x_rest:
            low = summed.astype(BF16)
            summed = low.astype(F32) + links.swap(low, "x", step).astype(F32)
        return summed

    head = Gather(links, rest_x(head_low, got[3]).astype(BF16))
    rate = 0.2 * math.sqrt(group_rows * lax.axis_size("dp"))

    focal_move, focal_finish = links.exchange(focal_finish(got[1]), "z", z_last)
    if split_x:
        one_move, one_finish = links.regather_x(total(one_finish(got[2])).astype(F32))
        zero_move, zero_finish = links.early(mlp_sum, "y")
    else:
        mlp_one = rest_x(one_low, got[2])
        zero_move, zero_finish = links.exchange(mlp_sum, "z", 0)
    lower_kept, got = together(made.kept, [(made.sent, "core", 1)])
    lower_move, lower_finish = links.early(links.open_sum(lower_kept, got[0]), "y")
    moves = [lower_move, focal_move, (head.stack, "z", z_first)]
    if split_x:
        moves.append(one_move)
    gate, got = together(here, moves)
    lower_move, lower_finish = links.exchange(lower_finish(got[0]), "z", 0)
    focal_low = total(focal_finish(got[1]))
    head.take(got[2], "z", z_first)
    if split_x:
        mlp_one = one_finish(got[3])
    moves = [lower_move, zero_move] + [(head.stack, "z", step) for step in z_rest]
    gate, got = together(gate, moves)
    lower_move, lower_finish = links.exchange(lower_finish(got[0]), "z", z_last)
    take_z(head, got[2:])
    mlp_zero = zero_finish(got[1])
    zero_move, zero_finish = links.exchange(mlp_zero, "z", 0 if split_x else z_last)
    head_move = head.early("y")
    moves = [lower_move, (focal_low, "x", x_first), (head.stack, *head_move), zero_move]
    (gate, mlp_one), got = together((gate, mlp_one), moves)
    lower_low = total(lower_finish(got[0]))
    focal_one = rest_x(focal_low, got[1])
    head.take(got[2], *head_move, True)
    mlp_zero = zero_finish(got[3])
    if split_x:
        zero_move, zero_finish = links.exchange(mlp_zero, "z", z_last)
    else:
        zero_low = total(mlp_zero)
        zero_move = (zero_low, "x", x_first)
    moves = [(lower_low, "x", x_first), zero_move]
    moves += [(part, "core", 1) for part in head.parts]
    (focal_one, mlp_one), got = together((focal_one, mlp_one), moves)
    lower = rest_x(lower_low, got[0])
    head_far = got[2:]
    if split_x:
        zero_rows = total(zero_finish(got[1])).astype(F32)
        zero_move, zero_finish = links.regather_x(zero_rows)
    else:
        mlp_zero = rest_x(zero_low, got[1])
    common = Gather(links, lower[2 * own :].astype(BF16))
    moves = common.direct()
    count = len(moves)
    if split_x:
        moves.append(zero_move)
    (focal_one, mlp_one, late), got = together((focal_one, mlp_one, lower[: 2 * own]), moves)
    common.take_direct(got[:count])
    if split_x:
        mlp_zero = zero_finish(got[count])
    y_move = common.early("y")
    common.take(links.swap(common.stack, *y_move), *y_move, True)
    rows_early = jnp.concatenate([mlp_one, mlp_zero, focal_one, late], axis=0)
    rows_early, _stack = lax.optimization_barrier((rows_early, common.stack))
    halves = links.both_halves(rows_early)
    head_far, _stack = lax.optimization_barrier((head_far, common.stack))
    head_pieces = Pieces(
        links.slots(head.masks, False),
        head.parts,
        head_far,
        dict(head0=(0, 0, embed_rows), head1=(1, 0, embed_rows)),
    )
    weight_out = (head_weight.shape, F32, FETCH)
    new_head = run_kernel(
        [update_head_stage(rate)],
        dict(weight=fetch(head_weight), moment=fetch(head_moment)),
        dict(new_weight=weight_out, new_moment=weight_out),
        {},
        [(head_pieces, dict(head0=0, head1=0))],
    )
    ends = (own_hidden, 2 * own_hidden)
    grad_mlp = jnp.stack(
        [
            jnp.stack([part[ends[0] : ends[1]] for part in halves]),
            jnp.stack([part[: ends[0]] for part in halves]),
        ]
    )
    one = [part[ends[1] : ends[1] + 2 * own] for part in halves]
    late = [part[ends[1] + 2 * own :] for part in halves]
    grad_focal = jnp.stack([jnp.stack([part[:own] for part in parts]) for parts in (late, one)])
    grad_mixer = jnp.stack([jnp.stack([part[own:] for part in parts]) for parts in (late, one)])
    results = []
    for weight, moment, average, gradient, order, back in (
        (focal_input, focal_moment, focal_average, grad_focal, (0, 2, 3, 1), (0, 3, 1, 2)),
        (mixers, mixer_moment, mixer_average, grad_mixer, (0, 1, 3, 2), (0, 1, 3, 2)),
        (mlp_weights, mlp_moment, mlp_average, grad_mlp, (0, 1, 3, 2), (0, 1, 3, 2)),
    ):
        weight, moment, average = (
            jnp.transpose(array, order) for array in (weight, moment, average)
        )
        new_weight, new_moment = nesterov(weight, moment, gradient, rate)
        new_average = AVERAGE * average + (1.0 - AVERAGE) * new_weight
        results.extend(
            jnp.transpose(array, back) for array in (new_weight, new_moment, new_average)
        )
    there, results, *held = lax.optimization_barrier(
        (common.parts[1], results, new_head.new_weight, new_head.new_moment)
    )
    common_near = [common.parts[0], there]
    common_far = [links.swap_core(part) for part in common_near]
    small_part = small_rows // (2 * links.chan)
    common_pieces = Pieces(
        links.slots(common.masks, False),
        common_near,
        common_far,
        dict(
            embed0=(0, 0, embed_rows),
            embed1=(1, 0, embed_rows),
            small0=(0, embed_rows, small_part),
            small1=(1, embed_rows, small_part),
        ),
    )
    weight_out = (embed_weight.shape, F32, FETCH)
    vector_out = (vectors.shape, F32, HOLD)
    kernel_out = (kernel_rows.shape, F32, HOLD)
    made = run_kernel(
        [update_shared_stage(tap_count, own, rate)],
        dict(
            weight=hold(embed_weight),
            moment=hold(embed_moment),
            vectors=hold(vectors),
            vector_moment=hold(vector_moment),
            vector_average=hold(vector_average),
            kernels=hold(kernel_rows),
            kernel_moment=hold(jnp.transpose(kernel_moment, (0, 2, 1))),
            kernel_average=hold(jnp.transpose(kernel_average, (0, 2, 1))),
        ),
        dict(
            new_weight=weight_out,
            new_moment=weight_out,
            new_vectors=vector_out,
            new_vector_moment=vector_out,
            new_vector_average=vector_out,
            new_kernels=kernel_out,
            new_kernel_moment=kernel_out,
            new_kernel_average=kernel_out,
            loss=((1, LANES), F32, HOLD),
        ),
        dict(packed=pltpu.VMEM((-(-vectors.shape[0] // 8) * 8, width), F32)),
        [(common_pieces, dict(embed0=0, embed1=0, small0=0, small1=0))],
    )
    return (
        made.loss[0, 0],
        made.new_weight,
        made.new_moment,
        *held,
        made.new_vectors,
        made.new_vector_moment,
        made.new_vector_average,
        *results,
        *[
            jnp.transpose(array, (0, 2, 1))
            for array in (made.new_kernels, made.new_kernel_moment, made.new_kernel_average)
        ],
    )


def solution(mesh):
    split = P(None, None, None, "chan")
    taps = P(None, None, "chan")
    return jax.shard_map(
        shards,
        mesh=mesh,
        in_specs=(P(("dp", "chan"), None), P("dp"), P("dp"), P("dp", None, None))
        + (P(),) * 7
        + (split,) * 9
        + (taps,) * 3,
        out_specs=(P(),) * 8 + (split,) * 9 + (taps,) * 3,
        check_vma=False,
    )
```

time: 1020 us -> 245 us (0.24)
  waiting for transfers between devices: 578 us -> 43.4 us
  local copies, waits for them, and re-layouts: 201 us -> 9.86 us
  Pallas kernels: 0 us -> 86.7 us
  blocking collectives: 79.8 us -> 0 us
  starting transfers between devices: 0.46 us -> 57.7 us
  other arithmetic: 86.4 us -> 40.1 us
  matrix products: 40.8 us -> 0 us
  between operations: 20.1 us -> 2.71 us
    reduce_scatter x4 -> x0, waiting for transfers between devices: 279 us -> none  [scatter_grads(): mine = lax.psum_scatter(stacked, 'chan', scatter_dimension=0, tiled=False)]
    psum x3 -> x0, waiting for transfers between devices: 213 us -> none  [the longest x1 137 us: shards(): lax.psum(grad_embed.astype(jnp.bfloat16), both).astype(jnp.float32)]
    another operation x166 -> x5, local copies, waits for them, and re-layouts: 115 us -> 0.42 us  [the longest x3 0.27 us: slots(): return jnp.stack([self.core, self.place] + places).astype(jnp.int32)]
    pallas_call x0 -> x15, Pallas kernels: none -> 86.7 us  [the longest x11 80.7 us: run_kernel(): pl.pallas_call(body, name=stages[-1].__name__, in_specs=in_specs, out_spe...]
    all_gather x4 -> x0, waiting for transfers between devices: 86.3 us -> none  [gather_weights(): gathered = lax.all_gather(packed, 'chan', axis=0, tiled=False)]
    ppermute x0 -> x63, starting transfers between devices: none -> 57.7 us  [the longest x35 47.8 us: swap(): lax.ppermute(values, 'chan', [(i, i ^ step) for i in range(self.chan)])]
    psum x2 -> x0, blocking collectives: 46.6 us -> none  [the longest x1 40 us: shards(): lax.psum((grad_vectors, jnp.stack(kernel_parts), loss_part), both)]
    reduce_sum x29 -> x1, other arithmetic: 45.3 us -> 1.32 us  [shards(): group_count = jnp.broadcast_to(jnp.sum(validity * masked), (8, LANES))]
  transfers between devices with their start and end apart: 11 -> 63, of which waited for: 10 -> 22; matrix products, arithmetic and copies ran while one was open for 11% -> 15% of each run, Pallas kernels for 0% -> 29%
where the time goes in v2:
time: 245 us; the launch traced here: 240 us
  Pallas kernels  86.7 us (35%)
  starting transfers between devices  57.7 us (24%)
  waiting for transfers between devices  43.4 us (18%)
  other arithmetic  40.1 us (16%)
  local copies, waits for them, and re-layouts  9.86 us (4%)
  between operations  2.71 us (1%)
    pallas_call x11, Pallas kernels, run_kernel(): pl.pallas_call(body, name=stages[-1].__name__, in_specs=in_specs, out_spe...  80.7 us
    ppermute x35, starting transfers between devices, swap(): lax.ppermute(values, 'chan', [(i, i ^ step) for i in range(self.chan)])  47.8 us
    ppermute x35, waiting for transfers between devices, swap(): lax.ppermute(values, 'chan', [(i, i ^ step) for i in range(self.chan)])  28.3 us
    convert_element_type x20, other arithmetic, total(): return result.astype(BF16)  22.7 us
    ppermute x28, waiting for transfers between devices, swap(): lax.ppermute(values, 'dp', [(i, i ^ step) for i in range(self.nx * self.n...  15.1 us
    ppermute x28, starting transfers between devices, swap(): lax.ppermute(values, 'dp', [(i, i ^ step) for i in range(self.nx * self.n...  9.87 us
    unnamed x115, local copies, waits for them, and re-layouts  8.17 us
    pallas_call x4, Pallas kernels, pack_rows(): pl.pallas_call(body, name=pack_rows.__name__, in_specs=[pl.BlockSpec(memo...  5.97 us
  transfers between devices with their start and end apart: 63, of which 22 were waited for; matrix products, arithmetic and copies ran while one was open for 15% of the time, Pallas kernels for 29%

profile of v2, /device:TPU:0, one launch (start us, length us, event | category | flops | bytes accessed | tf_op | source)
XLA Modules:
  0.0 240.4 jit_solution(18266325174912941827)
XLA Ops:
  3.1 3.1 %collective-permute-start = (bf16[1,144,384]{2,1,0:T(8,128)(2,1)S(1)}, bf16[1,144,384]{2,1,0:T(8,128)(2,1)S(1)}, u32[]{:S(2)}, u32[]{:S(2)}) collective-permute-start(bf16[1,144,384]{2,1,0:T(8,128)(2,1)S(1)} %bitcast.357), channel_id=1, source_target_pairs={{0,2},{1,3},{2,0},{3,1},{4,6},{5,7},{6,4},{7,5},{8,10},{9,11},{10,... | collective-permute-start | bytes 331784 | tf_op jit(solution)/shard_map/ppermute | solution.py:98
  6.1 2.6 %collective-permute-start.1 = (bf16[1,144,384]{2,1,0:T(8,128)(2,1)S(1)}, bf16[1,144,384]{2,1,0:T(8,128)(2,1)S(1)}, u32[]{:S(2)}, u32[]{:S(2)}) collective-permute-start(bf16[1,144,384]{2,1,0:T(8,128)(2,1)S(1)} %bitcast.358), channel_id=1, source_target_pairs={{0,4},{1,5},{2,6},{3,7},{4,0},{5,1},{6,2},{7,3},{8,12},{9,13},{10,... | collective-permute-start | bytes 331784 | tf_op jit(solution)/shard_map/ppermute | solution.py:98
  14.0 2.6 %embed_stage.1 = (f32[256,384]{1,0:T(8,128)S(1)}, f32[256,384]{1,0:T(8,128)}) custom-call(bf16[256,768]{1,0:T(8,128)(2,1)} %refs_26_.1, f32[768,384]{1,0:T(8,128)} %refs_0_.5, f32[26,384]{1,0:T(8,128)} %refs_2_.5, f32[256,8]{1,0:T(8,128)} %copy.76.refs_3_.refs_2_.refs_5_.refs_11_.refs_18_), custom_call_target="tpu_custom_call" | custom-call | tf_op jit(solution)/shard_map/embed_stage/pallas_call | solution.py:412
  19.2 2.8 %collective-permute-start.3 = (bf16[1,96,384]{2,1,0:T(8,128)(2,1)S(1)}, bf16[1,96,384]{2,1,0:T(8,128)(2,1)S(1)}, u32[]{:S(2)}, u32[]{:S(2)}) collective-permute-start(bf16[1,96,384]{2,1,0:T(8,128)(2,1)S(1)} %bitcast.332), channel_id=1, source_target_pairs={{0,4},{1,5},{2,6},{3,7},{4,0},{5,1},{6,2},{7,3},{8,12},{9,13},{10,... | collective-permute-start | bytes 221192 | tf_op jit(solution)/shard_map/ppermute | solution.py:98
  37.1 10.0 %mix_forward.2 = (f32[2,3,88,128]{3,2,1,0:T(8,128)}, f32[3,256,128]{2,1,0:T(8,128)}, f32[256,512]{1,0:T(8,128)}, f32[256,384]{1,0:T(8,128)}, f32[3,256,128]{2,1,...) custom-call(f32[256,384]{1,0:T(8,128)S(1)} %get-tuple-element.257.re, ...), custom_call_target="tpu_custom_call" | custom-call | tf_op jit(solution)/shard_map/mix_forward/pallas_call | solution.py:412
  51.9 5.4 %collective-permute-done.15 = bf16[2,192,384]{2,1,0:T(8,128)(2,1)S(1)} collective-permute-done((bf16[2,192,384]{2,1,0:T(8,128)(2,1)S(1)}, bf16[2,192,384]{2,1,0:T(8,128)(2,1)S(1)}, u32[]{:S(2)}, u32[]{:S(2)}) %collective-permute-start.15) | collective-permute-done | bytes 294944 | tf_op jit(solution)/shard_map/ppermute | solution.py:98
  58.4 5.0 %collective-permute-done.16.refs_7_.refs_8_ = bf16[8,96,384]{2,1,0:T(8,128)(2,1)} collective-permute-done((bf16[8,96,384]{2,1,0:T(8,128)(2,1)S(1)}, bf16[8,96,384]{2,1,0:T(8,128)(2,1)}, u32[]{:S(2)}, u32[]{:S(2)}) %collective-permute-start.16) | collective-permute-done | bytes 589856 | tf_op jit(solution)/shard_map/ppermute | solution.py:100
  68.5 10.2 %mix_forward.3 = (f32[256,384]{1,0:T(8,128)}, bf16[256,1536]{1,0:T(8,128)(2,1)}, f32[256,1536]{1,0:T(8,128)}, f32[3,256,128]{2,1,0:T(8,128)}, f32[256,512]{1,0:T...) custom-call(f32[256,384]{1,0:T(8,128)S(1)} %get-tuple-element.284.re, ...), custom_call_target="tpu_custom_call" | custom-call | tf_op jit(solution)/shard_map/mix_forward/pallas_call | solution.py:412
  83.8 10.4 %mlp_backward.2 = (bf16[8,48,384]{2,1,0:T(8,128)(2,1)S(1)}, bf16[8,48,384]{2,1,0:T(8,128)(2,1)S(1)}, f32[8,384]{1,0:T(8,128)}, f32[256,384]{1,0:T(8,128)S(1)}, b...) custom-call(f32[256,384]{1,0:T(8,128)S(1)} %get-tuple-element.308.refs_0_, ...), custom_call_target="tpu_custom_call" | custom-call | tf_op jit(solution)/shard_map/mlp_backward/pallas_call | solution.py:412
  95.0 4.2 %mix_backward.2 = (bf16[256,384]{1,0:T(8,128)(2,1)S(1)}, f32[3,256,128]{2,1,0:T(8,128)S(1)}, bf16[8,48,384]{2,1,0:T(8,128)(2,1)S(1)}, bf16[8,48,384]{2,1,0:T(8,128)(2,1)S(1)}, f32[8,384]{1,0:T(8,128)}) custom-call(f32[256,384]{1,0:T(8,128)S(1)} %get-tuple-element.315.refs_0_.refs_12_, f32[256,384]{1,0:T(8,128)} %get-tuple-element.316.refs_1_, ...), custom_call_target="tpu_custom_call" | custom-call | tf_op jit(solution)/shard_map/mix_backward/pallas_call | solution.py:412
  104.3 10.9 %inputs_backward.1 = (bf16[8,96,384]{2,1,0:T(8,128)(2,1)S(1)}, bf16[8,96,384]{2,1,0:T(8,128)(2,1)}, f32[256,384]{1,0:T(8,128)S(1)}, f32[8,384]{1,0:T(8,128)}, f32[88,384]{1,0:T(8,128)}) custom-call(f32[3,256,128]{2,1,0:T(8,128)S(1)} %get-tuple-element.329.refs_0_, f32[2,3,88,128]{3,2,1,0:T(8,128)} %get-tuple-element.285.refs_4_.refs_1_, ...), custom_call_target="tpu_custom_call" | custom-call | tf_op jit(solution)/shard_map/inputs_backward/pallas_call | solution.py:412
  121.4 8.5 %mlp_backward.3 = (f32[256,384]{1,0:T(8,128)S(1)}, bf16[8,192,384]{2,1,0:T(8,128)(2,1)S(1)}, bf16[8,192,384]{2,1,0:T(8,128)(2,1)}, f32[8,384]{1,0:T(8,128)}) custom-call(f32[256,384]{1,0:T(8,128)S(1)} %copy-done.11, bf16[256,1536]{1,0:T(8,128)(2,1)} %get-tuple-element.353.refs_1_, f32[256,1536]{1,0:T(8,128)} %get-tuple-element.354.refs_2_, ...), custom_call_target="tpu_custom_call" | custom-call | tf_op jit(solution)/shard_map/mlp_backward/pallas_call | solution.py:412
  140.1 4.2 %mix_backward.3 = (bf16[256,384]{1,0:T(8,128)(2,1)S(1)}, f32[3,256,128]{2,1,0:T(8,128)S(1)}, bf16[8,48,384]{2,1,0:T(8,128)(2,1)S(1)}, bf16[8,48,384]{2,1,0:T(8,128)(2,1)S(1)}, f32[8,384]{1,0:T(8,128)}) custom-call(f32[256,384]{1,0:T(8,128)S(1)} %get-tuple-element.365.refs_0_.refs_12_, f32[256,384]{1,0:T(8,128)} %get-tuple-element.366.refs_1_, ...), custom_call_target="tpu_custom_call" | custom-call | tf_op jit(solution)/shard_map/mix_backward/pallas_call | solution.py:412
  152.6 10.9 %embed_backward.1 = (bf16[8,160,384]{2,1,0:T(8,128)(2,1)S(1)}, bf16[8,160,384]{2,1,0:T(8,128)(2,1)S(1)}) custom-call(f32[3,256,128]{2,1,0:T(8,128)S(1)} %get-tuple-element.380.refs_0_, f32[2,3,88,128]{3,2,1,0:T(8,128)} %get-tuple-element.285.refs_4_.refs_1_, f32[3,256,128]{2,1,0:T(8,128)} %get-tuple-element.381.refs_2_, ...), custom_call_target="tpu_custom_call" | custom-call | tf_op jit(solution)/shard_map/embed_backward/pallas_call | solution.py:412
  174.2 3.0 %collective-permute-done.41 = bf16[96,384]{1,0:T(8,128)(2,1)S(1)} collective-permute-done((bf16[96,384]{1,0:T(8,128)(2,1)S(1)}, bf16[96,384]{1,0:T(8,128)(2,1)S(1)}, u32[]{:S(2)}, u32[]{:S(2)}) %collective-permute-start.41) | collective-permute-done | bytes 73760 | tf_op jit(solution)/shard_map/ppermute | solution.py:98
  177.2 3.2 %collective-permute-done.40 = bf16[2,2,160,384]{3,2,1,0:T(8,128)(2,1)S(1)} collective-permute-done((bf16[2,2,160,384]{3,2,1,0:T(8,128)(2,1)S(1)}, bf16[2,2,160,384]{3,2,1,0:T(8,128)(2,1)S(1)}, u32[]{:S(2)}, u32[]{:S(2)}) %collective-permute-start.40) | collective-permute-done | bytes 491552 | tf_op jit(solution)/shard_map/ppermute | solution.py:98
  183.2 2.7 %collective-permute-done.45 = bf16[2,2,96,384]{3,2,1,0:T(8,128)(2,1)S(1)} collective-permute-done((bf16[2,2,96,384]{3,2,1,0:T(8,128)(2,1)}, bf16[2,2,96,384]{3,2,1,0:T(8,128)(2,1)S(1)}, u32[]{:S(2)}, u32[]{:S(2)}) %collective-permute-start.45) | collective-permute-done | bytes 294944 | tf_op jit(solution)/shard_map/ppermute | solution.py:98
  185.9 2.7 %collective-permute-done.46 = bf16[2,48,384]{2,1,0:T(8,128)(2,1)} collective-permute-done((bf16[2,48,384]{2,1,0:T(8,128)(2,1)}, bf16[2,48,384]{2,1,0:T(8,128)(2,1)}, u32[]{:S(2)}, u32[]{:S(2)}) %collective-permute-start.46) | collective-permute-done | bytes 73760 | tf_op jit(solution)/shard_map/ppermute | solution.py:98
  194.6 2.2 collective-permute-start.47
  198.5 3.8 %collective-permute-done.48 = bf16[96,384]{1,0:T(8,128)(2,1)S(1)} collective-permute-done((bf16[96,384]{1,0:T(8,128)(2,1)S(1)}, bf16[96,384]{1,0:T(8,128)(2,1)S(1)}, u32[]{:S(2)}, u32[]{:S(2)}) %collective-permute-start.48) | collective-permute-done | bytes 73760 | tf_op jit(solution)/shard_map/ppermute | solution.py:100
  205.8 3.3 %collective-permute-done.52 = bf16[96,384]{1,0:T(8,128)(2,1)S(1)} collective-permute-done((bf16[96,384]{1,0:T(8,128)(2,1)S(1)}, bf16[96,384]{1,0:T(8,128)(2,1)S(1)}, u32[]{:S(2)}, u32[]{:S(2)}) %collective-permute-start.52) | collective-permute-done | bytes 73760 | tf_op jit(solution)/shard_map/ppermute | solution.py:98
  216.2 2.2 collective-permute-done.56
  221.1 4.4 %update_head.1 = (f32[384,768]{1,0:T(8,128)}, f32[384,768]{1,0:T(8,128)}) custom-call(f32[384,768]{1,0:T(8,128)} %refs_0_.4, f32[384,768]{1,0:T(8,128)} %refs_1_.10, s32[10]{0:T(128)S(1)} %stack.251.refs_10_.refs_6_.refs_19_.refs_2_, bf16[4,48,384]{2,1,0:T(8,128)(2,1)} %copy-done.33, bf16[4,48,384]{2,1,0:T(8,128)(2,1)} %copy-done.46, ...), custom_call_target="tpu_custom_call" | custom-call | tf_op jit(solution)/shard_map/update_head/pallas_call | solution.py:412
  235.8 4.4 %update_shared.1 = (f32[768,384]{1,0:T(8,128)}, f32[768,384]{1,0:T(8,128)}, f32[26,384]{1,0:T(8,128)}, f32[26,384]{1,0:T(8,128)}, f32[26,384]{1,0:T(8,128)}, /*i...) custom-call(f32[768,384]{1,0:T(8,128)S(1)} %copy-done.2, ...), custom_call_target="tpu_custom_call" | custom-call | tf_op jit(solution)/shard_map/update_shared/pallas_call | solution.py:412
  (300 shorter events, 115.0 us)
Async XLA Ops:
  3.1 13.5 %collective-permute-start = (bf16[1,144,384]{2,1,0:T(8,128)(2,1)S(1)}, bf16[1,144,384]{2,1,0:T(8,128)(2,1)S(1)}, u32[]{:S(2)}, u32[]{:S(2)}) collective-permute-start(bf16[1,144,384]{2,1,0:T(8,128)(2,1)S(1)} %bitcast.357), channel_id=1, source_target_pairs={{0,2},{1,3},{2,0},{3,1},{4,6},{5,7},{6,4},{7,5},{8,10},{9,11},{10,... | collective-permute-start | bytes 331784 | tf_op jit(solution)/shard_map/ppermute | solution.py:98
  17.6 14.0 %collective-permute-start.5 = (bf16[4,144,384]{2,1,0:T(8,128)(2,1)S(1)}, bf16[4,144,384]{2,1,0:T(8,128)(2,1)S(1)}, u32[]{:S(2)}, u32[]{:S(2)}) collective-permute-start(bf16[4,144,384]{2,1,0:T(8,128)(2,1)S(1)} %pad_maximum_fusion.4.refs_5_.refs_7_.refs_29_), channel_id=1, source_target_pairs={{0,1},{1,0},{2,3},{3,2},{4,5},{5,4},{6,7},{7,6},{8,9},{9,8},{10,11... | collective-permute-start | bytes 1327112 | tf_op jit(solution)/shard_map/ppermute | solution.py:98
  29.9 17.3 %collective-permute-start.12 = (bf16[1,192,384]{2,1,0:T(8,128)(2,1)S(1)}, bf16[1,192,384]{2,1,0:T(8,128)(2,1)S(1)}, u32[]{:S(2)}, u32[]{:S(2)}) collective-permute-start(bf16[1,192,384]{2,1,0:T(8,128)(2,1)S(1)} %bitcast.329), channel_id=1, source_target_pairs={{0,4},{1,5},{2,6},{3,7},{4,0},{5,1},{6,2},{7,3},{8,12},{9,13},{10,... | collective-permute-start | bytes 442376 | tf_op jit(solution)/shard_map/ppermute | solution.py:98
  32.4 14.8 %collective-permute-start.10 = (bf16[4,96,384]{2,1,0:T(8,128)(2,1)}, bf16[4,96,384]{2,1,0:T(8,128)(2,1)}, u32[]{:S(2)}, u32[]{:S(2)}) collective-permute-start(bf16[4,96,384]{2,1,0:T(8,128)(2,1)} %pad_maximum_fusion.5), channel_id=1, source_target_pairs={{0,1},{1,0},{2,3},{3,2},{4,5},{5,4},{6,7},{7,6},{8,9},{9,8},{10,11... | collective-permute-start | bytes 884744 | tf_op jit(solution)/shard_map/ppermute | solution.py:98
  32.9 14.3 %collective-permute-start.11 = (bf16[2,96,384]{2,1,0:T(8,128)(2,1)S(1)}, bf16[2,96,384]{2,1,0:T(8,128)(2,1)}, u32[]{:S(2)}, u32[]{:S(2)}) collective-permute-start(bf16[2,96,384]{2,1,0:T(8,128)(2,1)S(1)} %pad_maximum_fusion.12), channel_id=1, source_target_pairs={{0,2},{1,3},{2,0},{3,1},{4,6},{5,7},{6,4},{7,5},{8,10},{9,11},{10,... | collective-permute-start | bytes 442376 | tf_op jit(solution)/shard_map/ppermute | solution.py:98
  48.4 15.0 %collective-permute-start.16 = (bf16[8,96,384]{2,1,0:T(8,128)(2,1)S(1)}, bf16[8,96,384]{2,1,0:T(8,128)(2,1)}, u32[]{:S(2)}, u32[]{:S(2)}) collective-permute-start(bf16[8,96,384]{2,1,0:T(8,128)(2,1)S(1)} %pad_maximum_fusion.2.refs_6_.refs_7_), channel_id=1, source_target_pairs={{0,16},{8,24},{16,0},{24,8},{1,17},{9,25},{17,1},{25,9},{2,18},{10... | collective-permute-start | bytes 1769480 | tf_op jit(solution)/shard_map/ppermute | solution.py:100
  51.9 15.7 %collective-permute-start.17 = (bf16[8,96,384]{2,1,0:T(8,128)(2,1)S(1)}, bf16[8,96,384]{2,1,0:T(8,128)(2,1)}, u32[]{:S(2)}, u32[]{:S(2)}) collective-permute-start(bf16[8,96,384]{2,1,0:T(8,128)(2,1)S(1)} %pad_maximum_fusion.2.refs_6_.refs_7_), channel_id=1, source_target_pairs={{0,8},{8,0},{16,24},{24,16},{1,9},{9,1},{17,25},{25,17},{2,10},{10... | collective-permute-start | bytes 1769480 | tf_op jit(solution)/shard_map/ppermute | solution.py:100
  64.3 16.1 %collective-permute-start.21 = (bf16[4,192,384]{2,1,0:T(8,128)(2,1)}, bf16[4,192,384]{2,1,0:T(8,128)(2,1)}, u32[]{:S(2)}, u32[]{:S(2)}) collective-permute-start(bf16[4,192,384]{2,1,0:T(8,128)(2,1)} %pad_maximum_fusion.3.refs_7_), channel_id=1, source_target_pairs={{0,1},{1,0},{2,3},{3,2},{4,5},{5,4},{6,7},{7,6},{8,9},{9,8},{10,11... | collective-permute-start | bytes 1769480 | tf_op jit(solution)/shard_map/ppermute | solution.py:98
  67.4 14.8 %collective-permute-start.22 = (bf16[4,192,384]{2,1,0:T(8,128)(2,1)}, bf16[4,192,384]{2,1,0:T(8,128)(2,1)S(1)}, u32[]{:S(2)}, u32[]{:S(2)}) collective-permute-start(bf16[4,192,384]{2,1,0:T(8,128)(2,1)} %pad_maximum_fusion.3.refs_7_), channel_id=1, source_target_pairs={{0,8},{8,0},{16,24},{24,16},{1,9},{9,1},{17,25},{25,17},{2,10},{10... | collective-permute-start | bytes 1769480 | tf_op jit(solution)/shard_map/ppermute | solution.py:100
  101.3 16.0 %collective-permute-start.26 = (bf16[2,2,2,96,384]{4,3,2,1,0:T(8,128)(2,1)}, bf16[2,2,2,96,384]{4,3,2,1,0:T(8,128)(2,1)}, u32[]{:S(2)}, u32[]{:S(2)}) collective-permute-start(bf16[2,2,2,96,384]{4,3,2,1,0:T(8,128)(2,1)} %fusion.3), channel_id=1, source_target_pairs={{0,16},{8,24},{16,0},{24,8},{1,17},{9,25},{17,1},{25,9},{2,18},{10... | collective-permute-start | bytes 1769480 | tf_op jit(solution)/shard_map/ppermute | solution.py:100
  102.8 13.2 %collective-permute-start.27 = (bf16[2,2,48,384]{3,2,1,0:T(8,128)(2,1)S(1)}, bf16[2,2,48,384]{3,2,1,0:T(8,128)(2,1)}, u32[]{:S(2)}, u32[]{:S(2)}) collective-permute-start(bf16[2,2,48,384]{3,2,1,0:T(8,128)(2,1)S(1)} %fusion.22), channel_id=1, source_target_pairs={{0,1},{1,0},{2,3},{3,2},{4,5},{5,4},{6,7},{7,6},{8,9},{9,8},{10,11... | collective-permute-start | bytes 442376 | tf_op jit(solution)/shard_map/ppermute | solution.py:98
  117.3 13.4 %collective-permute-start.28 = (bf16[8,96,384]{2,1,0:T(8,128)(2,1)}, bf16[8,96,384]{2,1,0:T(8,128)(2,1)}, u32[]{:S(2)}, u32[]{:S(2)}) collective-permute-start(bf16[8,96,384]{2,1,0:T(8,128)(2,1)} %get-tuple-element.349), channel_id=1, source_target_pairs={{0,8},{8,0},{16,24},{24,16},{1,9},{9,1},{17,25},{25,17},{2,10},{10... | collective-permute-start | bytes 1769480 | tf_op jit(solution)/shard_map/ppermute | solution.py:100
  130.7 13.7 %collective-permute-start.31 = (bf16[8,192,384]{2,1,0:T(8,128)(2,1)}, bf16[8,192,384]{2,1,0:T(8,128)(2,1)}, u32[]{:S(2)}, u32[]{:S(2)}) collective-permute-start(bf16[8,192,384]{2,1,0:T(8,128)(2,1)} %get-tuple-element.360), channel_id=1, source_target_pairs={{0,8},{8,0},{16,24},{24,16},{1,9},{9,1},{17,25},{25,17},{2,10},{10... | collective-permute-start | bytes 3538952 | tf_op jit(solution)/shard_map/ppermute | solution.py:100
  132.5 11.9 %collective-permute-start.32 = (bf16[2,2,96,384]{3,2,1,0:T(8,128)(2,1)}, bf16[2,2,96,384]{3,2,1,0:T(8,128)(2,1)}, u32[]{:S(2)}, u32[]{:S(2)}) collective-permute-start(bf16[2,2,96,384]{3,2,1,0:T(8,128)(2,1)} %fusion.9), channel_id=1, source_target_pairs={{0,1},{1,0},{2,3},{3,2},{4,5},{5,4},{6,7},{7,6},{8,9},{9,8},{10,11... | collective-permute-start | bytes 884744 | tf_op jit(solution)/shard_map/ppermute | solution.py:98
  145.7 17.7 %collective-permute-start.35 = (bf16[2,2,2,96,384]{4,3,2,1,0:T(8,128)(2,1)S(1)}, bf16[2,2,2,96,384]{4,3,2,1,0:T(8,128)(2,1)S(1)}, u32[]{:S(2)}, u32[]{:S(2)}) collective-permute-start(bf16[2,2,2,96,384]{4,3,2,1,0:T(8,128)(2,1)S(1)} %fusion.4), channel_id=1, source_target_pairs={{0,16},{8,24},{16,0},{24,8},{1,17},{9,25},{17,1},{25,9},{2,18},{10... | collective-permute-start | bytes 1769480 | tf_op jit(solution)/shard_map/ppermute | solution.py:100
  147.4 16.1 %collective-permute-start.36 = (bf16[2,96,384]{2,1,0:T(8,128)(2,1)S(1)}, bf16[2,96,384]{2,1,0:T(8,128)(2,1)S(1)}, u32[]{:S(2)}, u32[]{:S(2)}) collective-permute-start(bf16[2,96,384]{2,1,0:T(8,128)(2,1)S(1)} %fusion.11), channel_id=1, source_target_pairs={{0,2},{1,3},{2,0},{3,1},{4,6},{5,7},{6,4},{7,5},{8,10},{9,11},{10,... | collective-permute-start | bytes 442376 | tf_op jit(solution)/shard_map/ppermute | solution.py:98
  148.8 14.7 %collective-permute-start.37 = (bf16[96,384]{1,0:T(8,128)(2,1)S(1)}, bf16[96,384]{1,0:T(8,128)(2,1)S(1)}, u32[]{:S(2)}, u32[]{:S(2)}) collective-permute-start(bf16[96,384]{1,0:T(8,128)(2,1)S(1)} %fusion.31), channel_id=1, source_target_pairs={{0,4},{1,5},{2,6},{3,7},{4,0},{5,1},{6,2},{7,3},{8,12},{9,13},{10,... | collective-permute-start | bytes 221192 | tf_op jit(solution)/shard_map/ppermute | solution.py:98
  151.0 12.4 %collective-permute-start.38 = (bf16[48,384]{1,0:T(8,128)(2,1)S(1)}, bf16[48,384]{1,0:T(8,128)(2,1)S(1)}, u32[]{:S(2)}, u32[]{:S(2)}) collective-permute-start(bf16[48,384]{1,0:T(8,128)(2,1)S(1)} %fusion.36), channel_id=1, source_target_pairs={{0,16},{8,24},{16,0},{24,8},{1,17},{9,25},{17,1},{25,9},{2,18},{10... | collective-permute-start | bytes 110600 | tf_op jit(solution)/shard_map/ppermute | solution.py:100
  164.8 12.4 %collective-permute-start.43 = (f32[96,384]{1,0:T(8,128)S(1)}, f32[96,384]{1,0:T(8,128)S(1)}, u32[]{:S(2)}, u32[]{:S(2)}) collective-permute-start(f32[96,384]{1,0:T(8,128)S(1)} %fusion.33), channel_id=1, source_target_pairs={{0,16},{8,24},{16,0},{24,8},{1,17},{9,25},{17,1},{25,9},{2,18},{10... | collective-permute-start | bytes 442376 | tf_op jit(solution)/shard_map/ppermute | solution.py:100
  166.2 14.1 %collective-permute-start.40 = (bf16[2,2,160,384]{3,2,1,0:T(8,128)(2,1)S(1)}, bf16[2,2,160,384]{3,2,1,0:T(8,128)(2,1)S(1)}, u32[]{:S(2)}, u32[]{:S(2)}) collective-permute-start(bf16[2,2,160,384]{3,2,1,0:T(8,128)(2,1)S(1)} %fusion.7), channel_id=1, source_target_pairs={{0,1},{1,0},{2,3},{3,2},{4,5},{5,4},{6,7},{7,6},{8,9},{9,8},{10,11... | collective-permute-start | bytes 1474568 | tf_op jit(solution)/shard_map/ppermute | solution.py:98
  173.5 12.4 %collective-permute-start.45 = (bf16[2,2,96,384]{3,2,1,0:T(8,128)(2,1)}, bf16[2,2,96,384]{3,2,1,0:T(8,128)(2,1)S(1)}, u32[]{:S(2)}, u32[]{:S(2)}) collective-permute-start(bf16[2,2,96,384]{3,2,1,0:T(8,128)(2,1)} %fusion.5), channel_id=1, source_target_pairs={{0,1},{1,0},{2,3},{3,2},{4,5},{5,4},{6,7},{7,6},{8,9},{9,8},{10,11... | collective-permute-start | bytes 884744 | tf_op jit(solution)/shard_map/ppermute | solution.py:98
  189.8 12.5 %collective-permute-start.50 = (bf16[2,96,384]{2,1,0:T(8,128)(2,1)S(1)}, bf16[2,96,384]{2,1,0:T(8,128)(2,1)S(1)}, u32[]{:S(2)}, u32[]{:S(2)}) collective-permute-start(bf16[2,96,384]{2,1,0:T(8,128)(2,1)S(1)} %fusion.10), channel_id=1, source_target_pairs={{0,2},{1,3},{2,0},{3,1},{4,6},{5,7},{6,4},{7,5},{8,10},{9,11},{10,... | collective-permute-start | bytes 442376 | tf_op jit(solution)/shard_map/ppermute | solution.py:98
  220.4 13.2 %collective-permute-start.59 = (bf16[4,64,384]{2,1,0:T(8,128)(2,1)S(1)}, bf16[4,64,384]{2,1,0:T(8,128)(2,1)S(1)}, u32[]{:S(2)}, u32[]{:S(2)}) collective-permute-start(bf16[4,64,384]{2,1,0:T(8,128)(2,1)S(1)} %pad_maximum_fusion.10.refs_9_), channel_id=1, source_target_pairs={{0,1},{1,0},{2,3},{3,2},{4,5},{5,4},{6,7},{7,6},{8,9},{9,8},{10,11... | collective-permute-start | bytes 589832 | tf_op jit(solution)/shard_map/ppermute | solution.py:98
  221.0 13.0 %collective-permute-start.61 = (bf16[4,64,384]{2,1,0:T(8,128)(2,1)S(1)}, bf16[4,64,384]{2,1,0:T(8,128)(2,1)S(1)}, u32[]{:S(2)}, u32[]{:S(2)}) collective-permute-start(bf16[4,64,384]{2,1,0:T(8,128)(2,1)S(1)} %pad_maximum_fusion.10.refs_9_), channel_id=1, source_target_pairs={{0,8},{8,0},{16,24},{24,16},{1,9},{9,1},{17,25},{25,17},{2,10},{10... | collective-permute-start | bytes 589832 | tf_op jit(solution)/shard_map/ppermute | solution.py:100
  (95 other events, 602.1 us)

commit v3 on v2

--- a/solution.py
+++ b/solution.py
@@ -21,7 +21,7 @@
 KERNEL_STARTS = (0, 9, 34)
 ROOT_HALF = math.sqrt(0.5)
 DENSITY = 1.0 / math.sqrt(2.0 * math.pi)
-VMEM_LIMIT = 24 << 20
+VMEM_LIMIT = 44 << 20
 F32 = jnp.float32
 BF16 = jnp.bfloat16
 
@@ -113,7 +113,7 @@
         return tuple(step if name == axis else 0 for name in ("z", "y", "x"))
 
     def here(self):
-        return jnp.stack([self.core, self.place, self.x]).astype(jnp.int32)
+        return jnp.stack([self.core, self.place, self.x, self.y, self.z]).astype(jnp.int32)
 
     def slots(self, masks, split_x):
         places = []
@@ -122,47 +122,6 @@
             places.append(place * self.nx + (self.x ^ mask_x) if split_x else place)
         return jnp.stack([self.core, self.place] + places).astype(jnp.int32)
 
-    def open_sum(self, kept, received, parts=1):
-        chan, rows, width = kept.shape
-        bits = [2] * ((chan * parts).bit_length() - 1)
-        return [term.reshape(*bits, rows // parts, width) for term in (kept, received)]
-
-    def exchange(self, terms, axis, level):
-        dims = terms[0].ndim - 2
-        at = len(self.bits("z")) - 1 - level if axis == "z" else dims - 1
-        index = self.index_on(axis) >> level & 1
-
-        def pick(term, which):
-            return lax.dynamic_index_in_dim(term, which, at, keepdims=False)
-
-        sent = total([pick(term, 1 - index) for term in terms])
-
-        def finish(received):
-            return [pick(term, index) for term in terms] + [received]
-
-        return ((sent, axis, 1 << level), finish)
-
-    def index_on(self, axis):
-        return self.y if axis == "y" else self.z if axis == "z" else self.x
-
-    def early(self, terms, axis):
-        levels = len(self.bits(axis))
-        for level in range(levels - 1):
-            move, finish = self.exchange(terms, axis, level)
-            terms = finish(self.swap(*move))
-        return self.exchange(terms, axis, levels - 1)
-
-    def regather_x(self, rows):
-        *steps, last = reversed(self.bits("x"))
-        for step in steps:
-            rows = self.beside_x(rows, self.swap(rows, "x", step), step)
-        return ((rows, "x", last), lambda received: self.beside_x(rows, received, last))
-
-    def beside_x(self, rows, received, step):
-        first = jnp.concatenate([rows, received])
-        second = jnp.concatenate([received, rows])
-        return jnp.where(self.x & step == 0, first, second)
-
     def both_halves(self, summed):
         other = self.swap_core(summed)
         first = self.core == 0
@@ -178,6 +137,181 @@
     for term in terms[1:]:
         result = result + term.astype(F32)
     return result.astype(BF16)
+
+
+class Chain:
+    def __init__(self, links, terms, rows, order):
+        self.terms = terms
+        self.rows = rows
+        self.order = list(order)
+        self.dims = [("z", k) for k in reversed(range(len(links.bits("z"))))]
+        self.dims += [("y", k) for k in reversed(range(len(links.bits("y"))))]
+
+    def low(self):
+        parts = [
+            lax.slice_in_dim(array[0], first, first + self.rows) for array, first in self.terms
+        ]
+        return total(parts)
+
+
+def halve(links, chains):
+    arrays = []
+    plans = []
+    groups = []
+    outs = []
+    for chain in chains:
+        axis, level = chain.order.pop(0)
+        places = []
+        for array, _first in chain.terms:
+            found = [k for k, other in enumerate(arrays) if other is array]
+            if not found:
+                arrays.append(array)
+            places.append(found[0] if found else len(arrays) - 1)
+        lead = 1 << len(chain.dims)
+        if axis == "x":
+            before, behind, rows, count = 0, lead, chain.rows // 2, lead
+        else:
+            at = chain.dims.index((axis, level))
+            before, behind = 1 << at, lead >> (at + 1)
+            rows, count = chain.rows, lead // 2
+            chain.dims.pop(at)
+        key = (axis, level, count)
+        mates = [group for group in groups if group[0] == key]
+        if mates:
+            group = mates[0]
+        else:
+            group = [key, 0]
+            groups.append(group)
+        plans.append((chain, places, before, behind, rows, count, group, group[1]))
+        group[1] += rows
+    width = arrays[0].shape[-1]
+    for key, rows in groups:
+        outs.append(jax.ShapeDtypeStruct((key[2], rows, width), BF16))
+    for _chain, _places, _before, _behind, rows, count, _group, _at in plans:
+        outs.append(jax.ShapeDtypeStruct((count, rows, width), BF16))
+
+    def body(here_ref, *refs):
+        ins, sends = refs[: len(arrays)], refs[len(arrays) : len(arrays) + len(groups)]
+        keeps = refs[len(arrays) + len(groups) :]
+        index = dict(y=here_ref[3], z=here_ref[4], x=here_ref[2])
+        for plan, keep in zip(plans, keeps):
+            chain, places, before, behind, rows, count, group, at = plan
+            axis, level, _count = group[0]
+            bit = index[axis] >> level & 1
+            send = sends[groups.index(group)]
+            for side, target, first_row in ((1 - bit, send, at), (bit, keep, 0)):
+                for out in range(count):
+                    summed = None
+                    for place, (_array, first) in zip(places, chain.terms):
+                        if axis == "x":
+                            start = pl.multiple_of(first + side * rows, 8)
+                            value = ins[place][out, pl.ds(start, rows), :]
+                        else:
+                            source = (out // behind * 2 + side) * behind + out % behind
+                            value = ins[place][source, first : first + rows, :]
+                        value = value.astype(F32)
+                        summed = value if summed is None else summed + value
+                    target[out, first_row : first_row + rows, :] = summed.astype(BF16)
+
+    made = pl.pallas_call(
+        body,
+        name=halve.__name__,
+        in_specs=[pl.BlockSpec(memory_space=pltpu.SMEM)]
+        + [pl.BlockSpec(memory_space=pltpu.VMEM) for _ in arrays],
+        out_specs=[pl.BlockSpec(memory_space=pltpu.VMEM) for _ in outs],
+        out_shape=outs,
+        compiler_params=pltpu.CompilerParams(vmem_limit_bytes=VMEM_LIMIT),
+    )(links.here(), *arrays)
+    moves = [(sent, key[0], 1 << key[1]) for sent, (key, _rows) in zip(made, groups)]
+
+    def take(received):
+        for plan, keep in zip(plans, made[len(groups) :]):
+            chain, _places, _before, _behind, rows, _count, group, at = plan
+            chain.terms = [(keep, 0), (received[groups.index(group)], at)]
+            chain.rows = rows
+
+    return (moves, take)
+
+
+class Reduction:
+    def __init__(self, links, kept, received):
+        self.links = links
+        count = kept.shape[1]
+        quantum = 16 * links.nx
+        cut = 2 * count // 5 // quantum * quantum if links.nx > 1 else 0
+        over_x = [("x", k) for k in reversed(range(len(links.bits("x"))))]
+        over_y = [("y", k) for k in range(len(links.bits("y")))]
+        over_z = [("z", k) for k in range(len(links.bits("z")))]
+        terms = lambda first: [(kept, first), (received, first)]
+        self.plain = Chain(links, terms(2 * cut), count - 2 * cut, over_y + over_z)
+        self.cut = []
+        if cut:
+            self.cut = [
+                Chain(links, terms(0), cut, over_x + over_y + over_z),
+                Chain(links, terms(cut), cut, over_z[:1] + over_x + over_y + over_z[1:]),
+            ]
+        self.sums = links.bits("x")[::-1]
+        self.gathers = list(self.sums) if cut else []
+        self.plain_rows = None
+        self.cut_rows = None
+
+    def open(self):
+        return [chain for chain in [self.plain] + self.cut if chain.order]
+
+    def done(self):
+        return not self.open() and not self.sums and not self.gathers
+
+    def last_moves(self):
+        moves, takes = [], []
+        if not self.plain.order and self.sums:
+            if self.plain_rows is None:
+                self.plain_rows = self.plain.low()
+            low = self.plain_rows.astype(BF16)
+            moves.append((low, "x", self.sums.pop(0)))
+
+            def take_sum(received):
+                self.plain_rows = low.astype(F32) + received.astype(F32)
+
+            takes.append(take_sum)
+        if self.gathers and not any(chain.order for chain in self.cut):
+            if self.cut_rows is None:
+                self.cut_rows = jnp.stack([chain.low() for chain in self.cut])
+            part = self.cut_rows
+            step = self.gathers.pop(0)
+            moves.append((part, "x", step))
+
+            def take_part(received):
+                first = jnp.concatenate([part, received], axis=1)
+                second = jnp.concatenate([received, part], axis=1)
+                self.cut_rows = jnp.where(self.links.x & step == 0, first, second)
+
+            takes.append(take_part)
+        return (moves, takes)
+
+    def result(self):
+        rows = self.plain_rows.astype(F32)
+        if self.cut_rows is None:
+            return rows
+        width = rows.shape[-1]
+        return jnp.concatenate([self.cut_rows.astype(F32).reshape(-1, width), rows])
+
+
+def next_round(links, reductions):
+    lasts = [reduction.last_moves() for reduction in reductions]
+    chains = [chain for reduction in reductions for chain in reduction.open()]
+    moves, take = halve(links, chains) if chains else ([], None)
+    count = len(moves)
+    for more, _takes in lasts:
+        moves = moves + more
+    takes = [one for _more, some in lasts for one in some]
+
+    def take_all(received):
+        if take is not None:
+            take(received[:count])
+        for one, part in zip(takes, received[count:]):
+            one(part)
+
+    return (moves, take_all)
 
 
 class Gather:
@@ -234,8 +368,11 @@
         slot = 0
         for near_part, far_part in zip(near, far):
             for d in range(near_part.shape[0]):
-                at = pl.multiple_of(where[2 + slot] * count, 8)
-                room = target.at[pl.ds(at, count), :]
+                if len(target.shape) == 3:
+                    room = target.at[where[2 + slot]]
+                else:
+                    at = pl.multiple_of(where[2 + slot] * count, 8)
+                    room = target.at[pl.ds(at, count), :]
                 rows = pl.ds(first, count)
                 pairs.append(
                     (
@@ -305,8 +442,11 @@
         self.room = room
         self.names = names
 
+    def __getitem__(self, key):
+        return self.room[self.names.get(key, key)]
+
     def __getattr__(self, key):
-        return self.room[self.names.get(key, key)]
+        return self[key]
 
     def flush(self, *refs):
         self.room.flush(*refs)
@@ -354,8 +494,11 @@
                 array = pltpu.with_memory_space_constraint(array, pltpu.HBM)
             operands.append(array)
             in_specs.append(pl.BlockSpec(memory_space=pltpu.HBM if pinned else pl.ANY))
-        for matrix in names:
-            place = scratch_for(pltpu.VMEM((pieces.rows(matrix), pieces.width), BF16))
+        for matrix, apart in names.items():
+            shape = (pieces.rows(matrix), pieces.width)
+            if apart:
+                shape = (pieces.slots, shape[0] // pieces.slots, shape[1])
+            place = scratch_for(pltpu.VMEM(shape, BF16))
             sems = scratch_for(pltpu.SemaphoreType.DMA((pieces.slots,)))
             loads.append((matrix, pieces, first, place, sems))
     out_specs, out_shapes, out_plan = [], [], []
@@ -376,6 +519,19 @@
         outs = refs[len(operands) : len(operands) + len(out_specs)]
         rooms = refs[len(operands) + len(out_specs) :]
         room = Room()
+        def load(group):
+            for matrix, pieces, first, place, sems in loads:
+                if pieces is group:
+                    where = ins[first]
+                    parts = ins[first + 1 : first + 1 + len(pieces.arrays())]
+                    start, wait = pieces.copies(matrix, where, parts, rooms[place], rooms[sems])
+                    start()
+                    room.refs[matrix] = rooms[place]
+                    room.waits[matrix] = wait
+                    room.refs.update(where=where)
+
+        for pieces, _names in weights[:1]:
+            load(pieces)
         for ref, (key, mode, more) in zip(ins, plan):
             if mode == FETCH:
                 place, sem = more
@@ -385,14 +541,8 @@
                 room.waits[key] = copy.wait
             else:
                 room.refs[key] = ref
-        for matrix, pieces, first, place, sems in loads:
-            where = ins[first]
-            parts = ins[first + 1 : first + 1 + len(pieces.arrays())]
-            start, wait = pieces.copies(matrix, where, parts, rooms[place], rooms[sems])
-            start()
-            room.refs[matrix] = rooms[place]
-            room.waits[matrix] = wait
-            room.refs.update(where=where)
+        for pieces, _names in weights[1:]:
+            load(pieces)
         for ref, (key, more) in zip(outs, out_plan):
             if more is None:
                 room.refs[key] = ref
@@ -734,33 +884,35 @@
         sent[:, at : at + rows, :] = first
 
 
-def head_stage(room):
-    outer = 10 * BLOCKS
-    gain = vector(room, outer + 3)
-    unit, scale = normalize(room.x[...])
-    low = (unit * gain + vector(room, outer + 4)).astype(BF16)
-    head_low = room.head[...].astype(BF16)
-    error = matmul(low, head_low) - room.patches[...].astype(F32)
-    denom = room.denom[0, 0]
-    weighted = column(room, COUNTED) * error
-    loss = column_sum(jnp.sum(weighted * error, axis=-1, keepdims=True)) / denom
-    d_pred = (2.0 * weighted / denom).astype(BF16)
-    grad = contract_rows(low, d_pred)
-    half = grad.shape[1] // 2
-    core = room.where[0]
-    store_halves(core, room.kept, room.sent, 0, grad[:, :half], grad[:, half:])
-    room.flush(room.kept, room.sent)
-    d_final = times_transposed(d_pred, head_low)
-    room.d_out[...] = norm_backward(d_final, unit, scale, gain)
-    sums = room.sums
-    width = low.shape[1]
-    sums[0:1, :] = column_sum(d_final * unit)
-    sums[1:2, :] = column_sum(d_final)
-    sums[2:3, :] = jnp.broadcast_to(loss, (1, width))
-    sums[3:8, :] = jnp.zeros((5, width), F32)
-
-
-def mlp_back_stage(block):
+def head_stage(at):
+    def head_step(room):
+        outer = 10 * BLOCKS
+        gain = vector(room, outer + 3)
+        unit, scale = normalize(room.x[...])
+        low = (unit * gain + vector(room, outer + 4)).astype(BF16)
+        head_low = room.head[...].astype(BF16)
+        error = matmul(low, head_low) - room.patches[...].astype(F32)
+        denom = room.denom[0, 0]
+        weighted = column(room, COUNTED) * error
+        loss = column_sum(jnp.sum(weighted * error, axis=-1, keepdims=True)) / denom
+        d_pred = (2.0 * weighted / denom).astype(BF16)
+        grad = contract_rows(low, d_pred)
+        half = grad.shape[1] // 2
+        core = room.where[0]
+        store_halves(core, room.kept, room.sent, at, grad[:, :half], grad[:, half:])
+        d_final = times_transposed(d_pred, head_low)
+        room.d_out[...] = norm_backward(d_final, unit, scale, gain)
+        sums = room.sums
+        width = low.shape[1]
+        sums[0:1, :] = column_sum(d_final * unit)
+        sums[1:2, :] = column_sum(d_final)
+        sums[2:3, :] = jnp.broadcast_to(loss, (1, width))
+        sums[3:8, :] = jnp.zeros((5, width), F32)
+
+    return head_step
+
+
+def mlp_back_stage(block, at):
     def mlp_backward(room):
         d_residual = room.d_in[...]
         d_down = d_residual * keep_of(room, block, 1)
@@ -772,8 +924,7 @@
         d_pre = (times_transposed(d_low, room.down[...]) * room.slope[...]).astype(BF16)
         grad_up = contract_rows(d_pre, second)
         core = room.where[0]
-        store_halves(core, room.kept, room.sent, 0, grad_up, grad_down)
-        room.flush(room.sent, room.kept)
+        store_halves(core, room.kept, room.sent, at, grad_up, grad_down)
         d_second = matmul(d_pre, room.up[...])
         room.d_out[...] = d_residual + norm_backward(d_second, unit, scale, gain)
         sums = room.sums
@@ -786,7 +937,7 @@
     return mlp_backward
 
 
-def mix_back_stage(block, groups, lanes):
+def mix_back_stage(block, groups, lanes, at):
     def mix_backward(room):
         d_proj = room.d_in[...] * keep_of(room, block, 0)
         d_low = d_proj.astype(BF16)
@@ -802,7 +953,7 @@
         grad_proj = contract_rows(product, d_low)
         grad_mix = contract_rows(d_mod, room.low[...])
         core = room.where[0]
-        store_halves(core, room.kept, room.sent, 0, grad_mix, grad_proj)
+        store_halves(core, room.kept, room.sent, at, grad_mix, grad_proj)
         sums = room.sums
         width = d_low.shape[1]
         sums[0:1, :] = column_sum(d_proj)
@@ -871,7 +1022,7 @@
     return levels_backward
 
 
-def inputs_back_stage(block):
+def inputs_back_stage(block, at):
     def inputs_backward(room):
         unit, scale = normalize(room.x[...])
         gain = vector(room, 10 * block)
@@ -900,10 +1051,7 @@
         grad_key = contract_rows(d_context, first)
         kept, sent = room.kept, room.sent
         core = room.where[0]
-        store_halves(core, kept, sent, 0, grad_query, grad_key)
-        at = width // kept.shape[0]
-        kept[:, at : 2 * at, :] = room.more_kept[...]
-        sent[:, at : 2 * at, :] = room.more_sent[...]
+        store_halves(core, kept, sent, at, grad_query, grad_key)
 
     return inputs_backward
 
@@ -939,8 +1087,7 @@
         small[at + 3 : at + 4, :] = column_sum(d_residual * mask)
         for key in sum_keys:
             at += 8
-            sums = room.input_sums if key is None else room[key]
-            small[at : at + 8, :] = sums[...]
+            small[at : at + 8, :] = room[key][...]
         grad = contract_rows(room.patches[...], d_embed.astype(BF16))
         core = room.where[0]
         kept, sent = room.kept, room.sent
@@ -954,38 +1101,32 @@
     return embed_backward
 
 
-def update_head_stage(rate):
-    def update_head(room):
-        half = room.weight.shape[1] // 2
-        for index in range(2):
-            here = slice(index * half, (index + 1) * half)
-            new_weight, new_moment = nesterov(
-                room.weight[:, here],
-                room.moment[:, here],
-                (room.head0, room.head1)[index][...].astype(F32),
-                rate,
-            )
-            room.new_weight[:, here] = new_weight
-            room.new_moment[:, here] = new_moment
-
-    return update_head
-
-
-def update_shared_stage(tap_count, own, rate):
+def update_shared_stage(tap_count, own, part, rate):
     def update_shared(room):
-        half = room.embed0.shape[0]
-        for index in range(2):
-            here = slice(index * half, (index + 1) * half)
-            gradient = (room.embed0, room.embed1)[index][...].astype(F32)
-            new_weight, new_moment = nesterov(
-                room.weight[here, :], room.moment[here, :], gradient, rate
-            )
-            room.new_weight[here, :] = new_weight
-            room.new_moment[here, :] = new_moment
-        room.flush(room.new_weight, room.new_moment)
-        small = jnp.concatenate([room.small0[...], room.small1[...]], axis=0)
-        grads = small.astype(F32)
-        width = small.shape[1]
+        slots = room.all0.shape[0]
+        width = room.all0.shape[2]
+        small_rows = []
+        for index, ref in enumerate((room.all0, room.all1)):
+            across = slice(index * width, (index + 1) * width)
+            for slot in range(slots):
+                gradient = ref[slot].astype(F32)
+                down = slice(slot * part, (slot + 1) * part)
+                new_weight, new_moment = nesterov(
+                    room.head[down, across], room.head_moment[down, across], gradient[:part], rate
+                )
+                room.new_head[down, across] = new_weight
+                room.new_head_moment[down, across] = new_moment
+                at = (index * slots + slot) * part
+                down = slice(at, at + part)
+                new_weight, new_moment = nesterov(
+                    room.embed[down, :], room.embed_moment[down, :], gradient[part : 2 * part], rate
+                )
+                room.new_embed[down, :] = new_weight
+                room.new_embed_moment[down, :] = new_moment
+                small_rows.append(gradient[2 * part :])
+        room.flush(room.new_head, room.new_head_moment, room.new_embed, room.new_embed_moment)
+        grads = jnp.concatenate(small_rows, axis=0)
+        small = grads.astype(BF16)
 
         def sum_row(index, row):
             at = sums_start(tap_count) + 8 * index + row
@@ -1374,301 +1515,269 @@
     mlp_pieces[1] = pieces_of(mlp[1], far, mlp_layout(own_hidden), False)
 
     sums_out = ((8, width), F32, FETCH)
-    head_part = (links.chan, patch_in // (2 * links.chan), width)
-    hidden_part = (links.chan, own_hidden, width)
-    own_part = (links.chan, own, width)
-    made = run_kernel(
-        [
-            renamed(mlp_stage(1), out=0),
-            renamed(head_stage, x=0, d_out=1, kept=2, sent=3, sums=4),
-            renamed(mlp_back_stage(1), d_in=1),
-        ],
-        {
-            **dict(middle=hold(middle), patches=fetch(patches), head=fetch(head_weight)),
-            **dict(denom=(denominator, SCALAR), **basic),
-        },
-        {
-            2: (head_part, BF16, HOLD),
-            3: (head_part, BF16, HOLD),
-            4: sums_out,
-            **dict(
-                d_out=(whole, F32, HOLD),
-                kept=(hidden_part, BF16, HOLD),
-                sent=(hidden_part, BF16, HOLD),
-                sums=sums_out,
-            ),
-        },
-        {
-            0: pltpu.VMEM(whole, F32),
-            1: pltpu.VMEM(whole, F32),
-            **dict(
-                hidden=pltpu.VMEM((rows, hidden_width), BF16),
-                slope=pltpu.VMEM((rows, hidden_width), F32),
-            ),
-        },
-        [(mlp_pieces[1], up_down)],
-    )
-    head_sums = made[4]
-    sums = [[None] * 3 for _ in range(BLOCKS)]
-    sums[1][1] = made.sums
-    d_middle = made.d_out
     embed_rows = patch_in // (2 * links.chan)
     small_rows = small_rows_for(tap_count, links.chan)
-
-    def mix_back(b, d_middle):
-        shape = (1, rows, width) if shared else field_shape
-        return run_kernel(
-            [mix_back_stage(b, shape[0], shape[2])],
+    small_part = small_rows // (2 * links.chan)
+    hidden_shape = (rows, hidden_width)
+    mix_at = own_hidden
+    upper_lead = own_hidden + own + embed_rows
+    lower_lead = own_hidden + own
+    upper_count = upper_lead + own
+    lower_count = lower_lead + own + embed_rows + small_part
+    d_shape = (1, rows, width) if shared else field_shape
+    levels_names = dict(context=0, gates=0, k1=0, k2=0, k3=0, s1=0, s2=0, s3=0, pool=0)
+    mix_names = dict(query_out=0, mod=0, low=0)
+    levels_temps = dict(padded=padded, d_padded=padded)
+    between = dict(
+        d_context=pltpu.VMEM(whole, BF16),
+        d_gates=pltpu.VMEM((rows, 4 * LANES), F32),
+        **levels_temps,
+    )
+    tap_shape = (room_rows, width)
+
+    def pair_of(count):
+        shape = (links.chan, count, width)
+        return dict(kept=(shape, BF16, HOLD), sent=(shape, BF16, HOLD))
+
+    def levels_in(b):
+        return dict(taps=fetch(taps), **fetch_all(saved[b], levels_names), **grid_columns)
+
+    head_names = dict(x=0, d_out=1, sums=5)
+    first_stages = [
+        renamed(mlp_stage(1), out=0),
+        renamed(head_stage(own_hidden + own), **head_names),
+        renamed(mlp_back_stage(1, 0), d_in=1, d_out=2, sums=3),
+        renamed(mix_back_stage(1, d_shape[0], d_shape[2], mix_at), d_in=2, sums=4),
+    ]
+    first_in = dict(
+        middle=hold(middle),
+        head=fetch(head_weight),
+        patches=fetch(patches),
+        denom=(denominator, SCALAR),
+        **basic,
+        **fetch_all(saved[1], mix_names),
+    )
+    first_temps = {
+        0: pltpu.VMEM(whole, F32),
+        1: pltpu.VMEM(whole, F32),
+        **dict(hidden=pltpu.VMEM(hidden_shape, BF16), slope=pltpu.VMEM(hidden_shape, F32)),
+    }
+    sums_outs = {3: sums_out, 4: sums_out, 5: sums_out}
+    mlp_weights_in = (mlp_pieces[1], up_down)
+    mixer_in = dict(proj=0, mix=0)
+    inputs_in = dict(query=0, key=0)
+
+    def levels_apart(b, d_sum):
+        made = run_kernel(
+            [focal_back_stage(b, groups, lanes)],
+            dict(d_sum=fetch(shares.to_images(d_sum)), **levels_in(b)),
             dict(
-                d_in=hold(d_middle),
-                **fetch_all(saved[b], dict(query_out=0, mod=0, low=0)),
+                d_context=((IMAGE_ROWS, channels), BF16, FETCH),
+                d_gates=((IMAGE_ROWS, 4 * LANES), F32, FETCH),
+                d_taps=((room_rows, channels), F32, FETCH),
+            ),
+            levels_temps,
+        )
+        return Box(
+            d_context=shares.to_rows(made.d_context),
+            d_gates=shares.sum_rows(made.d_gates),
+            d_taps=shares.spread(made.d_taps),
+        )
+
+    def joined(first, second):
+        return Box(
+            kept=jnp.concatenate([first.kept, second.kept], axis=1),
+            sent=jnp.concatenate([first.sent, second.sent], axis=1),
+        )
+
+    if shared:
+        first = run_kernel(
+            first_stages,
+            first_in,
+            {
+                2: (whole, F32, HOLD),
+                **sums_outs,
+                **dict(d_query=(whole, BF16, HOLD), d_sum=(d_shape, F32, HOLD)),
+                **pair_of(upper_lead),
+            },
+            first_temps,
+            [mlp_weights_in, (focal_pieces[1], mixer_in)],
+        )
+        levels = levels_apart(1, first.d_sum)
+        second = run_kernel(
+            [inputs_back_stage(1, 0)],
+            dict(
+                d_in=hold(first[2]),
+                d_query=hold(first.d_query),
+                d_context=fetch(levels.d_context),
+                d_gates=fetch(levels.d_gates),
+                x=fetch(saved[1].x),
                 **basic,
             ),
-            dict(
-                d_query=(whole, BF16, HOLD),
-                d_sum=(shape, F32, HOLD),
-                kept=(own_part, BF16, HOLD),
-                sent=(own_part, BF16, HOLD),
-                sums=sums_out,
+            dict(d_out=(whole, F32, HOLD), input_sums=sums_out, **pair_of(own)),
+            {},
+            [(focal_pieces[1], inputs_in)],
+        )
+        pair = joined(first, second)
+        d_x, d_taps = second.d_out, levels.d_taps
+        upper_sums = [second.input_sums, first[3], first[4], first[5]]
+    else:
+        first = run_kernel(
+            first_stages
+            + [
+                focal_back_stage(1, groups, lanes),
+                renamed(inputs_back_stage(1, upper_lead), d_in=2),
+            ],
+            dict(x=fetch(saved[1].x), **levels_in(1)) | first_in,
+            {
+                **sums_outs,
+                **dict(
+                    d_out=(whole, F32, HOLD),
+                    input_sums=sums_out,
+                    d_taps=(tap_shape, F32, FETCH),
+                ),
+                **pair_of(upper_count),
+            },
+            {
+                2: pltpu.VMEM(whole, F32),
+                **first_temps,
+                **dict(d_query=pltpu.VMEM(whole, BF16), d_sum=pltpu.VMEM(d_shape, F32)),
+                **between,
+            },
+            [mlp_weights_in, (focal_pieces[1], mixer_in | inputs_in)],
+        )
+        pair = first
+        d_x, d_taps = first.d_out, first.d_taps
+        upper_sums = [first.input_sums, first[3], first[4], first[5]]
+
+    lower_stages = [
+        renamed(mlp_back_stage(0, 0), d_out=2, sums=3),
+        renamed(mix_back_stage(0, d_shape[0], d_shape[2], mix_at), d_in=2, sums=4),
+    ]
+    lower_names = dict(hidden=0, slope=0, middle=0)
+    sum_keys = [10, 3, 4, 11, 12, 13, 14]
+    last_in = {
+        **dict(zip(sum_keys[3:], (fetch(array) for array in upper_sums))),
+        15: fetch(d_taps),
+        **dict(patches=fetch(patches), embedded=fetch(embedded.embedded), x=fetch(saved[0].x)),
+    }
+
+    def last_stages(at):
+        return [
+            renamed(inputs_back_stage(0, at), d_in=2, d_out=1, input_sums=10),
+            renamed(
+                embed_back_stage(tap_count, sum_keys, [None, 15], at + own), d_out=1
             ),
-            {},
-            [(focal_pieces[b], dict(proj=0, mix=0))],
-        )
-
-    def focal_back(b, d_sum, d_middle, mixed):
-        final = b == 0
-        kept = saved[b]
-        names = dict(context=0, gates=0, k1=0, k2=0, k3=0, s1=0, s2=0, s3=0, pool=0)
-        levels_in = dict(taps=fetch(taps), **fetch_all(kept, names), **grid_columns)
-        levels_temps = dict(padded=padded, d_padded=padded)
+        ]
+
+    last_temps = {
+        1: pltpu.VMEM(whole, F32),
+        10: pltpu.VMEM((8, width), F32),
+        **dict(small=pltpu.VMEM((small_rows, width), F32)),
+    }
+
+    def lower_back(d_x):
         inputs = dict(
-            d_in=hold(d_middle),
-            d_query=hold(mixed.d_query),
-            x=fetch(kept.x),
-            more_kept=hold(mixed.kept),
-            more_sent=hold(mixed.sent),
+            d_in=hold(d_x),
+            **fetch_all(saved[0], lower_names),
             **basic,
-        )
-        part_rows = 2 * own
-        if final:
-            part_rows += embed_rows + small_rows // (2 * links.chan)
-        part = (links.chan, part_rows, width)
-        outputs = dict(kept=(part, BF16, HOLD), sent=(part, BF16, HOLD))
-        temps = {}
-        stages = [inputs_back_stage(b)]
-        if final:
-            sum_keys = [None]
-            for c in range(BLOCKS):
-                for kind in range(3):
-                    if sums[c][kind] is not None:
-                        key = 3 * c + kind
-                        sum_keys.append(key)
-                        inputs[key] = fetch(sums[c][kind])
-            head_key, taps_key = 3 * BLOCKS, 3 * BLOCKS + 1
-            inputs[head_key] = fetch(head_sums)
-            inputs[taps_key] = fetch(d_taps)
-            sum_keys.append(head_key)
-            inputs.update(patches=fetch(patches), embedded=fetch(embedded.embedded))
-            stages.append(embed_back_stage(tap_count, sum_keys, [None, taps_key], 2 * own))
-            temps.update(
-                small=pltpu.VMEM((small_rows, width), F32),
-                input_sums=pltpu.VMEM((8, width), F32),
-                d_out=pltpu.VMEM(whole, F32),
+            **fetch_all(saved[0], mix_names),
+        )
+        weights = [(mlp_pieces[0], dict(down=0, up=0)), (focal_pieces[0], mixer_in)]
+        if shared:
+            first = run_kernel(
+                lower_stages,
+                inputs,
+                {
+                    2: (whole, F32, HOLD),
+                    3: sums_out,
+                    4: sums_out,
+                    **dict(d_query=(whole, BF16, HOLD), d_sum=(d_shape, F32, HOLD)),
+                    **pair_of(lower_lead),
+                },
+                {},
+                weights,
             )
-        else:
-            outputs.update(d_out=(whole, F32, HOLD), input_sums=sums_out)
-        weights = [(focal_pieces[b], dict(query=0, key=0))]
-        if shared:
-            levels = run_kernel(
-                [focal_back_stage(b, groups, lanes)],
-                dict(d_sum=fetch(shares.to_images(d_sum)), **levels_in),
-                dict(
-                    d_context=((IMAGE_ROWS, channels), BF16, FETCH),
-                    d_gates=((IMAGE_ROWS, 4 * LANES), F32, FETCH),
-                    d_taps=((room_rows, channels), F32, FETCH),
-                ),
-                levels_temps,
+            levels = levels_apart(0, first.d_sum)
+            second = run_kernel(
+                last_stages(0),
+                {
+                    2: hold(first[2]),
+                    3: fetch(first[3]),
+                    4: fetch(first[4]),
+                    **last_in,
+                    **dict(
+                        d_query=hold(first.d_query),
+                        d_context=fetch(levels.d_context),
+                        d_gates=fetch(levels.d_gates),
+                        d_taps=fetch(levels.d_taps),
+                        **basic,
+                    ),
+                },
+                pair_of(lower_count - lower_lead),
+                last_temps,
+                [(focal_pieces[0], inputs_in)],
             )
-            tap_grad = shares.spread(levels.d_taps)
-            inputs.update(
-                d_context=fetch(shares.to_rows(levels.d_context)),
-                d_gates=fetch(shares.sum_rows(levels.d_gates)),
-            )
-            if final:
-                inputs.update(d_taps=fetch(tap_grad))
-            made = run_kernel(stages, inputs, outputs, temps, weights)
-            return Box(made, d_taps=tap_grad)
-        temps.update(
-            d_context=pltpu.VMEM(whole, BF16),
-            d_gates=pltpu.VMEM((rows, 4 * LANES), F32),
-            **levels_temps,
-        )
-        tap_shape = (room_rows, width)
-        if final:
-            temps.update(d_taps=pltpu.VMEM(tap_shape, F32))
-        else:
-            outputs.update(d_taps=(tap_shape, F32, FETCH))
+            return joined(first, second)
         return run_kernel(
-            [focal_back_stage(b, groups, lanes)] + stages,
-            dict(d_sum=hold(d_sum), **levels_in) | inputs,
-            outputs,
-            temps,
-            weights,
-        )
-
-    def mlp_back(b, d_x):
-        return run_kernel(
-            [mlp_back_stage(b)],
-            dict(d_in=hold(d_x), **fetch_all(saved[b], dict(hidden=0, slope=0, middle=0)), **basic),
-            dict(
-                d_out=(whole, F32, HOLD),
-                kept=(hidden_part, BF16, HOLD),
-                sent=(hidden_part, BF16, HOLD),
-                sums=sums_out,
-            ),
-            {},
-            [(mlp_pieces[b], dict(down=0, up=0))],
-        )
-
-    z_last = len(links.bits("z")) - 1
-
-    def open_mlp(kept, received):
-        terms = links.open_sum(kept, received, parts_x)
-        return links.early(terms, "x") if split_x else links.early(terms, "y")
-
-    mixed, got = beside(
-        lambda gate: mix_back(1, gate), d_middle, [(made.sent, "core", 1), (made[3], "core", 1)]
+            lower_stages + [focal_back_stage(0, groups, lanes)] + last_stages(lower_lead),
+            {**inputs, **levels_in(0), **last_in},
+            pair_of(lower_count),
+            {
+                2: pltpu.VMEM(whole, F32),
+                3: pltpu.VMEM((8, width), F32),
+                4: pltpu.VMEM((8, width), F32),
+                **last_temps,
+                **dict(d_query=pltpu.VMEM(whole, BF16), d_sum=pltpu.VMEM(d_shape, F32)),
+                **dict(d_taps=pltpu.VMEM(tap_shape, F32)),
+                **between,
+            },
+            [weights[0], (focal_pieces[0], mixer_in | inputs_in)],
+        )
+
+    (d_x, upper_kept), got = together((d_x, pair.kept), [(pair.sent, "core", 1)])
+    upper = Reduction(links, upper_kept, got[0])
+    moves, take = next_round(links, [upper])
+    made, got = beside(lower_back, d_x, moves)
+    take(got)
+    moves, take = next_round(links, [upper])
+    lower_kept, got = together(made.kept, moves + [(made.sent, "core", 1)])
+    take(got[:-1])
+    lower = Reduction(links, lower_kept, got[-1])
+    rate = 0.2 * math.sqrt(group_rows * lax.axis_size("dp"))
+    gate = here
+    turn = [lower]
+    while not (lower.done() and upper.done()):
+        moves, take = next_round(links, turn)
+        gate, got = together(gate, moves)
+        take(got)
+        turn = [lower, upper]
+    upper_rows, lower_rows = upper.result(), lower.result()
+    head_at = own_hidden + own
+    common = Gather(
+        links,
+        jnp.concatenate(
+            [
+                upper_rows[head_at : head_at + embed_rows].astype(BF16),
+                lower_rows[lower_lead + own :].astype(BF16),
+            ]
+        ),
     )
-    sums[1][2] = mixed.sums
-    mlp_move, mlp_finish = open_mlp(made.kept, got[0])
-    head_move, head_finish = links.early(links.open_sum(made[2], got[1]), "y")
-    made, got = beside(
-        lambda gate: focal_back(1, gate, d_middle, mixed), mixed.d_sum, [mlp_move, head_move]
-    )
-    mlp_sum = mlp_finish(got[0])
-    sums[1][0] = made.input_sums
-    d_taps = made.d_taps
-    focal_kept = made.kept
-    mlp_move, mlp_finish = links.early(mlp_sum, "y") if split_x else links.exchange(
-        mlp_sum, "z", 0
-    )
-    head_move, head_finish = links.exchange(head_finish(got[1]), "z", 0)
-    made, got = beside(
-        lambda gate: mlp_back(0, gate),
-        made.d_out,
-        [(made.sent, "core", 1), mlp_move, head_move],
-    )
-    sums[0][1] = made.sums
-    mlp_one = mlp_finish(got[1])
-    d_middle = made.d_out
-    focal_move, focal_finish = links.early(links.open_sum(focal_kept, got[0]), "y")
-    one_move, one_finish = links.exchange(mlp_one, "z", 0 if split_x else z_last)
-    head_move, head_finish = links.exchange(head_finish(got[2]), "z", z_last)
-    mlp_kept = made.kept
-    mixed, got = beside(
-        lambda gate: mix_back(0, gate),
-        d_middle,
-        [(made.sent, "core", 1), focal_move, one_move, head_move],
-    )
-    sums[0][2] = mixed.sums
-    mlp_move, mlp_finish = open_mlp(mlp_kept, got[0])
-    focal_move, focal_finish = links.exchange(focal_finish(got[1]), "z", 0)
-    mlp_one = one_finish(got[2])
-    head_low = total(head_finish(got[3]))
-    if split_x:
-        one_move, one_finish = links.exchange(mlp_one, "z", z_last)
-    else:
-        one_low = total(mlp_one)
-        one_move = (one_low, "x", x_first)
-    moves = [mlp_move, focal_move, one_move, (head_low, "x", x_first)]
-    made, got = beside(lambda gate: focal_back(0, gate, d_middle, mixed), mixed.d_sum, moves)
-    mlp_sum = mlp_finish(got[0])
-
-    def rest_x(low, received):
-        summed = low.astype(F32) + received.astype(F32)
-        for step in x_rest:
-            low = summed.astype(BF16)
-            summed = low.astype(F32) + links.swap(low, "x", step).astype(F32)
-        return summed
-
-    head = Gather(links, rest_x(head_low, got[3]).astype(BF16))
-    rate = 0.2 * math.sqrt(group_rows * lax.axis_size("dp"))
-
-    focal_move, focal_finish = links.exchange(focal_finish(got[1]), "z", z_last)
-    if split_x:
-        one_move, one_finish = links.regather_x(total(one_finish(got[2])).astype(F32))
-        zero_move, zero_finish = links.early(mlp_sum, "y")
-    else:
-        mlp_one = rest_x(one_low, got[2])
-        zero_move, zero_finish = links.exchange(mlp_sum, "z", 0)
-    lower_kept, got = together(made.kept, [(made.sent, "core", 1)])
-    lower_move, lower_finish = links.early(links.open_sum(lower_kept, got[0]), "y")
-    moves = [lower_move, focal_move, (head.stack, "z", z_first)]
-    if split_x:
-        moves.append(one_move)
-    gate, got = together(here, moves)
-    lower_move, lower_finish = links.exchange(lower_finish(got[0]), "z", 0)
-    focal_low = total(focal_finish(got[1]))
-    head.take(got[2], "z", z_first)
-    if split_x:
-        mlp_one = one_finish(got[3])
-    moves = [lower_move, zero_move] + [(head.stack, "z", step) for step in z_rest]
-    gate, got = together(gate, moves)
-    lower_move, lower_finish = links.exchange(lower_finish(got[0]), "z", z_last)
-    take_z(head, got[2:])
-    mlp_zero = zero_finish(got[1])
-    zero_move, zero_finish = links.exchange(mlp_zero, "z", 0 if split_x else z_last)
-    head_move = head.early("y")
-    moves = [lower_move, (focal_low, "x", x_first), (head.stack, *head_move), zero_move]
-    (gate, mlp_one), got = together((gate, mlp_one), moves)
-    lower_low = total(lower_finish(got[0]))
-    focal_one = rest_x(focal_low, got[1])
-    head.take(got[2], *head_move, True)
-    mlp_zero = zero_finish(got[3])
-    if split_x:
-        zero_move, zero_finish = links.exchange(mlp_zero, "z", z_last)
-    else:
-        zero_low = total(mlp_zero)
-        zero_move = (zero_low, "x", x_first)
-    moves = [(lower_low, "x", x_first), zero_move]
-    moves += [(part, "core", 1) for part in head.parts]
-    (focal_one, mlp_one), got = together((focal_one, mlp_one), moves)
-    lower = rest_x(lower_low, got[0])
-    head_far = got[2:]
-    if split_x:
-        zero_rows = total(zero_finish(got[1])).astype(F32)
-        zero_move, zero_finish = links.regather_x(zero_rows)
-    else:
-        mlp_zero = rest_x(zero_low, got[1])
-    common = Gather(links, lower[2 * own :].astype(BF16))
-    moves = common.direct()
-    count = len(moves)
-    if split_x:
-        moves.append(zero_move)
-    (focal_one, mlp_one, late), got = together((focal_one, mlp_one, lower[: 2 * own]), moves)
-    common.take_direct(got[:count])
-    if split_x:
-        mlp_zero = zero_finish(got[count])
+    got = [links.swap(*move) for move in common.direct()]
+    common.take_direct(got)
     y_move = common.early("y")
     common.take(links.swap(common.stack, *y_move), *y_move, True)
-    rows_early = jnp.concatenate([mlp_one, mlp_zero, focal_one, late], axis=0)
+    rows_early = jnp.concatenate(
+        [
+            upper_rows[:own_hidden],
+            lower_rows[:own_hidden],
+            upper_rows[mix_at : mix_at + own],
+            upper_rows[upper_lead:],
+            lower_rows[mix_at : lower_lead + own],
+        ]
+    )
     rows_early, _stack = lax.optimization_barrier((rows_early, common.stack))
     halves = links.both_halves(rows_early)
-    head_far, _stack = lax.optimization_barrier((head_far, common.stack))
-    head_pieces = Pieces(
-        links.slots(head.masks, False),
-        head.parts,
-        head_far,
-        dict(head0=(0, 0, embed_rows), head1=(1, 0, embed_rows)),
-    )
-    weight_out = (head_weight.shape, F32, FETCH)
-    new_head = run_kernel(
-        [update_head_stage(rate)],
-        dict(weight=fetch(head_weight), moment=fetch(head_moment)),
-        dict(new_weight=weight_out, new_moment=weight_out),
-        {},
-        [(head_pieces, dict(head0=0, head1=0))],
-    )
     ends = (own_hidden, 2 * own_hidden)
     grad_mlp = jnp.stack(
         [
@@ -1676,10 +1785,12 @@
             jnp.stack([part[: ends[0]] for part in halves]),
         ]
     )
-    one = [part[ends[1] : ends[1] + 2 * own] for part in halves]
-    late = [part[ends[1] + 2 * own :] for part in halves]
-    grad_focal = jnp.stack([jnp.stack([part[:own] for part in parts]) for parts in (late, one)])
-    grad_mixer = jnp.stack([jnp.stack([part[own:] for part in parts]) for parts in (late, one)])
+    places = [ends[1] + k * own for k in range(5)]
+    mix_one, inputs_one, mix_zero, inputs_zero = (
+        [part[first:end] for part in halves] for first, end in zip(places, places[1:])
+    )
+    grad_focal = jnp.stack([jnp.stack(inputs_zero), jnp.stack(inputs_one)])
+    grad_mixer = jnp.stack([jnp.stack(mix_zero), jnp.stack(mix_one)])
     results = []
     for weight, moment, average, gradient, order, back in (
         (focal_input, focal_moment, focal_average, grad_focal, (0, 2, 3, 1), (0, 3, 1, 2)),
@@ -1694,31 +1805,27 @@
         results.extend(
             jnp.transpose(array, back) for array in (new_weight, new_moment, new_average)
         )
-    there, results, *held = lax.optimization_barrier(
-        (common.parts[1], results, new_head.new_weight, new_head.new_moment)
-    )
+    there, results = lax.optimization_barrier((common.parts[1], results))
     common_near = [common.parts[0], there]
     common_far = [links.swap_core(part) for part in common_near]
-    small_part = small_rows // (2 * links.chan)
+    count = 2 * embed_rows + small_part
     common_pieces = Pieces(
         links.slots(common.masks, False),
         common_near,
         common_far,
-        dict(
-            embed0=(0, 0, embed_rows),
-            embed1=(1, 0, embed_rows),
-            small0=(0, embed_rows, small_part),
-            small1=(1, embed_rows, small_part),
-        ),
+        dict(all0=(0, 0, count), all1=(1, 0, count)),
     )
-    weight_out = (embed_weight.shape, F32, FETCH)
+    head_out = (head_weight.shape, F32, FETCH)
+    embed_out = (embed_weight.shape, F32, FETCH)
     vector_out = (vectors.shape, F32, HOLD)
     kernel_out = (kernel_rows.shape, F32, HOLD)
     made = run_kernel(
-        [update_shared_stage(tap_count, own, rate)],
+        [update_shared_stage(tap_count, own, embed_rows, rate)],
         dict(
-            weight=hold(embed_weight),
-            moment=hold(embed_moment),
+            head=hold(head_weight),
+            head_moment=hold(head_moment),
+            embed=hold(embed_weight),
+            embed_moment=hold(embed_moment),
             vectors=hold(vectors),
             vector_moment=hold(vector_moment),
             vector_average=hold(vector_average),
@@ -1727,8 +1834,10 @@
             kernel_average=hold(jnp.transpose(kernel_average, (0, 2, 1))),
         ),
         dict(
-            new_weight=weight_out,
-            new_moment=weight_out,
+            new_head=head_out,
+            new_head_moment=head_out,
+            new_embed=embed_out,
+            new_embed_moment=embed_out,
             new_vectors=vector_out,
             new_vector_moment=vector_out,
             new_vector_average=vector_out,
@@ -1738,13 +1847,15 @@
             loss=((1, LANES), F32, HOLD),
         ),
         dict(packed=pltpu.VMEM((-(-vectors.shape[0] // 8) * 8, width), F32)),
-        [(common_pieces, dict(embed0=0, embed1=0, small0=0, small1=0))],
+        [(common_pieces, dict(all0=1, all1=1))],
+        False,
     )
     return (
         made.loss[0, 0],
-        made.new_weight,
-        made.new_moment,
-        *held,
+        made.new_embed,
+        made.new_embed_moment,
+        made.new_head,
+        made.new_head_moment,
         made.new_vectors,
         made.new_vector_moment,
         made.new_vector_average,

time: 245 us -> 216 us (0.88)
  other arithmetic: 40.1 us -> 13.5 us
  waiting for transfers between devices: 43.4 us -> 57.6 us
  Pallas kernels: 86.7 us -> 75.5 us
    convert_element_type x20 -> x4, other arithmetic: 22.7 us -> 0.1 us  [total(): return result.astype(BF16)]
    pallas_call x11 -> x6, Pallas kernels: 80.7 us -> 64.4 us  [run_kernel(): pl.pallas_call(body, name=stages[-1].__name__, in_specs=in_specs, out_spe...]
    ppermute x28 -> x24, waiting for transfers between devices: 15.1 us -> 23 us  [swap(): lax.ppermute(values, 'dp', [(i, i ^ step) for i in range(self.nx * self.n...]
    ppermute x35 -> x31, starting transfers between devices: 47.8 us -> 41.3 us  [swap(): lax.ppermute(values, 'chan', [(i, i ^ step) for i in range(self.chan)])]
    ppermute x35 -> x31, waiting for transfers between devices: 28.3 us -> 34.6 us  [swap(): lax.ppermute(values, 'chan', [(i, i ^ step) for i in range(self.chan)])]
    pallas_call x0 -> x6, Pallas kernels: none -> 5.19 us  [halve(): pl.pallas_call(body, name=halve.__name__, in_specs=[pl.BlockSpec(memory_s...]
    ppermute x28 -> x24, starting transfers between devices: 9.87 us -> 14.2 us  [swap(): lax.ppermute(values, 'dp', [(i, i ^ step) for i in range(self.nx * self.n...]
    unnamed x115 -> x73, local copies, waits for them, and re-layouts: 8.17 us -> 6.06 us
  transfers between devices with their start and end apart: 63 -> 55, of which waited for: 22 -> 30; matrix products, arithmetic and copies ran while one was open for 15% -> 7% of each run, Pallas kernels for 29% -> 21%
where the time goes in v3:
time: 216 us; the launch traced here: 213 us
  Pallas kernels  75.5 us (35%)
  waiting for transfers between devices  57.6 us (27%)
  starting transfers between devices  55.4 us (26%)
  other arithmetic  13.5 us (6%)
  local copies, waits for them, and re-layouts  7.79 us (4%)
  between operations  2.65 us (1%)
    pallas_call x6, Pallas kernels, run_kernel(): pl.pallas_call(body, name=stages[-1].__name__, in_specs=in_specs, out_spe...  64.4 us
    ppermute x31, starting transfers between devices, swap(): lax.ppermute(values, 'chan', [(i, i ^ step) for i in range(self.chan)])  41.3 us
    ppermute x31, waiting for transfers between devices, swap(): lax.ppermute(values, 'chan', [(i, i ^ step) for i in range(self.chan)])  34.6 us
    ppermute x24, waiting for transfers between devices, swap(): lax.ppermute(values, 'dp', [(i, i ^ step) for i in range(self.nx * self.n...  23 us
    ppermute x24, starting transfers between devices, swap(): lax.ppermute(values, 'dp', [(i, i ^ step) for i in range(self.nx * self.n...  14.2 us
    unnamed x73, local copies, waits for them, and re-layouts  6.06 us
    pallas_call x4, Pallas kernels, pack_rows(): pl.pallas_call(body, name=pack_rows.__name__, in_specs=[pl.BlockSpec(memo...  5.98 us
    pallas_call x6, Pallas kernels, halve(): pl.pallas_call(body, name=halve.__name__, in_specs=[pl.BlockSpec(memory_s...  5.19 us
  transfers between devices with their start and end apart: 55, of which 30 were waited for; matrix products, arithmetic and copies ran while one was open for 7% of the time, Pallas kernels for 21%

profile of v3, /device:TPU:0, one launch (start us, length us, event | category | flops | bytes accessed | tf_op | source)
XLA Modules:
  0.0 212.5 jit_solution(9008310985059170348)
XLA Ops:
  3.1 5.1 %collective-permute-start.2 = (bf16[1,144,384]{2,1,0:T(8,128)(2,1)S(1)}, bf16[1,144,384]{2,1,0:T(8,128)(2,1)S(1)}, u32[]{:S(2)}, u32[]{:S(2)}) collective-permute-start(bf16[1,144,384]{2,1,0:T(8,128)(2,1)S(1)} %bitcast.191), channel_id=1, source_target_pairs={{0,6},{1,7},{2,4},{3,5},{4,2},{5,3},{6,0},{7,1},{8,14},{9,15},{10,... | collective-permute-start | bytes 331784 | tf_op jit(solution)/shard_map/ppermute | solution.py:98
  14.7 2.6 %embed_stage.1 = (f32[256,384]{1,0:T(8,128)S(1)}, f32[256,384]{1,0:T(8,128)}) custom-call(bf16[256,768]{1,0:T(8,128)(2,1)} %refs_25_.1, f32[768,384]{1,0:T(8,128)} %refs_2_.3, f32[26,384]{1,0:T(8,128)} %refs_4_.3, f32[256,8]{1,0:T(8,128)} %copy.49.refs_3_.refs_2_.refs_11_.refs_17_.refs_5_.refs_19_), custom_call_target="tpu_custom_call" | custom-call | tf_op jit(solution)/shard_map/embed_stage/pallas_call | solution.py:562
  19.2 2.1 %collective-permute-start.3 = (bf16[1,96,384]{2,1,0:T(8,128)(2,1)S(1)}, bf16[1,96,384]{2,1,0:T(8,128)(2,1)S(1)}, u32[]{:S(2)}, u32[]{:S(2)}) collective-permute-start(bf16[1,96,384]{2,1,0:T(8,128)(2,1)S(1)} %bitcast.184), channel_id=1, source_target_pairs={{0,4},{1,5},{2,6},{3,7},{4,0},{5,1},{6,2},{7,3},{8,12},{9,13},{10,... | collective-permute-start | bytes 221192 | tf_op jit(solution)/shard_map/ppermute | solution.py:98
  26.5 2.4 %collective-permute-start.6 = (bf16[1,96,384]{2,1,0:T(8,128)(2,1)S(1)}, bf16[1,96,384]{2,1,0:T(8,128)(2,1)S(1)}, u32[]{:S(2)}, u32[]{:S(2)}) collective-permute-start(bf16[1,96,384]{2,1,0:T(8,128)(2,1)S(1)} %bitcast.188), channel_id=1, source_target_pairs={{0,4},{1,5},{2,6},{3,7},{4,0},{5,1},{6,2},{7,3},{8,12},{9,13},{10,... | collective-permute-start | bytes 221192 | tf_op jit(solution)/shard_map/ppermute | solution.py:98
  36.7 10.0 %mix_forward.2 = (f32[2,3,88,128]{3,2,1,0:T(8,128)}, f32[3,256,128]{2,1,0:T(8,128)}, f32[256,512]{1,0:T(8,128)}, f32[256,384]{1,0:T(8,128)}, f32[3,256,128]{2,1,...) custom-call(f32[256,384]{1,0:T(8,128)S(1)} %get-tuple-element.236.re, ...), custom_call_target="tpu_custom_call" | custom-call | tf_op jit(solution)/shard_map/mix_forward/pallas_call | solution.py:562
  52.8 5.1 %collective-permute-done.15 = bf16[2,192,384]{2,1,0:T(8,128)(2,1)S(1)} collective-permute-done((bf16[2,192,384]{2,1,0:T(8,128)(2,1)S(1)}, bf16[2,192,384]{2,1,0:T(8,128)(2,1)S(1)}, u32[]{:S(2)}, u32[]{:S(2)}) %collective-permute-start.15) | collective-permute-done | bytes 294944 | tf_op jit(solution)/shard_map/ppermute | solution.py:98
  59.4 3.5 %collective-permute-done.16.refs_7_.refs_30_ = bf16[8,96,384]{2,1,0:T(8,128)(2,1)S(1)} collective-permute-done((bf16[8,96,384]{2,1,0:T(8,128)(2,1)S(1)}, bf16[8,96,384]{2,1,0:T(8,128)(2,1)S(1)}, u32[]{:S(2)}, u32[]{:S(2)}) %collective-permute-start.16) | collective-permute-done | bytes 589856 | tf_op jit(solution)/shard_map/ppermute | solution.py:100
  68.9 10.2 %mix_forward.3 = (f32[256,384]{1,0:T(8,128)}, bf16[256,1536]{1,0:T(8,128)(2,1)}, f32[256,1536]{1,0:T(8,128)}, f32[3,256,128]{2,1,0:T(8,128)}, f32[256,512]{1,0:T...) custom-call(f32[256,384]{1,0:T(8,128)S(1)} %get-tuple-element.263.re, ...), custom_call_target="tpu_custom_call" | custom-call | tf_op jit(solution)/shard_map/mix_forward/pallas_call | solution.py:562
  83.4 18.9 %inputs_backward.1 = (f32[8,384]{1,0:T(8,128)}, f32[8,384]{1,0:T(8,128)}, f32[8,384]{1,0:T(8,128)}, f32[256,384]{1,0:T(8,128)S(1)}, f32[8,384]{1,0:T(8,128)}, /*...) custom-call(f32[256,384]{1,0:T(8,128)} %get-tuple-element.285.refs_0_, ...), custom_call_target="tpu_custom_call" | custom-call | tf_op jit(solution)/shard_map/inputs_backward/pallas_call | solution.py:562
  102.9 3.7 %collective-permute-done.24.refs_1_ = bf16[8,336,384]{2,1,0:T(8,128)(2,1)S(1)} collective-permute-done((bf16[8,336,384]{2,1,0:T(8,128)(2,1)S(1)}, bf16[8,336,384]{2,1,0:T(8,128)(2,1)S(1)}, u32[]{:S(2)}, u32[]{:S(2)}) %collective-permute-start.24) | collective-permute-done | bytes 2064416 | tf_op jit(solution)/shard_map/ppermute | solution.py:100
  111.4 16.5 %embed_backward.1 = (bf16[8,352,384]{2,1,0:T(8,128)(2,1)S(1)}, bf16[8,352,384]{2,1,0:T(8,128)(2,1)S(1)}) custom-call(f32[256,384]{1,0:T(8,128)S(1)} %get-tuple-element.313.refs_0_, bf16[256,1536]{1,0:T(8,128)(2,1)} %get-tuple-element.314.refs_1_, f32[256,1536]{1,0:T(8,128)} %get-tuple-element.315.refs_2_, f32[256,384]{1,0:T(8,128)} %copy-done.7, ...), custom_call_target="tpu_custom_call" | custom-call | tf_op jit(solution)/shard_map/embed_backward/pallas_call | solution.py:562
  131.3 4.7 %collective-permute-done.28.refs_7_ = bf16[2,80,384]{2,1,0:T(8,128)(2,1)S(1)} collective-permute-done((bf16[2,80,384]{2,1,0:T(8,128)(2,1)S(1)}, bf16[2,80,384]{2,1,0:T(8,128)(2,1)S(1)}, u32[]{:S(2)}, u32[]{:S(2)}) %collective-permute-start.28) | collective-permute-done | bytes 122912 | tf_op jit(solution)/shard_map/ppermute | solution.py:98
  141.0 6.3 %collective-permute-done.32.refs_1_ = bf16[4,96,384]{2,1,0:T(8,128)(2,1)S(1)} collective-permute-done((bf16[4,96,384]{2,1,0:T(8,128)(2,1)S(1)}, bf16[4,96,384]{2,1,0:T(8,128)(2,1)S(1)}, u32[]{:S(2)}, u32[]{:S(2)}) %collective-permute-start.32) | collective-permute-done | bytes 294944 | tf_op jit(solution)/shard_map/ppermute | solution.py:98
  153.2 1.9 collective-permute-start.38
  155.1 3.3 %collective-permute-done.38 = bf16[1,80,384]{2,1,0:T(8,128)(2,1)S(1)} collective-permute-done((bf16[1,80,384]{2,1,0:T(8,128)(2,1)S(1)}, bf16[1,80,384]{2,1,0:T(8,128)(2,1)S(1)}, u32[]{:S(2)}, u32[]{:S(2)}) %collective-permute-start.38) | collective-permute-done | bytes 61472 | tf_op jit(solution)/shard_map/ppermute | solution.py:98
  162.3 2.4 %collective-permute-start.40 = (bf16[1,224,384]{2,1,0:T(8,128)(2,1)S(1)}, bf16[1,224,384]{2,1,0:T(8,128)(2,1)S(1)}, u32[]{:S(2)}, u32[]{:S(2)}) collective-permute-start(bf16[1,224,384]{2,1,0:T(8,128)(2,1)S(1)} %get-tuple-element.379), channel_id=1, source_target_pairs={{0,4},{1,5},{2,6},{3,7},{4,0},{5,1},{6,2},{7,3},{8,12},{9,13},{10,... | collective-permute-start | bytes 516104 | tf_op jit(solution)/shard_map/ppermute | solution.py:98
  166.2 3.2 %collective-permute-done.43 = bf16[80,384]{1,0:T(8,128)(2,1)S(1)} collective-permute-done((bf16[80,384]{1,0:T(8,128)(2,1)S(1)}, bf16[80,384]{1,0:T(8,128)(2,1)S(1)}, u32[]{:S(2)}, u32[]{:S(2)}) %collective-permute-start.43) | collective-permute-done | bytes 61472 | tf_op jit(solution)/shard_map/ppermute | solution.py:100
  174.7 2.3 %collective-permute-done.46 = bf16[2,64,384]{2,1,0:T(8,128)(2,1)S(1)} collective-permute-done((bf16[2,64,384]{2,1,0:T(8,128)(2,1)S(1)}, bf16[2,64,384]{2,1,0:T(8,128)(2,1)S(1)}, u32[]{:S(2)}, u32[]{:S(2)}) %collective-permute-start.46) | collective-permute-done | bytes 98336 | tf_op jit(solution)/shard_map/ppermute | solution.py:100
  177.0 3.4 %collective-permute-done.44 = bf16[1,128,384]{2,1,0:T(8,128)(2,1)S(1)} collective-permute-done((bf16[1,128,384]{2,1,0:T(8,128)(2,1)S(1)}, bf16[1,128,384]{2,1,0:T(8,128)(2,1)S(1)}, u32[]{:S(2)}, u32[]{:S(2)}) %collective-permute-start.44) | collective-permute-done | bytes 98336 | tf_op jit(solution)/shard_map/ppermute | solution.py:98
  182.1 3.0 %collective-permute-done.51 = bf16[2,64,384]{2,1,0:T(8,128)(2,1)S(1)} collective-permute-done((bf16[2,64,384]{2,1,0:T(8,128)(2,1)S(1)}, bf16[2,64,384]{2,1,0:T(8,128)(2,1)S(1)}, u32[]{:S(2)}, u32[]{:S(2)}) %collective-permute-start.51) | collective-permute-done | bytes 98336 | tf_op jit(solution)/shard_map/ppermute | solution.py:100
  185.3 2.2 %collective-permute-start.49 = (bf16[1,112,384]{2,1,0:T(8,128)(2,1)S(1)}, bf16[1,112,384]{2,1,0:T(8,128)(2,1)S(1)}, u32[]{:S(2)}, u32[]{:S(2)}) collective-permute-start(bf16[1,112,384]{2,1,0:T(8,128)(2,1)S(1)} %fusion.13), channel_id=1, source_target_pairs={{0,6},{1,7},{2,4},{3,5},{4,2},{5,3},{6,0},{7,1},{8,14},{9,15},{10,... | collective-permute-start | bytes 258056 | tf_op jit(solution)/shard_map/ppermute | solution.py:98
  187.5 2.2 %collective-permute-start.47 = (bf16[1,112,384]{2,1,0:T(8,128)(2,1)S(1)}, bf16[1,112,384]{2,1,0:T(8,128)(2,1)S(1)}, u32[]{:S(2)}, u32[]{:S(2)}) collective-permute-start(bf16[1,112,384]{2,1,0:T(8,128)(2,1)S(1)} %fusion.13), channel_id=1, source_target_pairs={{0,2},{1,3},{2,0},{3,1},{4,6},{5,7},{6,4},{7,5},{8,10},{9,11},{10,... | collective-permute-start | bytes 258056 | tf_op jit(solution)/shard_map/ppermute | solution.py:98
  200.5 2.1 fusion.1
  205.9 6.2 %update_shared.1 = (f32[384,768]{1,0:T(8,128)}, f32[384,768]{1,0:T(8,128)}, f32[768,384]{1,0:T(8,128)}, f32[768,384]{1,0:T(8,128)}, f32[26,384]{1,0:T(8,128)}, /...) custom-call(f32[384,768]{1,0:T(8,128)S(1)} %copy-done.1, ...), custom_call_target="tpu_custom_call" | custom-call | tf_op jit(solution)/shard_map/update_shared/pallas_call | solution.py:562
  (227 shorter events, 86.3 us)
Async XLA Ops:
  3.1 14.3 %collective-permute-start.2 = (bf16[1,144,384]{2,1,0:T(8,128)(2,1)S(1)}, bf16[1,144,384]{2,1,0:T(8,128)(2,1)S(1)}, u32[]{:S(2)}, u32[]{:S(2)}) collective-permute-start(bf16[1,144,384]{2,1,0:T(8,128)(2,1)S(1)} %bitcast.191), channel_id=1, source_target_pairs={{0,6},{1,7},{2,4},{3,5},{4,2},{5,3},{6,0},{7,1},{8,14},{9,15},{10,... | collective-permute-start | bytes 331784 | tf_op jit(solution)/shard_map/ppermute | solution.py:98
  8.2 9.3 %collective-permute-start.1 = (bf16[1,144,384]{2,1,0:T(8,128)(2,1)S(1)}, bf16[1,144,384]{2,1,0:T(8,128)(2,1)S(1)}, u32[]{:S(2)}, u32[]{:S(2)}) collective-permute-start(bf16[1,144,384]{2,1,0:T(8,128)(2,1)S(1)} %bitcast.192), channel_id=1, source_target_pairs={{0,4},{1,5},{2,6},{3,7},{4,0},{5,1},{6,2},{7,3},{8,12},{9,13},{10,... | collective-permute-start | bytes 331784 | tf_op jit(solution)/shard_map/ppermute | solution.py:98
  8.2 9.3 %collective-permute-start = (bf16[1,144,384]{2,1,0:T(8,128)(2,1)S(1)}, bf16[1,144,384]{2,1,0:T(8,128)(2,1)S(1)}, u32[]{:S(2)}, u32[]{:S(2)}) collective-permute-start(bf16[1,144,384]{2,1,0:T(8,128)(2,1)S(1)} %bitcast.193), channel_id=1, source_target_pairs={{0,2},{1,3},{2,0},{3,1},{4,6},{5,7},{6,4},{7,5},{8,10},{9,11},{10,... | collective-permute-start | bytes 331784 | tf_op jit(solution)/shard_map/ppermute | solution.py:98
  17.6 14.9 %collective-permute-start.5 = (bf16[4,144,384]{2,1,0:T(8,128)(2,1)S(1)}, bf16[4,144,384]{2,1,0:T(8,128)(2,1)S(1)}, u32[]{:S(2)}, u32[]{:S(2)}) collective-permute-start(bf16[4,144,384]{2,1,0:T(8,128)(2,1)S(1)} %pad_maximum_fusion.3.refs_5_.refs_34_), channel_id=1, source_target_pairs={{0,1},{1,0},{2,3},{3,2},{4,5},{5,4},{6,7},{7,6},{8,9},{9,8},{10,11... | collective-permute-start | bytes 1327112 | tf_op jit(solution)/shard_map/ppermute | solution.py:98
  30.8 16.0 %collective-permute-start.12 = (bf16[1,192,384]{2,1,0:T(8,128)(2,1)S(1)}, bf16[1,192,384]{2,1,0:T(8,128)(2,1)S(1)}, u32[]{:S(2)}, u32[]{:S(2)}) collective-permute-start(bf16[1,192,384]{2,1,0:T(8,128)(2,1)S(1)} %bitcast.181), channel_id=1, source_target_pairs={{0,4},{1,5},{2,6},{3,7},{4,0},{5,1},{6,2},{7,3},{8,12},{9,13},{10,... | collective-permute-start | bytes 442376 | tf_op jit(solution)/shard_map/ppermute | solution.py:98
  33.4 13.4 %collective-permute-start.10 = (bf16[4,96,384]{2,1,0:T(8,128)(2,1)}, bf16[4,96,384]{2,1,0:T(8,128)(2,1)}, u32[]{:S(2)}, u32[]{:S(2)}) collective-permute-start(bf16[4,96,384]{2,1,0:T(8,128)(2,1)} %pad_maximum_fusion.5), channel_id=1, source_target_pairs={{0,1},{1,0},{2,3},{3,2},{4,5},{5,4},{6,7},{7,6},{8,9},{9,8},{10,11... | collective-permute-start | bytes 884744 | tf_op jit(solution)/shard_map/ppermute | solution.py:98
  33.9 12.9 %collective-permute-start.11 = (bf16[2,96,384]{2,1,0:T(8,128)(2,1)S(1)}, bf16[2,96,384]{2,1,0:T(8,128)(2,1)}, u32[]{:S(2)}, u32[]{:S(2)}) collective-permute-start(bf16[2,96,384]{2,1,0:T(8,128)(2,1)S(1)} %pad_maximum_fusion.12), channel_id=1, source_target_pairs={{0,2},{1,3},{2,0},{3,1},{4,6},{5,7},{6,4},{7,5},{8,10},{9,11},{10,... | collective-permute-start | bytes 442376 | tf_op jit(solution)/shard_map/ppermute | solution.py:98
  35.1 11.7 %collective-permute-start.13 = (f32[8,128]{1,0:T(8,128)S(1)}, f32[8,128]{1,0:T(8,128)S(1)}, u32[]{:S(2)}, u32[]{:S(2)}) collective-permute-start(f32[8,128]{1,0:T(8,128)S(1)} %broadcast_add_fusion), channel_id=1, source_target_pairs={{0,16},{8,24},{16,0},{24,8},{1,17},{9,25},{17,1},{25,9},{2,18},{10... | collective-permute-start | bytes 12296 | tf_op jit(solution)/shard_map/ppermute | solution.py:100
  48.0 14.9 %collective-permute-start.16 = (bf16[8,96,384]{2,1,0:T(8,128)(2,1)S(1)}, bf16[8,96,384]{2,1,0:T(8,128)(2,1)S(1)}, u32[]{:S(2)}, u32[]{:S(2)}) collective-permute-start(bf16[8,96,384]{2,1,0:T(8,128)(2,1)S(1)} %pad_maximum_fusion.1.refs_6_.refs_29_), channel_id=1, source_target_pairs={{0,16},{8,24},{16,0},{24,8},{1,17},{9,25},{17,1},{25,9},{2,18},{10... | collective-permute-start | bytes 1769480 | tf_op jit(solution)/shard_map/ppermute | solution.py:100
  49.6 8.3 %collective-permute-start.15 = (bf16[2,192,384]{2,1,0:T(8,128)(2,1)S(1)}, bf16[2,192,384]{2,1,0:T(8,128)(2,1)S(1)}, u32[]{:S(2)}, u32[]{:S(2)}) collective-permute-start(bf16[2,192,384]{2,1,0:T(8,128)(2,1)S(1)} %pad_maximum_fusion.7), channel_id=1, source_target_pairs={{0,2},{1,3},{2,0},{3,1},{4,6},{5,7},{6,4},{7,5},{8,10},{9,11},{10,... | collective-permute-start | bytes 884744 | tf_op jit(solution)/shard_map/ppermute | solution.py:98
  52.8 14.5 %collective-permute-start.17 = (bf16[8,96,384]{2,1,0:T(8,128)(2,1)S(1)}, bf16[8,96,384]{2,1,0:T(8,128)(2,1)S(1)}, u32[]{:S(2)}, u32[]{:S(2)}) collective-permute-start(bf16[8,96,384]{2,1,0:T(8,128)(2,1)S(1)} %pad_maximum_fusion.1.refs_6_.refs_29_), channel_id=1, source_target_pairs={{0,8},{8,0},{16,24},{24,16},{1,9},{9,1},{17,25},{25,17},{2,10},{10... | collective-permute-start | bytes 1769480 | tf_op jit(solution)/shard_map/ppermute | solution.py:100
  63.9 16.0 %collective-permute-start.21 = (bf16[4,192,384]{2,1,0:T(8,128)(2,1)}, bf16[4,192,384]{2,1,0:T(8,128)(2,1)}, u32[]{:S(2)}, u32[]{:S(2)}) collective-permute-start(bf16[4,192,384]{2,1,0:T(8,128)(2,1)} %pad_maximum_fusion.2.refs_22_), channel_id=1, source_target_pairs={{0,1},{1,0},{2,3},{3,2},{4,5},{5,4},{6,7},{7,6},{8,9},{9,8},{10,11... | collective-permute-start | bytes 1769480 | tf_op jit(solution)/shard_map/ppermute | solution.py:98
  67.2 14.6 %collective-permute-start.22 = (bf16[4,192,384]{2,1,0:T(8,128)(2,1)}, bf16[4,192,384]{2,1,0:T(8,128)(2,1)S(1)}, u32[]{:S(2)}, u32[]{:S(2)}) collective-permute-start(bf16[4,192,384]{2,1,0:T(8,128)(2,1)} %pad_maximum_fusion.2.refs_22_), channel_id=1, source_target_pairs={{0,8},{8,0},{16,24},{24,16},{1,9},{9,1},{17,25},{25,17},{2,10},{10... | collective-permute-start | bytes 1769480 | tf_op jit(solution)/shard_map/ppermute | solution.py:100
  107.7 20.2 %collective-permute-start.26 = (bf16[8,64,384]{2,1,0:T(8,128)(2,1)S(1)}, bf16[8,64,384]{2,1,0:T(8,128)(2,1)S(1)}, u32[]{:S(2)}, u32[]{:S(2)}) collective-permute-start(bf16[8,64,384]{2,1,0:T(8,128)(2,1)S(1)} %get-tuple-element.311), channel_id=1, source_target_pairs={{0,16},{8,24},{16,0},{24,8},{1,17},{9,25},{17,1},{25,9},{2,18},{10... | collective-permute-start | bytes 1179656 | tf_op jit(solution)/shard_map/ppermute | solution.py:100
  108.3 19.7 %collective-permute-start.27 = (bf16[4,128,384]{2,1,0:T(8,128)(2,1)S(1)}, bf16[4,128,384]{2,1,0:T(8,128)(2,1)S(1)}, u32[]{:S(2)}, u32[]{:S(2)}) collective-permute-start(bf16[4,128,384]{2,1,0:T(8,128)(2,1)S(1)} %get-tuple-element.312), channel_id=1, source_target_pairs={{0,2},{1,3},{2,0},{3,1},{4,6},{5,7},{6,4},{7,5},{8,10},{9,11},{10,... | collective-permute-start | bytes 1179656 | tf_op jit(solution)/shard_map/ppermute | solution.py:98
  109.9 18.0 %collective-permute-start.25 = (bf16[4,80,384]{2,1,0:T(8,128)(2,1)S(1)}, bf16[4,80,384]{2,1,0:T(8,128)(2,1)S(1)}, u32[]{:S(2)}, u32[]{:S(2)}) collective-permute-start(bf16[4,80,384]{2,1,0:T(8,128)(2,1)S(1)} %get-tuple-element.310), channel_id=1, source_target_pairs={{0,1},{1,0},{2,3},{3,2},{4,5},{5,4},{6,7},{7,6},{8,9},{9,8},{10,11... | collective-permute-start | bytes 737288 | tf_op jit(solution)/shard_map/ppermute | solution.py:98
  127.9 8.5 %collective-permute-start.31 = (bf16[8,352,384]{2,1,0:T(8,128)(2,1)S(1)}, bf16[8,352,384]{2,1,0:T(8,128)(2,1)S(1)}, u32[]{:S(2)}, u32[]{:S(2)}) collective-permute-start(bf16[8,352,384]{2,1,0:T(8,128)(2,1)S(1)} %get-tuple-element.346), channel_id=1, source_target_pairs={{0,8},{8,0},{16,24},{24,16},{1,9},{9,1},{17,25},{25,17},{2,10},{10... | collective-permute-start | bytes 6488072 | tf_op jit(solution)/shard_map/ppermute | solution.py:100
  137.5 10.6 %collective-permute-start.33 = (bf16[8,64,384]{2,1,0:T(8,128)(2,1)S(1)}, bf16[8,64,384]{2,1,0:T(8,128)(2,1)S(1)}, u32[]{:S(2)}, u32[]{:S(2)}) collective-permute-start(bf16[8,64,384]{2,1,0:T(8,128)(2,1)S(1)} %get-tuple-element.351), channel_id=1, source_target_pairs={{0,16},{8,24},{16,0},{24,8},{1,17},{9,25},{17,1},{25,9},{2,18},{10... | collective-permute-start | bytes 1179656 | tf_op jit(solution)/shard_map/ppermute | solution.py:100
  139.0 10.2 %collective-permute-start.34 = (bf16[4,128,384]{2,1,0:T(8,128)(2,1)S(1)}, bf16[4,128,384]{2,1,0:T(8,128)(2,1)S(1)}, u32[]{:S(2)}, u32[]{:S(2)}) collective-permute-start(bf16[4,128,384]{2,1,0:T(8,128)(2,1)S(1)} %get-tuple-element.352), channel_id=1, source_target_pairs={{0,2},{1,3},{2,0},{3,1},{4,6},{5,7},{6,4},{7,5},{8,10},{9,11},{10,... | collective-permute-start | bytes 1179656 | tf_op jit(solution)/shard_map/ppermute | solution.py:98
  150.2 8.2 %collective-permute-start.35 = (bf16[2,160,384]{2,1,0:T(8,128)(2,1)S(1)}, bf16[2,160,384]{2,1,0:T(8,128)(2,1)S(1)}, u32[]{:S(2)}, u32[]{:S(2)}) collective-permute-start(bf16[2,160,384]{2,1,0:T(8,128)(2,1)S(1)} %get-tuple-element.365), channel_id=1, source_target_pairs={{0,2},{1,3},{2,0},{3,1},{4,6},{5,7},{6,4},{7,5},{8,10},{9,11},{10,... | collective-permute-start | bytes 737288 | tf_op jit(solution)/shard_map/ppermute | solution.py:98
  159.1 10.3 %collective-permute-start.41 = (bf16[2,64,384]{2,1,0:T(8,128)(2,1)S(1)}, bf16[2,64,384]{2,1,0:T(8,128)(2,1)S(1)}, u32[]{:S(2)}, u32[]{:S(2)}) collective-permute-start(bf16[2,64,384]{2,1,0:T(8,128)(2,1)S(1)} %get-tuple-element.380), channel_id=1, source_target_pairs={{0,2},{1,3},{2,0},{3,1},{4,6},{5,7},{6,4},{7,5},{8,10},{9,11},{10,... | collective-permute-start | bytes 294920 | tf_op jit(solution)/shard_map/ppermute | solution.py:98
  160.8 8.6 %collective-permute-start.42 = (bf16[2,64,384]{2,1,0:T(8,128)(2,1)S(1)}, bf16[2,64,384]{2,1,0:T(8,128)(2,1)S(1)}, u32[]{:S(2)}, u32[]{:S(2)}) collective-permute-start(bf16[2,64,384]{2,1,0:T(8,128)(2,1)S(1)} %get-tuple-element.381), channel_id=1, source_target_pairs={{0,1},{1,0},{2,3},{3,2},{4,5},{5,4},{6,7},{7,6},{8,9},{9,8},{10,11... | collective-permute-start | bytes 294920 | tf_op jit(solution)/shard_map/ppermute | solution.py:98
  193.6 10.5 %collective-permute-start.53 = (bf16[4,112,384]{2,1,0:T(8,128)(2,1)S(1)}, bf16[4,112,384]{2,1,0:T(8,128)(2,1)S(1)}, u32[]{:S(2)}, u32[]{:S(2)}) collective-permute-start(bf16[4,112,384]{2,1,0:T(8,128)(2,1)S(1)} %pad_maximum_fusion.4.refs_11_), channel_id=1, source_target_pairs={{0,8},{8,0},{16,24},{24,16},{1,9},{9,1},{17,25},{25,17},{2,10},{10... | collective-permute-start | bytes 1032200 | tf_op jit(solution)/shard_map/ppermute | solution.py:100
  194.1 10.1 %collective-permute-start.50 = (bf16[4,112,384]{2,1,0:T(8,128)(2,1)S(1)}, bf16[4,112,384]{2,1,0:T(8,128)(2,1)S(1)}, u32[]{:S(2)}, u32[]{:S(2)}) collective-permute-start(bf16[4,112,384]{2,1,0:T(8,128)(2,1)S(1)} %pad_maximum_fusion.4.refs_11_), channel_id=1, source_target_pairs={{0,1},{1,0},{2,3},{3,2},{4,5},{5,4},{6,7},{7,6},{8,9},{9,8},{10,11... | collective-permute-start | bytes 1032200 | tf_op jit(solution)/shard_map/ppermute | solution.py:98
  (64 other events, 372.0 us)
